TPU v7x, 256 devices: a whole 4x4x8 slice. The times are simulated.
256 devices in a mesh: cfg: 2 (over core), req: 128 (over y, z, x).
Axes of the slice: x: 4, y: 4, z: 8, core: 2. Of those that a mesh axis runs over, the one named last changes fastest.
Arguments:
- query_rows: bfloat16 [2, 65536, 2560], P('cfg', 'req'), may hold values from -32 to 32
- key_rows: bfloat16 [2, 65536, 2560], P('cfg', 'req'), may hold values from -6 to 6
- value_rows: bfloat16 [2, 65536, 2560], P('cfg', 'req'), may hold values from -600 to 600
- positions: int32 [3, 65536], P(None, 'req'), may hold values from 0 to 51
- latents: float32 [65536, 64], P('req', 'cfg'), may hold values from -6 to 6
- w_head: bfloat16 [2560, 64], replicated, may hold values from -0.125 to 0.125
- modulation: float32 [2, 2560], replicated, may hold values from -0.5 to 1
- guide_scale: float32 [1], replicated, may hold values from 4 to 6
- step_sizes: float32 [256], replicated, may hold values from -0.4 to -0.1
- lengths: int32 [256], replicated, may hold values from 1 to 512, 65536 in all
Outputs:
- next_latents: float32 [65536, 64], P('req', 'cfg')
Inputs may be any that keep to these rules, and one draw needn't show every extreme that they name: Videos are laid end to end in the given order and their lengths sum to 65536.
All inputs are finite; a program needn't handle non-finite values.
Results may differ from a plain program's by a relative error of at most 0.0059.
Values may be sent and summed in bfloat16 or wider, within the bound.
A program may use at most 128 MiB of HBM per device.

v0:
```python
import math

import jax
import jax.numpy as jnp
from jax import lax
from jax.sharding import PartitionSpec as P

HD = 128
LMAX = 512


masked_score = -1e30
rope_theta = 10000.0


def shifted(value, axis, steps):
    count = lax.axis_size(axis)
    leading, last = (max(0, -steps), min(count, count - steps))
    return lax.ppermute(value, axis, [(source, source + steps) for source in range(leading, last)])


def from_partner(x, axis, distance):
    return lax.ppermute(x, axis, [(i, i ^ 1 << distance) for i in range(lax.axis_size(axis))])


def angles(positions):
    pair_total = HD // 2
    side_pairs = HD // 6
    time_pairs = pair_total - 2 * side_pairs
    column = jnp.arange(pair_total, dtype=jnp.int32)
    in_time = column < time_pairs
    in_height = (column >= time_pairs) & (column < time_pairs + side_pairs)
    in_width = column >= time_pairs + side_pairs
    local_index = jnp.where(
        in_time, column, jnp.where(in_height, column - time_pairs, column - time_pairs - side_pairs)
    )
    axis_pairs = jnp.where(in_time, time_pairs, side_pairs)
    frequency = jnp.exp(
        -(local_index.astype(jnp.float32) / axis_pairs.astype(jnp.float32)) * math.log(rope_theta)
    )
    selector = jnp.stack([in_time, in_height, in_width]).astype(jnp.float32) * frequency[None, :]
    placed = positions.astype(jnp.float32)
    return (
        placed[0][:, None] * selector[0][None, :]
        + placed[1][:, None] * selector[1][None, :]
        + placed[2][:, None] * selector[2][None, :]
    )


def rotate(features, angle_table):
    row_total = features.shape[0]
    heads_here = features.shape[1] // HD
    paired = features.astype(jnp.float32).reshape(row_total, heads_here, HD // 2, 2)
    cosine = jnp.cos(angle_table)[:, None, :]
    sine_part = jnp.sin(angle_table)[:, None, :]
    real_part = paired[..., 0]
    imag_part = paired[..., 1]
    turned = jnp.stack(
        [real_part * cosine - imag_part * sine_part, real_part * sine_part + imag_part * cosine],
        axis=-1,
    )
    return turned.reshape(row_total, heads_here * HD).astype(jnp.bfloat16)


def video_of(global_rows, video_ends, row_count):
    inside = (global_rows >= 0) & (global_rows < row_count)
    counted = jnp.sum((video_ends[None, :] <= global_rows[:, None]).astype(jnp.int32), axis=1)
    return jnp.where(inside, counted, -1)


def attend_masked(query_block, key_block, value_block, query_video, key_video):
    rows_here = query_block.shape[0]
    feature_count = query_block.shape[1]
    heads_here = feature_count // HD
    key_count = key_block.shape[0]
    same_video = query_video[:, None] == key_video[None, :]
    score_scale = 1.0 / math.sqrt(HD)
    query_heads = query_block.reshape(rows_here, heads_here, HD).transpose(1, 0, 2)
    key_heads = key_block.reshape(key_count, heads_here, HD).transpose(1, 0, 2)
    value_heads = value_block.reshape(key_count, heads_here, HD).transpose(1, 0, 2)

    def one_head(operands):
        query_head, key_head, value_head = operands
        scores = jnp.dot(query_head, key_head.T, preferred_element_type=jnp.float32) * score_scale
        scores = jnp.where(same_video, scores, masked_score)
        row_max = jnp.max(scores, axis=1, keepdims=True)
        weights = jnp.exp(scores - row_max)
        denominator = jnp.sum(weights, axis=1, keepdims=True)
        summed = jnp.dot(
            weights.astype(jnp.bfloat16), value_head, preferred_element_type=jnp.float32
        )
        return (summed / denominator).astype(jnp.bfloat16)

    outputs = lax.map(one_head, (query_heads, key_heads, value_heads))
    return outputs.transpose(1, 0, 2).reshape(rows_here, feature_count)


def project(attended, modulation, w_head):
    widened = attended.astype(jnp.float32)
    mean_square = jnp.mean(widened * widened, axis=1, keepdims=True)
    normed = (
        widened * lax.rsqrt(mean_square + 1e-06) * (1.0 + modulation[1][None, :])
        + modulation[0][None, :]
    )
    return jnp.dot(normed.astype(jnp.bfloat16), w_head, preferred_element_type=jnp.float32)


def step_rows(video_ids, step_sizes):
    video_count = step_sizes.shape[0]
    chosen = video_ids[:, None] == jnp.arange(video_count, dtype=jnp.int32)[None, :]
    return jnp.sum(
        jnp.where(chosen, step_sizes[None, :], jnp.zeros_like(step_sizes)[None, :]), axis=1
    )


def per_device(
    query_rows,
    key_rows,
    value_rows,
    positions,
    latents,
    w_head,
    modulation,
    guide_scale,
    step_sizes,
    lengths,
):
    rows_here = query_rows.shape[1]
    feature_count = query_rows.shape[2]
    row_count = rows_here * lax.axis_size("req")
    first_row = lax.axis_index("req") * rows_here
    angle_table = angles(positions)
    video_ends = jnp.cumsum(lengths)
    query_rot = rotate(query_rows[0], angle_table)
    key_rot = rotate(key_rows[0], angle_table)
    stacked = jnp.concatenate([query_rot, key_rot, value_rows[0]], axis=1)
    incoming = shifted(stacked, "req", -1)
    all_rows = jnp.concatenate([stacked, incoming], axis=0)
    global_rows = first_row + jnp.arange(rows_here + LMAX, dtype=jnp.int32)
    row_video = video_of(global_rows, video_ends, row_count)
    video_starts = video_ends - lengths
    matched = row_video[:, None] == jnp.arange(video_starts.shape[0], dtype=jnp.int32)[None, :]
    row_start = jnp.sum(jnp.where(matched, video_starts[None, :], 0), axis=1)
    owned = (row_video >= 0) & (row_start >= first_row) & (row_start < first_row + rows_here)
    key_video = jnp.where(owned, row_video, -1)
    attended = attend_masked(
        all_rows[:, :feature_count],
        all_rows[:, feature_count : 2 * feature_count],
        all_rows[:, 2 * feature_count :],
        row_video,
        key_video,
    )
    computed = project(attended, modulation, w_head)
    returned = shifted(computed[rows_here:], "req", 1)
    filler = jnp.zeros((rows_here - LMAX, computed.shape[1]), jnp.float32)
    returned_rows = jnp.concatenate([returned, filler], axis=0)
    velocity = jnp.where(owned[:rows_here, None], computed[:rows_here], returned_rows)
    parity = lax.axis_index("cfg")
    video_ids = video_of(first_row + jnp.arange(rows_here, dtype=jnp.int32), video_ends, row_count)
    steps_here = step_rows(video_ids, step_sizes)
    half_cols = latents.shape[1]
    own_start = parity * half_cols
    partner = from_partner(velocity, "cfg", 0)
    conditional = jnp.where(parity == 0, velocity, partner)
    unconditional = jnp.where(parity == 0, partner, velocity)
    guided = unconditional + guide_scale[0] * (conditional - unconditional)
    own_guided = lax.dynamic_slice_in_dim(guided, own_start, half_cols, 1)
    return latents + steps_here[:, None] * own_guided


def solution(mesh):
    in_specs = (
        P("cfg", "req", None),
        P("cfg", "req", None),
        P("cfg", "req", None),
        P(None, "req"),
        P("req", "cfg"),
        P(),
        P(),
        P(),
        P(),
        P(),
    )
    out_specs = P("req", "cfg")
    return jax.shard_map(
        per_device, mesh=mesh, in_specs=in_specs, out_specs=out_specs, check_vma=False
    )
```

profile of v0, /device:TPU:25, one launch (start us, length us, event | category | flops | bytes accessed | tf_op | source)
XLA Modules:
  0.0 426.5 jit_solution(7666185514573223956)
XLA Ops:
  0.8 4.9 %copy.18 = f32[1,512,2560]{1,2,0:T(8,128)} copy(bf16[1,512,2560]{2,1,0:T(8,128)(2,1)} %param.12) | data formatting | bytes 7864320 | tf_op jit(solution)/shard_map/convert_element_type | solution.py:53
  5.7 7.7 %reshape.319 = f32[512,20,64,2]{0,3,2,1:T(2,128)} reshape(f32[1,512,2560]{1,2,0:T(8,128)} %copy.18) | data formatting | bytes 10485760 | tf_op jit(solution)/shard_map/convert_element_type | solution.py:53
  13.4 3.2 copy.19
  16.6 7.6 %reshape.320 = f32[512,20,64,2]{0,3,2,1:T(2,128)} reshape(f32[1,512,2560]{1,2,0:T(8,128)} %copy.19) | data formatting | bytes 10485760 | tf_op jit(solution)/shard_map/convert_element_type | solution.py:53
  24.7 16.5 %subtract_convert_fusion.1 = (bf16[512,20,64,1]{0,3,2,1:T(2,128)(2,1)S(1)}, bf16[512,20,64,1]{0,3,2,1:T(2,128)(2,1)S(1)}, bf16[512,20,64,1]{0,3,2,1:T(2,128)(2,1)}, bf16[512,20,64,1]{0,3,2,1:T(2,128)(2,1)}) fusion(f32[512,20,64,2]{0,3,2,1:T(2,128)} %reshape.319, f32[512,64]{0,1:T(8,128)S(1)} %get-tuple-element.105, f32[512,64]{0,1:T(8,128)S(1)} %get-tuple-element.104, ...), kind=kLoop, calls=%fused_computation.35 | loop fusion | flops 10485760 | bytes 15990784 | tf_op jit(solution)/shard_map/convert.6
  41.3 6.3 %pad_maximum_fusion.2 = bf16[512,20,64,2]{0,3,2,1:T(2,128)(2,1)} fusion(bf16[512,20,64,1]{0,3,2,1:T(2,128)(2,1)S(1)} %get-tuple-element.96, bf16[512,20,64,1]{0,3,2,1:T(2,128)(2,1)S(1)} %get-tuple-element.95), kind=kLoop, calls=%fused_computation.30 | loop fusion | flops 5242880 | bytes 5242880 | tf_op jit(solution)/shard_map/stack | solution.py:58
  47.6 3.8 convert_element_type.75
  51.3 8.1 %pad_maximum_fusion.3 = bf16[512,20,64,2]{0,3,2,1:T(2,128)(2,1)} fusion(bf16[512,20,64,1]{0,3,2,1:T(2,128)(2,1)} %get-tuple-element.99, bf16[512,20,64,1]{0,3,2,1:T(2,128)(2,1)} %get-tuple-element.100), kind=kLoop, calls=%fused_computation.31 | loop fusion | flops 5242880 | bytes 5242880 | tf_op jit(solution)/shard_map/stack | solution.py:58
  59.4 5.1 %convert_element_type.78 = bf16[512,2560]{0,1:T(8,128)(2,1)} reshape(bf16[512,20,64,2]{0,3,2,1:T(2,128)(2,1)} %pad_maximum_fusion.3) | data formatting | bytes 5242880 | tf_op jit(solution)/shard_map/convert_element_type | solution.py:62
  64.6 4.5 %copy.20 = bf16[1,512,2560]{1,2,0:T(8,128)(2,1)} copy(bf16[1,512,2560]{2,1,0:T(8,128)(2,1)} %param.14) | data formatting | bytes 5242880 | tf_op args[2]
  69.0 6.3 %pad_maximum_fusion.1 = bf16[512,7680]{0,1:T(8,128)(2,1)} fusion(bf16[512,2560]{0,1:T(8,128)(2,1)} %bitcast.71, bf16[512,2560]{0,1:T(8,128)(2,1)} %convert_element_type.78, bf16[512,2560]{0,1:T(8,128)(2,1)S(1)} %convert_element_type.75), kind=kLoop, calls=%fused_computation.29 | loop fusion | flops 23592960 | bytes 15728640 | tf_op jit(solution)/shard_map/concatenate | solution.py:136
  75.4 10.0 %collective-permute-start = (bf16[512,7680]{0,1:T(8,128)(2,1)}, bf16[512,7680]{0,1:T(8,128)(2,1)}, u32[]{:S(2)}, u32[]{:S(2)}) collective-permute-start(bf16[512,7680]{0,1:T(8,128)(2,1)} %pad_maximum_fusion.1), channel_id=1, source_target_pairs={{1,0},{2,1},{3,2},{4,3},{5,4},{6,5},{7,6},{8,7},{9,8},{10,9},{11,1... | collective-permute-start | bytes 23592968 | tf_op jit(solution)/shard_map/ppermute | solution.py:19
  86.9 166.5 %collective-permute-done = bf16[512,7680]{0,1:T(8,128)(2,1)} collective-permute-done((bf16[512,7680]{0,1:T(8,128)(2,1)}, bf16[512,7680]{0,1:T(8,128)(2,1)}, u32[]{:S(2)}, u32[]{:S(2)}) %collective-permute-start) | collective-permute-done | bytes 7864352 | tf_op jit(solution)/shard_map/ppermute | solution.py:19
  253.4 23.2 %pad_maximum_fusion = bf16[1024,7680]{0,1:T(8,128)(2,1)S(1)} fusion(bf16[512,7680]{0,1:T(8,128)(2,1)} %collective-permute-done, bf16[512,2560]{0,1:T(8,128)(2,1)} %bitcast.72, bf16[512,2560]{0,1:T(8,128)(2,1)} %convert_element_type.78, bf16[512,2560]{0,1:T(8,128)(2,1)S(1)} %convert_element_type.75), kind=kLoop, calls=%fused_computation.23 | loop fusion | flops 62914560 | bytes 31457280 | tf_op jit(solution)/shard_map/concatenate | solution.py:138
  276.6 6.2 %fusion.40 = (bf16[1024,2560]{0,1:T(8,128)(2,1)}, bf16[1024,2560]{0,1:T(8,128)(2,1)}, bf16[1024,2560]{0,1:T(8,128)(2,1)}) fusion(bf16[1024,7680]{0,1:T(8,128)(2,1)S(1)} %pad_maximum_fusion), kind=kLoop, calls=%fused_computation.77 | loop fusion | bytes 31457280 | tf_op jit(solution)/shard_map/slice | solution.py:149
  282.8 121.9 %while.11 = (s32[]{:T(128)}, bf16[20,1024,128]{1,2,0:T(8,128)(2,1)}, bf16[20,1024,128]{1,2,0:T(8,128)(2,1)}, bf16[20,1024,128]{1,2,0:T(8,128)(2,1)}, bf16[20,102...) while((s32[]{:T(128)}, bf16[20,1024,128]{1,2,0:T(8,128)(2,1)}, ...), condition=%wide.region_9.10_spmd.clone, body=%wide.region_6.9_spmd.clone.sunk | while | flops 551811072 | bytes 14727253 | solution.py:94
  291.8 2.2 fusion.54
  297.9 2.2 fusion.54
  316.2 2.2 fusion.54
  340.6 2.2 fusion.54
  365.0 2.2 fusion.54
  404.7 3.8 multiply_reduce_fusion
  413.9 8.5 %collective-permute-done.1 = f32[512,64]{0,1:T(8,128)S(1)} collective-permute-done((f32[512,64]{0,1:T(8,128)S(1)}, f32[512,64]{0,1:T(8,128)S(1)}, u32[]{:S(2)}, u32[]{:S(2)}) %collective-permute-start.1) | collective-permute-done | bytes 131104 | tf_op jit(solution)/shard_map/ppermute | solution.py:19
  422.4 2.5 collective-permute-start.2
  (142 shorter events, 119.1 us)
Async XLA Ops:
  0.0 410.6 %copy-start = (bf16[2560,64]{0,1:T(8,128)(2,1)S(1)}, bf16[2560,64]{0,1:T(8,128)(2,1)}, u32[]{:S(2)}) copy-start(bf16[2560,64]{0,1:T(8,128)(2,1)} %param.17) | copy-start | bytes 983044
  5.7 7.7 %copy-start.2 = (bf16[1,512,2560]{2,1,0:T(8,128)(2,1)S(1)}, bf16[1,512,2560]{2,1,0:T(8,128)(2,1)}, u32[]{:S(2)}) copy-start(bf16[1,512,2560]{2,1,0:T(8,128)(2,1)} %param.13) | copy-start | bytes 7864324
  69.0 16.4 %copy-start.5 = (s32[256]{0:T(256)S(1)}, s32[256]{0:T(256)}, u32[]{:S(2)}) copy-start(s32[256]{0:T(256)} %param.21) | copy-start | bytes 3076
  69.0 17.0 %copy-start.4 = (f32[2,2560]{1,0:T(2,128)S(1)}, f32[2,2560]{1,0:T(2,128)}, u32[]{:S(2)}) copy-start(f32[2,2560]{1,0:T(2,128)} %param.18) | copy-start | bytes 61444
  75.4 178.1 %collective-permute-start = (bf16[512,7680]{0,1:T(8,128)(2,1)}, bf16[512,7680]{0,1:T(8,128)(2,1)}, u32[]{:S(2)}, u32[]{:S(2)}) collective-permute-start(bf16[512,7680]{0,1:T(8,128)(2,1)} %pad_maximum_fusion.1), channel_id=1, source_target_pairs={{1,0},{2,1},{3,2},{4,3},{5,4},{6,5},{7,6},{8,7},{9,8},{10,9},{11,1... | collective-permute-start | bytes 23592968 | tf_op jit(solution)/shard_map/ppermute | solution.py:19
  404.7 4.0 copy-start.1
  410.6 15.0 %copy-start.6 = (f32[256]{0:T(256)S(1)}, f32[256]{0:T(256)}, u32[]{:S(2)}) copy-start(f32[256]{0:T(256)} %param.20) | copy-start | bytes 3076
  410.6 15.3 %copy-start.3 = (f32[512,32]{0,1:T(8,128)S(1)}, f32[512,32]{0,1:T(8,128)}, u32[]{:S(2)}) copy-start(f32[512,32]{0,1:T(8,128)} %param.16) | copy-start | bytes 196612
  411.7 10.7 %collective-permute-start.1 = (f32[512,64]{0,1:T(8,128)S(1)}, f32[512,64]{0,1:T(8,128)S(1)}, u32[]{:S(2)}, u32[]{:S(2)}) collective-permute-start(f32[512,64]{0,1:T(8,128)S(1)} %slice.92), channel_id=1, source_target_pairs={{0,1},{1,2},{2,3},{3,4},{4,5},{5,6},{6,7},{7,8},{8,9},{9,10},{10,1... | collective-permute-start | bytes 393224 | tf_op jit(solution)/shard_map/ppermute | solution.py:19
  422.4 3.5 collective-permute-start.2
where the time goes:
time: 428 us; the launch traced here: 427 us
  waiting for transfers between devices  175 us (41%)
  other arithmetic  90.4 us (21%)
  matrix products  84.1 us (20%)
  local copies, waits for them, and re-layouts  60.9 us (14%)
  starting transfers between devices  14.4 us (3%)
    ppermute x2, waiting for transfers between devices, shifted(): lax.ppermute(value, axis, [(source, source + steps) for source in range(l...  175 us
    dot_general x20, matrix products, one_head(): jnp.dot(weights.astype(jnp.bfloat16), value_head, preferred_element_type=...  44.9 us
    dot_general x20, matrix products, one_head(): jnp.dot(query_head, key_head.T, preferred_element_type=jnp.float32)  38.1 us
    convert_element_type x4, local copies, waits for them, and re-layouts, rotate(): features.astype(jnp.float32).reshape(row_total, heads_here, HD // 2, 2)  23.4 us
    concatenate x1, other arithmetic, per_device(): all_rows = jnp.concatenate([stacked, incoming], axis=0)  23.2 us
    reduce_sum x20, other arithmetic, one_head(): denominator = jnp.sum(weights, axis=1, keepdims=True)  20.6 us
    dynamic_update_slice x40, local copies, waits for them, and re-layouts, attend_masked(): outputs = lax.map(one_head, (query_heads, key_heads, value_heads))  17.5 us
    another operation x3, other arithmetic  16.9 us
  transfers between devices with their start and end apart: 3, of which 3 were waited for; matrix products, arithmetic and copies ran while one was open for 0% of the time, Pallas kernels for 0%

commit v1 on v0

v1 whole, which is shorter than its diff:
```python
import functools
import math

import jax
import jax.numpy as jnp
import numpy as np
from jax import lax
from jax.experimental import pallas as pl
from jax.experimental.pallas import tpu as pltpu
from jax.sharding import PartitionSpec as P


HD = 128
ROWS = 512
LATC = 64
TILE = 16
TILES = ROWS // TILE
FAR = 24
REACH = FAR * TILE
SPAN = 2 * ROWS + 128
ACCR = 72
masked_score = -1e30
rope_theta = 10000.0
MESH = pl.DeviceIdType.MESH
SMEM = pl.BlockSpec(memory_space=pltpu.SMEM)
VMEM = pl.BlockSpec(memory_space=pltpu.VMEM)
ANY = pl.BlockSpec(memory_space=pl.ANY)


def share_static(ta, tb, heads):
    if ta > FAR:
        return 0
    if tb > FAR:
        return heads
    costs = [max(n * ta, (heads - n) * tb) for n in range(heads + 1)]
    return costs.index(min(costs))


def capacity(heads):
    most = 0
    for ta in range(1, TILES + 1):
        for tb in range(1, TILES + 2 - ta):
            n = share_static(ta, tb, heads)
            most = max(most, n * ta, (heads - n) * tb)
    return most


def chunk_tiles(heads):
    cap = capacity(heads)
    if cap >= 150:
        return (48, 48, 42, cap - 138)
    return (FAR, cap - FAR)


def share(ta, tb, heads):
    best = heads * tb
    chosen = jnp.int32(0)
    for n in range(1, heads + 1):
        cost = jnp.maximum(n * ta, (heads - n) * tb)
        better = cost < best
        best = jnp.where(better, cost, best)
        chosen = jnp.where(better, n, chosen)
    chosen = jnp.where(tb > FAR, heads, chosen)
    return jnp.where(ta > FAR, 0, chosen)


def selector():
    pair_total = HD // 2
    side = HD // 6
    time = pair_total - 2 * side
    axis = np.array([0] * time + [1] * side + [2] * side)
    local = np.array(list(range(time)) + list(range(side)) * 2, np.float32)
    pairs = np.array([time] * time + [side] * (2 * side), np.float32)
    frequency = np.exp(-(local / pairs) * np.float32(math.log(rope_theta))).astype(np.float32)
    table = np.zeros((4, TILE, HD), np.float32)
    for group in range(4):
        for lane in range(HD):
            table[group, axis[lane // 2] * 4 + group, lane] = frequency[lane // 2]
    parts = []
    rest = table
    for _ in range(3):
        part = rest.astype(jnp.bfloat16)
        parts.append(part)
        rest = rest - part.astype(np.float32)
    return np.stack(parts)


def turner():
    table = np.zeros((HD, HD), np.float32)
    for pair in range(HD // 2):
        table[2 * pair + 1, 2 * pair] = -1.0
        table[2 * pair, 2 * pair + 1] = 1.0
    return table.astype(jnp.bfloat16)


def cdiv(value, unit):
    return (value + unit - 1) // unit


def pack_kernel(heads, chunks, lens_ref, pos_ref, q_ref, k_ref, v_ref, scal_ref, place_ref, *rest):
    count = len(chunks)
    right_refs, left_refs = rest[:count], rest[count : 2 * count]
    rows_in, packed, in_sem, out_sem = rest[2 * count :]
    groups = 4 if heads % 4 == 0 else 1
    width = heads // groups * HD
    loads = []
    for group in range(groups):
        columns = pl.ds(group * width, width)
        for j, source in enumerate((q_ref, k_ref, v_ref)):
            copy = pltpu.make_async_copy(
                source.at[:, :, columns],
                rows_in.at[j, pl.ds(0, TILES), :, columns],
                in_sem.at[group, j],
            )
            copy.start()
            loads.append(copy)
    low = lax.axis_index("req") * ROWS
    high = low + ROWS

    def scan(i, carry):
        end, start_low, end_low, start_high, end_high = carry
        start = end
        end = start + lens_ref[i]
        before_low = start < low
        before_high = start < high
        return (
            end,
            jnp.where(before_low, start, start_low),
            jnp.where(before_low, end, end_low),
            jnp.where(before_high, start, start_high),
            jnp.where(before_high, end, end_high),
        )

    zero = jnp.int32(0)
    _, start_low, end_low, start_high, end_high = lax.fori_loop(
        0, lens_ref.shape[0], scan, (zero, low, low, high, high), unroll=8
    )
    cut_low = end_low > low
    cut_high = end_high > high
    a_low = jnp.where(cut_low, low - start_low, 0)
    b_low = jnp.where(cut_low, end_low - low, 0)
    a_high = jnp.where(cut_high, high - start_high, 0)
    b_high = jnp.where(cut_high, end_high - high, 0)
    n_low = share(cdiv(a_low, TILE), cdiv(b_low, TILE), heads)
    n_high = share(cdiv(a_high, TILE), cdiv(b_high, TILE), heads)
    for i, value in enumerate((a_low, b_low, n_low, a_high, b_high, n_high)):
        scal_ref[i] = value
    scal_ref[6] = zero
    scal_ref[7] = zero

    placed = pos_ref[...].astype(jnp.float32)
    pieces = [placed[a : a + 1, g * HD : (g + 1) * HD] for a in range(3) for g in range(4)]
    pieces.append(jnp.zeros((TILE - 12, HD), jnp.float32))
    place_ref[...] = jnp.concatenate(pieces, axis=0).astype(jnp.bfloat16)
    for copy in loads:
        copy.wait()

    def pack(direction, first_tile, first_head, tiles, total):
        def one(slot, carry):
            columns = pl.ds(pl.multiple_of((first_head + slot) * HD, HD), HD)
            for j in range(3):
                packed[direction, j, pl.ds(slot * tiles, FAR)] = rows_in[
                    j, pl.ds(first_tile, FAR), :, columns
                ]
            return carry

        lax.fori_loop(0, total, one, 0)

    ta, tb = cdiv(a_high, TILE), cdiv(b_low, TILE)
    pack(0, TILES - ta, 0, ta, jnp.where(a_high > 0, n_high, 0))
    pack(1, 0, n_low, tb, jnp.where(b_low > 0, heads - n_low, 0))
    stores = []
    for direction, targets in enumerate((right_refs, left_refs)):
        begin = 0
        for c, tiles in enumerate(chunks):
            copy = pltpu.make_async_copy(
                packed.at[direction, :, pl.ds(begin, tiles)],
                targets[c].at[:, pl.ds(0, tiles)],
                out_sem.at[direction, c],
            )
            copy.start()
            stores.append(copy)
            begin += tiles
        copy = pltpu.make_async_copy(
            place_ref, targets[0].at[0, chunks[0]], out_sem.at[direction, count]
        )
        copy.start()
        stores.append(copy)
    for copy in stores:
        copy.wait()


def tables(place, select_ref, groups):
    parts = []
    for group in groups:
        angle = None
        for part in range(3):
            term = lax.dot_general(
                place,
                select_ref[part, group],
                (((0,), (0,)), ((), ())),
                preferred_element_type=jnp.float32,
            )
            angle = term if angle is None else angle + term
        parts.append(angle)
    angle = jnp.concatenate(parts, axis=0)
    return jnp.cos(angle), jnp.sin(angle)


def rotate(x, cosine, sine, turn):
    swapped = jnp.dot(x, turn, preferred_element_type=jnp.float32)
    return x.astype(jnp.float32) * cosine + swapped * sine


def attend(q, k, v, bias):
    scale = math.log2(math.e) / math.sqrt(HD)
    scores = lax.dot_general(q, k, (((1,), (1,)), ((), ())), preferred_element_type=jnp.float32)
    scores = scores * scale + bias
    top = jnp.max(scores, axis=1, keepdims=True)
    weight = jnp.exp2(scores - top)
    total = jnp.sum(weight, axis=1, keepdims=True)
    summed = jnp.dot(weight.astype(jnp.bfloat16), v, preferred_element_type=jnp.float32)
    return (summed * (1.0 / total)).astype(jnp.bfloat16)


def head_weights(w_block, scale_row):
    scaled = (w_block.astype(jnp.float32) * (1.0 + scale_row)).astype(jnp.bfloat16)
    zeros = jnp.zeros((HD - LATC, HD), jnp.bfloat16)
    first = jnp.concatenate([scaled, zeros], axis=0)
    row = lax.broadcasted_iota(jnp.int32, (HD, HD), 0)
    second = (row == LATC).astype(jnp.bfloat16)
    return jnp.concatenate([first, second], axis=1)


def contribution(attended, weights):
    wide = attended.astype(jnp.float32)
    squared = (wide * wide).astype(jnp.bfloat16)
    joined = jnp.concatenate([attended, squared], axis=1)
    return lax.dot_general(
        joined, weights, (((1,), (1,)), ((), ())), preferred_element_type=jnp.float32
    )


def local_kernel(
    scal_ref, place_ref, select_ref, turn_ref, seg_row_ref, seg_col_ref,
    q_ref, k_ref, v_ref, w_ref, mod_ref, turned_ref, acc_ref, cos_ref, sin_ref, bias_ref,
):
    head = pl.program_id(0)

    @pl.when(head == 0)
    def _():
        cosine, sine = tables(place_ref[...], select_ref, range(4))
        cos_ref[...] = cosine
        sin_ref[...] = sine
        same = seg_col_ref[...] == seg_row_ref[...]
        bias_ref[...] = jnp.where(same, 0.0, masked_score)
        acc_ref[...] = jnp.zeros_like(acc_ref)

    turn = turn_ref[...]
    turned_ref[0, 0] = rotate(q_ref[...], cos_ref[...], sin_ref[...], turn).astype(jnp.bfloat16)
    turned_ref[0, 1] = rotate(k_ref[...], cos_ref[...], sin_ref[...], turn).astype(jnp.bfloat16)
    turned_ref[0, 2] = v_ref[...]
    first = scal_ref[1]
    last = ROWS - scal_ref[3]
    start = jnp.minimum(first // HD * HD, ROWS // 2)
    narrow = last <= start + ROWS // 2
    weights = head_weights(w_ref[...], mod_ref[1:2, :])

    def run(begin, width):
        keys = turned_ref[0, 1, pl.ds(begin, width)]
        values = turned_ref[0, 2, pl.ds(begin, width)]
        for part in range(width // 128):
            rows = pl.ds(begin + part * 128, 128)
            bias = bias_ref[rows, pl.ds(begin, width)]
            attended = attend(turned_ref[0, 0, rows], keys, values, bias)
            acc_ref[rows] += contribution(attended, weights)

    @pl.when((first < last) & narrow)
    def _():
        run(pl.multiple_of(start, HD), ROWS // 2)

    @pl.when((first < last) & jnp.logical_not(narrow))
    def _():
        run(0, ROWS)


def cut_kernel(heads, chunks, c, *refs):
    final = c == len(chunks) - 1
    refs = list(refs)
    scal_ref, select_ref, turn_ref, w_ref, mod_ref, turned_ref = refs[:6]
    del refs[:6]
    here = [i for i in (c - 1, c) if i >= 0]
    sources = [refs[: len(here)], refs[len(here) : 2 * len(here)]]
    del refs[: 2 * len(here)]
    if c == 0:
        acc_ref, table_ref = refs[:2]
        del refs[:2]
    else:
        table_ref, before_ref = refs[:2]
        del refs[:2]
        if final:
            local_ref, own_ref, left_out, right_out, shift_ref = refs[:5]
            del refs[:5]
        else:
            acc_ref = refs.pop(0)
    if final:
        span, mine, recv, loc_sem, recv_sem, acc_ref = refs
    else:
        span, mine, recv, loc_sem, recv_sem = refs
    begins = [sum(chunks[:i]) for i in range(len(chunks) + 1)]
    base = begins[here[0]]
    loads = []
    for side in range(2):
        for i, index in enumerate(here):
            copy = pltpu.make_async_copy(
                sources[side][i].at[:, pl.ds(0, chunks[index])],
                recv.at[side, :, pl.ds(FAR + begins[index] - base, chunks[index])],
                recv_sem.at[side, i],
            )
            copy.start()
            loads.append(copy)
    if c == 0:
        place_copies = []
        for side in range(2):
            copy = pltpu.make_async_copy(
                sources[side][0].at[0, chunks[0]], recv.at[side, 0, 0], recv_sem.at[side, 2]
            )
            copy.start()
            place_copies.append(copy)
    a_low, b_low, n_low = scal_ref[0], scal_ref[1], scal_ref[2]
    a_high, b_high, n_high = scal_ref[3], scal_ref[4], scal_ref[5]
    ta_low = cdiv(a_low, TILE)
    tb_high = cdiv(b_high, TILE)

    def done(limit, tiles, total):
        if limit == 0:
            return jnp.int32(0)
        return jnp.where(tiles > 0, jnp.minimum(total, limit // jnp.maximum(tiles, 1)), 0)

    low_first = done(begins[c], ta_low, n_low)
    low_count = done(begins[c + 1], ta_low, n_low) - low_first
    high_first = done(begins[c], tb_high, heads - n_high)
    high_count = done(begins[c + 1], tb_high, heads - n_high) - high_first
    items = low_count + high_count

    def slot_of(i):
        return jnp.where(i < low_count, low_first + i, high_first + i - low_count)

    def head_of(i):
        return jnp.where(i < low_count, low_first + i, n_high + high_first + i - low_count)

    def fetch(i, buffer):
        return pltpu.make_async_copy(turned_ref.at[head_of(i)], mine.at[buffer], loc_sem.at[buffer])

    @pl.when(items > 0)
    def _():
        fetch(jnp.int32(0), 0).start()

    span[...] = jnp.zeros_like(span)
    if c == 0:
        acc_ref[...] = jnp.zeros_like(acc_ref)
        for side, copy in enumerate(place_copies):
            copy.wait()
            groups = range(1, 4) if side == 0 else range(3)
            cosine, sine = tables(recv[side, 0, 0], select_ref, groups)
            table_ref[side, 0] = cosine
            table_ref[side, 1] = sine
    else:
        acc_ref[...] = before_ref[...]
    for copy in loads:
        copy.wait()
    turn = turn_ref[...]

    def one(i, carry):
        buffer = lax.rem(i, 2)
        fetch(i, buffer).wait()

        @pl.when(i + 1 < items)
        def _():
            fetch(i + 1, 1 - buffer).start()

        side = (i >= low_count).astype(jnp.int32)
        is_low = side == 0
        slot = slot_of(i)
        head = head_of(i)
        a = jnp.where(is_low, a_low, a_high)
        b = jnp.where(is_low, b_low, b_high)
        ta, tb = cdiv(a, TILE), cdiv(b, TILE)
        offset = jnp.where(is_low, slot * ta + ta, slot * tb + FAR) - base
        row = lax.broadcasted_iota(jnp.int32, (REACH, HD), 0)
        keep = (row >= jnp.where(is_low, REACH - ta * TILE, 0)) & (
            row < jnp.where(is_low, REACH, tb * TILE)
        )
        cosine, sine = table_ref[side, 0], table_ref[side, 1]
        target = pl.ds(pl.multiple_of(jnp.where(is_low, ROWS - REACH, ROWS), 128), REACH)
        for j in range(3):
            x = recv[side, j, pl.ds(offset, FAR)].reshape(REACH, HD)
            if j < 2:
                x = rotate(x, cosine, sine, turn)
            else:
                x = x.astype(jnp.float32)
            span[j, target] = jnp.where(keep, x, 0.0).astype(jnp.bfloat16)
        for j in range(3):
            span[j, pl.ds(pl.multiple_of(jnp.where(is_low, ROWS, 0), ROWS), ROWS)] = mine[buffer, j]
        columns = pl.ds(pl.multiple_of(head * HD, HD), HD)
        weights = head_weights(w_ref[:, columns], mod_ref[1:2, columns])
        start = pl.multiple_of(ROWS - ta * TILE, TILE)
        extent = (ta + tb) * TILE

        def run(width):
            keys = span[1, pl.ds(start, width)]
            values = span[2, pl.ds(start, width)]
            lane = lax.broadcasted_iota(jnp.int32, (1, width), 1)
            valid = (lane >= ta * TILE - a) & (lane < ta * TILE + b)
            bias = jnp.where(valid, 0.0, masked_score)
            for part in range(width // 128):
                rows = pl.ds(pl.multiple_of(start + part * 128, TILE), 128)
                attended = attend(span[0, rows], keys, values, bias)
                acc_ref[side, rows] += contribution(attended, weights)

        below = 0
        for width in (256, 384, 512, 640):

            @pl.when((extent > below) & (extent <= width))
            def _(width=width):
                run(width)

            below = width
        return carry

    lax.fori_loop(0, items, one, 0)
    if final:
        row = lax.broadcasted_iota(jnp.int32, (ROWS, HD), 0)
        own = jnp.where(row < b_low, acc_ref[0, ROWS : 2 * ROWS], 0.0)
        own = own + jnp.where(row >= ROWS - a_high, acc_ref[1, 0:ROWS], 0.0)
        own = own + jnp.where((row >= b_low) & (row < ROWS - a_high), local_ref[...], 0.0)
        own_ref[...] = own.T[:ACCR]
        row = lax.broadcasted_iota(jnp.int32, (REACH, HD), 0)
        back = jnp.where(row >= REACH - a_low, acc_ref[0, ROWS - REACH : ROWS], 0.0)
        left_out[...] = back.T[:ACCR]
        back = jnp.where(row < b_high, acc_ref[1, ROWS : ROWS + REACH], 0.0)
        right_out[...] = back.T[:ACCR]
        shift = jnp.sum(w_ref[...].astype(jnp.float32) * mod_ref[0:1, :], axis=1, keepdims=True)
        shift_ref[...] = jnp.broadcast_to(shift, (LATC, HD))


def finish_kernel(
    features, ring, own_ref, left_ref, right_ref, shift_ref, guide_ref, out_ref,
    from_left, from_right, velocity, other, send_sem, recv_sem,
):
    me = lax.axis_index("req")
    parity = lax.axis_index("cfg")
    left, right = lax.rem(me + ring - 1, ring), lax.rem(me + 1, ring)
    partner = {"cfg": 1 - parity}
    barrier = pltpu.get_barrier_semaphore()
    for target in ({"req": left}, {"req": right}, partner):
        pl.semaphore_signal(barrier, inc=1, device_id=target, device_id_type=MESH)
    pl.semaphore_wait(barrier, 3)
    to_left = pltpu.make_async_remote_copy(
        left_ref, from_right, send_sem.at[0], recv_sem.at[0],
        device_id={"req": left}, device_id_type=MESH,
    )
    to_left.start()
    to_right = pltpu.make_async_remote_copy(
        right_ref, from_left, send_sem.at[1], recv_sem.at[1],
        device_id={"req": right}, device_id_type=MESH,
    )
    to_right.start()
    to_left.wait()
    to_right.wait()
    none = jnp.zeros((ACCR, ROWS - REACH), jnp.float32)
    total = own_ref[...]
    total = total + jnp.concatenate([none, from_right[...]], axis=1)
    total = total + jnp.concatenate([from_left[...], none], axis=1)
    inverse = lax.rsqrt(total[LATC : LATC + 1] * (1.0 / features) + 1e-06)
    velocity[...] = total[:LATC] * inverse + shift_ref[:, 0:1]
    half = LATC // 2
    give = pltpu.make_async_remote_copy(
        velocity.at[pl.ds(pl.multiple_of((1 - parity) * half, half), half)],
        other, send_sem.at[2], recv_sem.at[2], device_id=partner, device_id_type=MESH,
    )
    give.start()
    kept = velocity[pl.ds(pl.multiple_of(parity * half, half), half)]
    give.wait()
    theirs = other[...]
    conditional = jnp.where(parity == 0, kept, theirs)
    unconditional = jnp.where(parity == 0, theirs, kept)
    out_ref[...] = unconditional + guide_ref[0] * (conditional - unconditional)


def moved(value, step, ring):
    return lax.ppermute(value, "req", [(i, (i + step) % ring) for i in range(ring)])


def per_device(
    query_rows, key_rows, value_rows, positions, latents, w_head, modulation, guide_scale,
    step_sizes, lengths,
):
    features = query_rows.shape[2]
    heads = features // HD
    ring = lax.axis_size("req")
    chunks = chunk_tiles(heads)
    count = len(chunks)
    bf16, f32 = jnp.bfloat16, jnp.float32
    sized = jax.ShapeDtypeStruct
    q, k, v = query_rows[0], key_rows[0], value_rows[0]

    def tiled(x):
        return x.reshape(TILES, TILE, features)

    shapes = [sized((3, t + (i == 0), TILE, HD), bf16) for i, t in enumerate(chunks)]
    packed_tiles = sum(chunks) + FAR
    outs = pl.pallas_call(
        functools.partial(pack_kernel, heads, chunks),
        out_shape=[sized((8,), jnp.int32), sized((TILE, HD), bf16)] + shapes + shapes,
        in_specs=[SMEM, VMEM, ANY, ANY, ANY],
        out_specs=[SMEM, VMEM] + [ANY] * (2 * count),
        scratch_shapes=[
            pltpu.VMEM((3, TILES + FAR, TILE, features), bf16),
            pltpu.VMEM((2, 3, packed_tiles, TILE, HD), bf16),
            pltpu.SemaphoreType.DMA((4, 3)),
            pltpu.SemaphoreType.DMA((2, count + 1)),
        ],
        name="pack",
    )(lengths, positions, tiled(q), tiled(k), tiled(v))
    scal, place = outs[:2]
    to_right, to_left = outs[2 : 2 + count], outs[2 + count :]
    from_left = []
    from_right = []
    for c in range(count):
        from_left.append(moved(to_right[c], 1, ring))
        from_right.append(moved(to_left[c], -1, ring))

    video_ends = jnp.cumsum(lengths)
    first_row = lax.axis_index("req") * ROWS
    rows_here = first_row + jnp.arange(ROWS, dtype=jnp.int32)
    videos = jnp.sum((video_ends[:, None] <= rows_here[None, :]).astype(jnp.int32), axis=0)
    chosen = videos[None, :] == jnp.arange(step_sizes.shape[0], dtype=jnp.int32)[:, None]
    steps = jnp.sum(jnp.where(chosen, step_sizes[:, None], 0.0), axis=0)

    select = jnp.asarray(selector())
    turn = jnp.asarray(turner())
    w_turned = w_head.T
    pair_ops = ROWS * ROWS * HD * 4
    turned, local_acc = pl.pallas_call(
        local_kernel,
        grid=(heads,),
        out_shape=[sized((heads, 3, ROWS, HD), bf16), sized((ROWS, HD), f32)],
        in_specs=[
            SMEM,
            VMEM,
            VMEM,
            VMEM,
            pl.BlockSpec((1, ROWS), lambda h: (0, 0)),
            pl.BlockSpec((ROWS, 1), lambda h: (0, 0)),
            pl.BlockSpec((ROWS, HD), lambda h: (0, h)),
            pl.BlockSpec((ROWS, HD), lambda h: (0, h)),
            pl.BlockSpec((ROWS, HD), lambda h: (0, h)),
            pl.BlockSpec((LATC, HD), lambda h: (0, h)),
            pl.BlockSpec((2, HD), lambda h: (0, h)),
        ],
        out_specs=[
            pl.BlockSpec((1, 3, ROWS, HD), lambda h: (h, 0, 0, 0)),
            pl.BlockSpec((ROWS, HD), lambda h: (0, 0)),
        ],
        scratch_shapes=[
            pltpu.VMEM((ROWS, HD), f32),
            pltpu.VMEM((ROWS, HD), f32),
            pltpu.VMEM((ROWS, ROWS), f32),
        ],
        cost_estimate=pl.CostEstimate(
            flops=heads * pair_ops, bytes_accessed=6 * ROWS * features * 2, transcendentals=0
        ),
        name="local",
    )(
        scal, place, select, turn, videos[None, :], videos[:, None], q, k, v, w_turned, modulation
    )

    acc = table = None
    for c in range(count):
        final = c == count - 1
        here = [i for i in (c - 1, c) if i >= 0]
        operands = [scal, select, turn, w_turned, modulation, turned]
        specs = [SMEM, VMEM, VMEM, VMEM, VMEM, ANY]
        operands += [from_left[i] for i in here] + [from_right[i] for i in here]
        specs += [ANY] * (2 * len(here))
        if c > 0:
            operands += [table, acc]
            specs += [VMEM, VMEM]
        acc_shape = sized((2, SPAN, HD), f32)
        if final:
            operands.append(local_acc)
            specs.append(VMEM)
            out_shape = [
                sized((ACCR, ROWS), f32),
                sized((ACCR, REACH), f32),
                sized((ACCR, REACH), f32),
                sized((LATC, HD), f32),
            ]
        elif c == 0:
            out_shape = [acc_shape, sized((2, 2, REACH, HD), f32)]
        else:
            out_shape = [acc_shape]
        scratch = [
            pltpu.VMEM((3, SPAN, HD), bf16),
            pltpu.VMEM((2, 3, ROWS, HD), bf16),
            pltpu.VMEM((2, 3, 2 * FAR + sum(chunks[i] for i in here), TILE, HD), bf16),
            pltpu.SemaphoreType.DMA((2,)),
            pltpu.SemaphoreType.DMA((2, 3)),
        ]
        if final:
            scratch.append(pltpu.VMEM((2, SPAN, HD), f32))
        results = pl.pallas_call(
            functools.partial(cut_kernel, heads, chunks, c),
            out_shape=out_shape,
            in_specs=specs,
            out_specs=[VMEM] * len(out_shape),
            scratch_shapes=scratch,
            cost_estimate=pl.CostEstimate(
                flops=heads * pair_ops // count, bytes_accessed=4 << 20, transcendentals=0
            ),
        )(*operands)
        if final:
            own, back_left, back_right, shift = results
        elif c == 0:
            acc, table = results
        else:
            (acc,) = results

    guided = pl.pallas_call(
        functools.partial(finish_kernel, features, ring),
        out_shape=sized((LATC // 2, ROWS), f32),
        in_specs=[VMEM, VMEM, VMEM, VMEM, SMEM],
        out_specs=VMEM,
        scratch_shapes=[
            pltpu.VMEM((ACCR, REACH), f32),
            pltpu.VMEM((ACCR, REACH), f32),
            pltpu.VMEM((LATC, ROWS), f32),
            pltpu.VMEM((LATC // 2, ROWS), f32),
            pltpu.SemaphoreType.DMA((3,)),
            pltpu.SemaphoreType.DMA((3,)),
        ],
        compiler_params=pltpu.CompilerParams(collective_id=0, has_side_effects=True),
        name="finish",
    )(own, back_left, back_right, shift, guide_scale)
    return (latents.T + steps[None, :] * guided).T


def solution(mesh):
    in_specs = (
        P("cfg", "req", None),
        P("cfg", "req", None),
        P("cfg", "req", None),
        P(None, "req"),
        P("req", "cfg"),
        P(),
        P(),
        P(),
        P(),
        P(),
    )
    return jax.shard_map(
        per_device, mesh=mesh, in_specs=in_specs, out_specs=P("req", "cfg"), check_vma=False
    )
```

time: 428 us -> 173 us (0.40)
  the two profiles are of different devices: /device:TPU:25 before, /device:TPU:17 now
where the time goes in v1:
time: 173 us; the launch traced here: 171 us
  Pallas kernels  118 us (68%)
  waiting for transfers between devices  31.2 us (18%)
  starting transfers between devices  15.9 us (9%)
  local copies, waits for them, and re-layouts  3.54 us (2%)
  other arithmetic  2.17 us (1%)
    pallas_call x1, Pallas kernels, per_device(): pl.pallas_call(local_kernel, grid=(heads,), out_shape=[sized((heads, 3, R...  41.9 us
    pallas_call x1, Pallas kernels, per_device(): pl.pallas_call(functools.partial(finish_kernel, features, ring), out_shap...  35 us
    pallas_call x4, Pallas kernels, per_device(): pl.pallas_call(functools.partial(cut_kernel, heads, chunks, c), out_shape...  32.6 us
    ppermute x8, waiting for transfers between devices, moved(): lax.ppermute(value, 'req', [(i, (i + step) % ring) for i in range(ring)])  31.2 us
    ppermute x8, starting transfers between devices, moved(): lax.ppermute(value, 'req', [(i, (i + step) % ring) for i in range(ring)])  15.9 us
    pallas_call x1, Pallas kernels, per_device(): pl.pallas_call(functools.partial(pack_kernel, heads, chunks), out_shape=[...  8.42 us
  transfers between devices with their start and end apart: 8, of which 2 were waited for; matrix products, arithmetic and copies ran while one was open for 1% of the time, Pallas kernels for 41%

profile of v1, /device:TPU:17, one launch (start us, length us, event | category | flops | bytes accessed | tf_op | source)
XLA Modules:
  0.0 171.4 jit_solution(9494763491696976336)
XLA Ops:
  0.0 8.4 %pack.1 = (s32[8]{0:T(128)}, bf16[16,128]{1,0:T(8,128)(2,1)}, bf16[3,49,16,128]{3,2,1,0:T(8,128)(2,1)}, bf16[3,48,16,128]{3,2,1,0:T(8,128)(2,1)}, bf16[3,42,16,1...) custom-call(s32[256]{0:T(256)} %lens_ref.1, ...), custom_call_target="tpu_custom_call" | custom-call | tf_op jit(solution)/shard_map/pack/pallas_call | solution.py:513
  8.4 0.1 collective-permute-start.6
  8.6 2.4 %collective-permute-start = (bf16[3,42,16,128]{3,2,1,0:T(8,128)(2,1)}, bf16[3,42,16,128]{3,2,1,0:T(8,128)(2,1)S(1)}, u32[]{:S(2)}, u32[]{:S(2)}) collective-permute-start(bf16[3,42,16,128]{3,2,1,0:T(8,128)(2,1)} %get-tuple-element.26), channel_id=1, source_target_pairs={{0,1},{1,2},{2,3},{3,4},{4,5},{5,6},{6,7},{7,8},{8,9},{9,10},{10,1... | collective-permute-start | bytes 1548296 | tf_op jit(solution)/shard_map/ppermute | solution.py:492
  11.0 0.2 collective-permute-start.4
  11.2 5.5 %collective-permute-start.5 = (bf16[3,49,16,128]{3,2,1,0:T(8,128)(2,1)}, bf16[3,49,16,128]{3,2,1,0:T(8,128)(2,1)S(1)}, u32[]{:S(2)}, u32[]{:S(2)}) collective-permute-start(bf16[3,49,16,128]{3,2,1,0:T(8,128)(2,1)} %get-tuple-element.31), channel_id=1, source_target_pairs={{0,127},{1,0},{2,1},{3,2},{4,3},{5,4},{6,5},{7,6},{8,7},{9,8},{10,... | collective-permute-start | bytes 1806344 | tf_op jit(solution)/shard_map/ppermute | solution.py:492
  16.7 0.3 collective-permute-start.7
  17.0 0.3 reduce-window.9
  17.6 10.7 %collective-permute-done.6.refs_7_.refs_6_ = bf16[3,48,16,128]{3,2,1,0:T(8,128)(2,1)S(1)} collective-permute-done((bf16[3,48,16,128]{3,2,1,0:T(8,128)(2,1)}, bf16[3,48,16,128]{3,2,1,0:T(8,128)(2,1)S(1)}, u32[]{:S(2)}, u32[]{:S(2)}) %collective-permute-start.6) | collective-permute-done | bytes 589856 | tf_op jit(solution)/shard_map/ppermute | solution.py:492
  28.3 1.6 collective-permute-start.2
  29.9 0.1 convert_reduce_fusion
  30.0 0.9 copy.14.seg_col_ref
  31.6 0.1 select_reduce_fusion
  31.7 20.5 %collective-permute-done.4.refs_6_ = bf16[3,49,16,128]{3,2,1,0:T(8,128)(2,1)S(1)} collective-permute-done((bf16[3,49,16,128]{3,2,1,0:T(8,128)(2,1)}, bf16[3,49,16,128]{3,2,1,0:T(8,128)(2,1)S(1)}, u32[]{:S(2)}, u32[]{:S(2)}) %collective-permute-start.4) | collective-permute-done | bytes 602144 | tf_op jit(solution)/shard_map/ppermute | solution.py:492
  52.3 5.7 %collective-permute-start.3 = (bf16[3,32,16,128]{3,2,1,0:T(8,128)(2,1)}, bf16[3,32,16,128]{3,2,1,0:T(8,128)(2,1)}, u32[]{:S(2)}, u32[]{:S(2)}) collective-permute-start(bf16[3,32,16,128]{3,2,1,0:T(8,128)(2,1)} %get-tuple-element.29), channel_id=1, source_target_pairs={{0,127},{1,0},{2,1},{3,2},{4,3},{5,4},{6,5},{7,6},{8,7},{9,8},{10,... | collective-permute-start | bytes 1179656 | tf_op jit(solution)/shard_map/ppermute | solution.py:492
  57.9 41.9 %local.1 = (bf16[20,3,512,128]{3,2,1,0:T(8,128)(2,1)}, f32[512,128]{1,0:T(8,128)}) custom-call(s32[8]{0:T(128)} %get-tuple-element.23.scal_ref.refs_0_, bf16[16,128]{1,0:T(8,128)(2,1)} %get-tuple-element.24.place_ref, bf16[3,4,16,128]{3,2,1,0:T(8,128)(2,1)} %constant.17.clone.select_ref.refs_1_, bf16[128,128]{1,0:T(8,128)(2,1)} %constant.18.clone.turn_ref.refs_2_, ...), custom_call_target="tpu_custom_call" | custom-call | flops 2684354560 | bytes 15728640 | tf_op jit(solution)/shard_map/local/pallas_call | solution.py:545
  99.8 16.1 %shard_map.118 = (f32[2,1152,128]{2,1,0:T(8,128)}, f32[2,2,384,128]{3,2,1,0:T(8,128)}) custom-call(s32[8]{0:T(128)} %get-tuple-element.23.scal_ref.refs_0_, bf16[3,4,16,128]{3,2,1,0:T(8,128)(2,1)} %constant.17.clone.select_ref.refs_1_, bf16[128,128]{1,0:T(8,128)(2,1)} %constant.18.clone.turn_ref.refs_2_, bf16[64,2560]{1,0:T(8,128)(2,1)} %bitcast.19, ...), custom_call_target="tpu_custom_call" | custom-call | flops 671088640 | bytes 4194304 | tf_op jit(solution)/shard_map/pallas_call | solution.py:613
  115.9 0.9 copy-done.3
  116.8 7.9 %shard_map.119.refs_11_ = f32[2,1152,128]{2,1,0:T(8,128)} custom-call(s32[8]{0:T(128)} %get-tuple-element.23.scal_ref.refs_0_, bf16[3,4,16,128]{3,2,1,0:T(8,128)(2,1)} %constant.17.clone.select_ref.refs_1_, bf16[128,128]{1,0:T(8,128)(2,1)} %constant.18.clone.turn_ref.refs_2_, bf16[64,2560]{1,0:T(8,128)(2,1)} %bitcast.20, f32[2,2560]{1,0:T(2,128)} %refs_4_.7, ...), custom_call_target="tpu_custom_call" | custom-call | flops 671088640 | bytes 4194304 | tf_op jit(solution)/shard_map/pallas_call | solution.py:613
  124.8 0.8 copy-done.4
  125.5 0.8 copy-done.5
  126.3 4.4 %shard_map.120.refs_11_ = f32[2,1152,128]{2,1,0:T(8,128)} custom-call(s32[8]{0:T(128)} %get-tuple-element.23.scal_ref.refs_0_, bf16[3,4,16,128]{3,2,1,0:T(8,128)(2,1)} %constant.17.clone.select_ref.refs_1_, bf16[128,128]{1,0:T(8,128)(2,1)} %constant.18.clone.turn_ref.refs_2_, bf16[64,2560]{1,0:T(8,128)(2,1)} %bitcast.21, f32[2,2560]{1,0:T(2,128)} %refs_4_.7, ...), custom_call_target="tpu_custom_call" | custom-call | flops 671088640 | bytes 4194304 | tf_op jit(solution)/shard_map/pallas_call | solution.py:613
  130.8 4.2 %shard_map.121 = (f32[72,512]{1,0:T(8,128)}, f32[72,384]{1,0:T(8,128)}, f32[72,384]{1,0:T(8,128)}, f32[64,128]{1,0:T(8,128)}) custom-call(s32[8]{0:T(128)} %get-tuple-element.23.scal_ref.refs_0_, bf16[3,4,16,128]{3,2,1,0:T(8,128)(2,1)} %constant.17.clone.select_ref.refs_1_, bf16[128,128]{1,0:T(8,128)(2,1)} %constant.18.clone.turn_ref.refs_2_, ...), custom_call_target="tpu_custom_call" | custom-call | flops 671088640 | bytes 4194304 | tf_op jit(solution)/shard_map/pallas_call | solution.py:613
  135.0 35.0 %finish.1 = f32[32,512]{1,0:T(8,128)} custom-call(f32[72,512]{1,0:T(8,128)} %get-tuple-element.37.own_ref, f32[72,384]{1,0:T(8,128)} %get-tuple-element.38.left_ref, f32[72,384]{1,0:T(8,128)} %get-tuple-element.39.right_ref, f32[64,128]{1,0:T(8,128)} %get-tuple-element.40.shift_ref, f32[1]{0:T(128)S(6)} %copy.15.guide_ref), custom_call_target="tpu_custom_call" | custom-call | tf_op jit(solution)/shard_map/finish/pallas_call | solution.py:630
  169.9 1.5 fusion
  (29 shorter events, 0.4 us)
Async XLA Ops:
  0.0 17.0 %copy-start.8 = (s32[256]{0:T(256)S(1)}, s32[256]{0:T(256)}, u32[]{:S(2)}) copy-start(s32[256]{0:T(256)} %lens_ref.1) | copy-start | bytes 3076
  0.0 31.6 %copy-start.9 = (f32[256]{0:T(256)S(1)}, f32[256]{0:T(256)}, u32[]{:S(2)}) copy-start(f32[256]{0:T(256)} %param.20) | copy-start | bytes 3076
  8.4 19.8 %collective-permute-start.6 = (bf16[3,48,16,128]{3,2,1,0:T(8,128)(2,1)}, bf16[3,48,16,128]{3,2,1,0:T(8,128)(2,1)S(1)}, u32[]{:S(2)}, u32[]{:S(2)}) collective-permute-start(bf16[3,48,16,128]{3,2,1,0:T(8,128)(2,1)} %get-tuple-element.33), channel_id=1, source_target_pairs={{0,1},{1,2},{2,3},{3,4},{4,5},{5,6},{6,7},{7,8},{8,9},{9,10},{10,1... | collective-permute-start | bytes 1769480 | tf_op jit(solution)/shard_map/ppermute | solution.py:492
  8.6 116.1 %collective-permute-start = (bf16[3,42,16,128]{3,2,1,0:T(8,128)(2,1)}, bf16[3,42,16,128]{3,2,1,0:T(8,128)(2,1)S(1)}, u32[]{:S(2)}, u32[]{:S(2)}) collective-permute-start(bf16[3,42,16,128]{3,2,1,0:T(8,128)(2,1)} %get-tuple-element.26), channel_id=1, source_target_pairs={{0,1},{1,2},{2,3},{3,4},{4,5},{5,6},{6,7},{7,8},{8,9},{9,10},{10,1... | collective-permute-start | bytes 1548296 | tf_op jit(solution)/shard_map/ppermute | solution.py:492
  11.0 41.2 %collective-permute-start.4 = (bf16[3,49,16,128]{3,2,1,0:T(8,128)(2,1)}, bf16[3,49,16,128]{3,2,1,0:T(8,128)(2,1)S(1)}, u32[]{:S(2)}, u32[]{:S(2)}) collective-permute-start(bf16[3,49,16,128]{3,2,1,0:T(8,128)(2,1)} %get-tuple-element.30), channel_id=1, source_target_pairs={{0,1},{1,2},{2,3},{3,4},{4,5},{5,6},{6,7},{7,8},{8,9},{9,10},{10,1... | collective-permute-start | bytes 1806344 | tf_op jit(solution)/shard_map/ppermute | solution.py:492
  11.2 41.1 %collective-permute-start.5 = (bf16[3,49,16,128]{3,2,1,0:T(8,128)(2,1)}, bf16[3,49,16,128]{3,2,1,0:T(8,128)(2,1)S(1)}, u32[]{:S(2)}, u32[]{:S(2)}) collective-permute-start(bf16[3,49,16,128]{3,2,1,0:T(8,128)(2,1)} %get-tuple-element.31), channel_id=1, source_target_pairs={{0,127},{1,0},{2,1},{3,2},{4,3},{5,4},{6,5},{7,6},{8,7},{9,8},{10,... | collective-permute-start | bytes 1806344 | tf_op jit(solution)/shard_map/ppermute | solution.py:492
  16.7 99.2 %collective-permute-start.7 = (bf16[3,48,16,128]{3,2,1,0:T(8,128)(2,1)}, bf16[3,48,16,128]{3,2,1,0:T(8,128)(2,1)S(1)}, u32[]{:S(2)}, u32[]{:S(2)}) collective-permute-start(bf16[3,48,16,128]{3,2,1,0:T(8,128)(2,1)} %get-tuple-element.34), channel_id=1, source_target_pairs={{0,127},{1,0},{2,1},{3,2},{4,3},{5,4},{6,5},{7,6},{8,7},{9,8},{10,... | collective-permute-start | bytes 1769480 | tf_op jit(solution)/shard_map/ppermute | solution.py:492
  28.3 71.5 %copy-start.2 = (bf16[3,48,16,128]{3,2,1,0:T(8,128)(2,1)}, bf16[3,48,16,128]{3,2,1,0:T(8,128)(2,1)S(1)}, u32[]{:S(2)}) copy-start(bf16[3,48,16,128]{3,2,1,0:T(8,128)(2,1)S(1)} %collective-permute-done.6.refs_7_.refs_6_) | copy-start | bytes 1769476
  28.3 96.5 %collective-permute-start.2 = (bf16[3,42,16,128]{3,2,1,0:T(8,128)(2,1)}, bf16[3,42,16,128]{3,2,1,0:T(8,128)(2,1)S(1)}, u32[]{:S(2)}, u32[]{:S(2)}) collective-permute-start(bf16[3,42,16,128]{3,2,1,0:T(8,128)(2,1)} %get-tuple-element.28), channel_id=1, source_target_pairs={{0,127},{1,0},{2,1},{3,2},{4,3},{5,4},{6,5},{7,6},{8,7},{9,8},{10,... | collective-permute-start | bytes 1548296 | tf_op jit(solution)/shard_map/ppermute | solution.py:492
  30.0 27.9 %copy-start.7 = (s32[512]{0:T(512)}, s32[512]{0:T(512)S(1)}, u32[]{:S(2)}) copy-start(s32[512]{0:T(512)S(1)} %convert_reduce_fusion) | copy-start | bytes 6148
  52.2 47.6 %copy-start = (bf16[3,49,16,128]{3,2,1,0:T(8,128)(2,1)}, bf16[3,49,16,128]{3,2,1,0:T(8,128)(2,1)S(1)}, u32[]{:S(2)}) copy-start(bf16[3,49,16,128]{3,2,1,0:T(8,128)(2,1)S(1)} %collective-permute-done.4.refs_6_) | copy-start | bytes 1806340
  52.2 78.5 %collective-permute-start.1 = (bf16[3,32,16,128]{3,2,1,0:T(8,128)(2,1)}, bf16[3,32,16,128]{3,2,1,0:T(8,128)(2,1)}, u32[]{:S(2)}, u32[]{:S(2)}) collective-permute-start(bf16[3,32,16,128]{3,2,1,0:T(8,128)(2,1)} %get-tuple-element.27), channel_id=1, source_target_pairs={{0,1},{1,2},{2,3},{3,4},{4,5},{5,6},{6,7},{7,8},{8,9},{9,10},{10,1... | collective-permute-start | bytes 1179656 | tf_op jit(solution)/shard_map/ppermute | solution.py:492
  52.3 47.6 %copy-start.1 = (bf16[3,49,16,128]{3,2,1,0:T(8,128)(2,1)}, bf16[3,49,16,128]{3,2,1,0:T(8,128)(2,1)S(1)}, u32[]{:S(2)}) copy-start(bf16[3,49,16,128]{3,2,1,0:T(8,128)(2,1)S(1)} %collective-permute-done.5.refs_7_.refs_8_) | copy-start | bytes 1806340
  52.3 78.5 %collective-permute-start.3 = (bf16[3,32,16,128]{3,2,1,0:T(8,128)(2,1)}, bf16[3,32,16,128]{3,2,1,0:T(8,128)(2,1)}, u32[]{:S(2)}, u32[]{:S(2)}) collective-permute-start(bf16[3,32,16,128]{3,2,1,0:T(8,128)(2,1)} %get-tuple-element.29), channel_id=1, source_target_pairs={{0,127},{1,0},{2,1},{3,2},{4,3},{5,4},{6,5},{7,6},{8,7},{9,8},{10,... | collective-permute-start | bytes 1179656 | tf_op jit(solution)/shard_map/ppermute | solution.py:492
  115.9 0.9 copy-start.3
  124.7 0.8 copy-start.4
  125.5 0.8 copy-start.5
  130.8 39.2 %copy-start.6 = (f32[512,32]{0,1:T(8,128)S(1)}, f32[512,32]{0,1:T(8,128)}, u32[]{:S(2)}) copy-start(f32[512,32]{0,1:T(8,128)} %param.16) | copy-start | bytes 196612

commit v2 on v1

v2 whole, which is shorter than its diff:
```python
import functools
import math

import jax
import jax.numpy as jnp
import numpy as np
from jax import lax
from jax.experimental import pallas as pl
from jax.experimental.pallas import tpu as pltpu
from jax.sharding import PartitionSpec as P

HD = 128
ROWS = 512
LATC = 64
TILE = 16
TILES = ROWS // TILE
FAR = 24
REACH = FAR * TILE
SPAN = 2 * ROWS + 128
ACCR = 72
masked_score = -1e30
score_scale = math.log2(math.e) / math.sqrt(HD)
rope_theta = 10000.0
MESH = pl.DeviceIdType.MESH
SMEM = pl.BlockSpec(memory_space=pltpu.SMEM)
VMEM = pl.BlockSpec(memory_space=pltpu.VMEM)
ANY = pl.BlockSpec(memory_space=pl.ANY)


def share_static(ta, tb, heads):
    if ta > FAR:
        return 0
    if tb > FAR:
        return heads
    costs = [max(n * ta, (heads - n) * tb) for n in range(heads + 1)]
    return costs.index(min(costs))


def capacity(heads):
    most = 0
    for ta in range(1, TILES + 1):
        for tb in range(1, TILES + 2 - ta):
            n = share_static(ta, tb, heads)
            most = max(most, n * ta, (heads - n) * tb)
    return most


def chunking(heads):
    cap = capacity(heads)
    count = max(1, cap // 34)
    return cdiv(cap, count), count


def share(ta, tb, heads):
    best = heads * tb
    chosen = jnp.int32(0)
    for n in range(1, heads + 1):
        cost = jnp.maximum(n * ta, (heads - n) * tb)
        better = cost < best
        best = jnp.where(better, cost, best)
        chosen = jnp.where(better, n, chosen)
    chosen = jnp.where(tb > FAR, heads, chosen)
    return jnp.where(ta > FAR, 0, chosen)


def selector():
    pair_total = HD // 2
    side = HD // 6
    time = pair_total - 2 * side
    axis = np.array([0] * time + [1] * side + [2] * side)
    local = np.array(list(range(time)) + list(range(side)) * 2, np.float32)
    pairs = np.array([time] * time + [side] * (2 * side), np.float32)
    frequency = np.exp(-(local / pairs) * np.float32(math.log(rope_theta))).astype(np.float32)
    table = np.zeros((4, TILE, HD), np.float32)
    for group in range(4):
        for lane in range(HD):
            table[group, axis[lane // 2] * 4 + group, lane] = frequency[lane // 2]
    parts = []
    rest = table
    for _ in range(3):
        part = rest.astype(jnp.bfloat16)
        parts.append(part)
        rest = rest - part.astype(np.float32)
    return np.stack(parts)


def turner():
    table = np.zeros((2 * HD, 2 * HD), np.float32)
    for pair in range(HD):
        table[2 * pair + 1, 2 * pair] = -1.0
        table[2 * pair, 2 * pair + 1] = 1.0
    return table.astype(jnp.bfloat16)


def cdiv(value, unit):
    return (value + unit - 1) // unit


def tables(place, select_ref, groups):
    parts = []
    for group in groups:
        angle = None
        for part in range(3):
            term = lax.dot_general(
                place,
                select_ref[part, group],
                (((0,), (0,)), ((), ())),
                preferred_element_type=jnp.float32,
            )
            angle = term if angle is None else angle + term
        parts.append(angle)
    angle = jnp.concatenate(parts, axis=0)
    return jnp.cos(angle), jnp.sin(angle)


def rotate(q, k, cosine, sine, turn):
    both = jnp.concatenate([q, k], axis=1)
    swapped = jnp.dot(both, turn, preferred_element_type=jnp.float32)
    return (
        q.astype(jnp.float32) * cosine + swapped[:, :HD] * sine,
        k.astype(jnp.float32) * cosine + swapped[:, HD:] * sine,
    )


def attend(q, k, v, bias):
    scores = lax.dot_general(q, k, (((1,), (1,)), ((), ())), preferred_element_type=jnp.float32)
    scores = scores + bias
    top = jnp.max(scores, axis=1, keepdims=True)
    weight = jnp.exp2((scores - top) * score_scale).astype(jnp.bfloat16)
    widened = jnp.concatenate([v, jnp.ones(v.shape, jnp.bfloat16)], axis=1)
    summed = jnp.dot(weight, widened, preferred_element_type=jnp.float32)
    return (summed[:, :HD] * (1.0 / summed[:, HD:])).astype(jnp.bfloat16)


def head_weights(w_block, scale_row):
    scaled = (w_block.astype(jnp.float32) * (1.0 + scale_row)).astype(jnp.bfloat16)
    return jnp.concatenate([scaled, jnp.zeros_like(scaled)], axis=0)


def project(attended, weights):
    return lax.dot_general(
        attended, weights, (((1,), (1,)), ((), ())), preferred_element_type=jnp.float32
    )


def squares(attended):
    wide = attended.astype(jnp.float32)
    return wide * wide


def with_squares(acc, squared):
    lane = lax.broadcasted_iota(jnp.int32, acc.shape, 1)
    return jnp.where(lane == LATC, jnp.sum(squared, axis=1, keepdims=True), acc)


def pack_kernel(
    heads, unit, count, lens_ref, pos_ref, q_ref, k_ref, v_ref, scal_ref, place, out_ref,
    rows_in, packed, in_sem, out_sem,
):
    me = lax.axis_index("req")
    groups = 4 if heads % 4 == 0 else 1
    width = heads // groups * HD
    loads = []
    for group in range(groups):
        columns = pl.ds(group * width, width)
        for j, source in enumerate((q_ref, k_ref, v_ref)):
            copy = pltpu.make_async_copy(
                source.at[:, :, columns], rows_in.at[j, :, :, columns], in_sem.at[group, j]
            )
            copy.start()
            loads.append(copy)
    low = me * ROWS
    high = low + ROWS

    def scan(i, carry):
        end, start_low, end_low, start_high, end_high = carry
        start = end
        end = start + lens_ref[i]
        before_low = start < low
        before_high = start < high
        return (
            end,
            jnp.where(before_low, start, start_low),
            jnp.where(before_low, end, end_low),
            jnp.where(before_high, start, start_high),
            jnp.where(before_high, end, end_high),
        )

    zero = jnp.int32(0)
    _, start_low, end_low, start_high, end_high = lax.fori_loop(
        0, lens_ref.shape[0], scan, (zero, low, low, high, high), unroll=8
    )
    cut_low = end_low > low
    cut_high = end_high > high
    a_low = jnp.where(cut_low, low - start_low, 0)
    b_low = jnp.where(cut_low, end_low - low, 0)
    a_high = jnp.where(cut_high, high - start_high, 0)
    b_high = jnp.where(cut_high, end_high - high, 0)
    n_low = share(cdiv(a_low, TILE), cdiv(b_low, TILE), heads)
    n_high = share(cdiv(a_high, TILE), cdiv(b_high, TILE), heads)
    for i, value in enumerate((a_low, b_low, n_low, a_high, b_high, n_high, zero, zero)):
        scal_ref[i] = value

    placed = pos_ref[...].astype(jnp.float32)
    pieces = [placed[a : a + 1, g * HD : (g + 1) * HD] for a in range(3) for g in range(4)]
    pieces.append(jnp.zeros((TILE - 12, HD), jnp.float32))
    place[...] = jnp.concatenate(pieces, axis=0).astype(jnp.bfloat16)
    for copy in loads:
        copy.wait()
    ta, tb = cdiv(a_high, TILE), cdiv(b_low, TILE)

    def pack(t, carry):
        head_r, tile_r, head_l, tile_l = carry
        columns = pl.ds(pl.multiple_of(head_r * HD, HD), HD)
        source = jnp.minimum(TILES - ta + tile_r, TILES - 1)
        for j in range(3):
            packed[0, j, t] = rows_in[j, source, :, columns]
        columns = pl.ds(pl.multiple_of(head_l * HD, HD), HD)
        for j in range(3):
            packed[1, j, t] = rows_in[j, tile_l, :, columns]
        over_r = tile_r + 1 >= ta
        over_l = tile_l + 1 >= tb
        return (
            jnp.minimum(jnp.where(over_r, head_r + 1, head_r), heads - 1),
            jnp.where(over_r, 0, tile_r + 1),
            jnp.minimum(jnp.where(over_l, head_l + 1, head_l), heads - 1),
            jnp.where(over_l, 0, tile_l + 1),
        )

    carry = (zero, zero, jnp.minimum(n_low, heads - 1), zero)
    stores = []
    for c in range(count):
        carry = lax.fori_loop(c * unit, (c + 1) * unit, pack, carry, unroll=2)
        chunk = pl.ds(c * unit, unit)
        copy = pltpu.make_async_copy(packed.at[:, :, chunk], out_ref.at[:, :, chunk], out_sem.at[c])
        copy.start()
        stores.append(copy)
    for copy in stores:
        copy.wait()


def main_kernel(
    heads, ring, unit, count, lens_ref, step_ref, place, packed, select_ref, turn_ref, w_ref,
    mod_ref, q_ref, k_ref, v_ref, steps_ref, table_ref, acc_ref, turned_ref, recv_ref,
    rows_in, places, cos_ref, sin_ref, bias_ref, square_ref, mine,
    in_sem, send_sem, recv_sem, place_send, place_recv, out_sem,
):
    me = lax.axis_index("req")
    left, right = lax.rem(me + ring - 1, ring), lax.rem(me + 1, ring)
    barrier = pltpu.get_barrier_semaphore()
    for target in (left, right):
        pl.semaphore_signal(barrier, inc=1, device_id={"req": target}, device_id_type=MESH)
    pl.semaphore_wait(barrier, 2)
    sends = []
    for direction, target in ((0, right), (1, left)):
        copy = pltpu.make_async_remote_copy(
            place, places.at[direction], place_send.at[direction],
            place_recv.at[direction], device_id={"req": target}, device_id_type=MESH,
        )
        copy.start()
        sends.append(copy)
    for c in range(count):
        chunk = pl.ds(c * unit, unit)
        for direction, target in ((0, right), (1, left)):
            copy = pltpu.make_async_remote_copy(
                packed.at[direction, :, chunk], recv_ref.at[direction, :, chunk],
                send_sem.at[direction, c], recv_sem.at[direction, c],
                device_id={"req": target}, device_id_type=MESH,
            )
            copy.start()
            sends.append(copy)
    groups = 4 if heads % 4 == 0 else 1
    width = heads // groups * HD
    loads = []
    for group in range(groups):
        columns = pl.ds(group * width, width)
        for j, source in enumerate((q_ref, k_ref, v_ref)):
            copy = pltpu.make_async_copy(
                source.at[:, :, columns], rows_in.at[j, :, :, columns], in_sem.at[group, j]
            )
            copy.start()
            loads.append(copy)
    low = me * ROWS
    zero = jnp.int32(0)
    lane = lax.broadcasted_iota(jnp.int32, (1, ROWS), 1) + low

    def label(i, carry):
        end, video, step = carry
        end = end + lens_ref[i]
        past = lane >= end
        video = video + past.astype(jnp.int32)
        following = step_ref[jnp.minimum(i + 1, lens_ref.shape[0] - 1)]
        return end, video, jnp.where(past, following, step)

    start = jnp.full((1, ROWS), step_ref[0], jnp.float32)
    _, video, step = lax.fori_loop(
        0, lens_ref.shape[0], label, (zero, jnp.zeros((1, ROWS), jnp.int32), start), unroll=8
    )
    steps_ref[...] = step
    tall = jnp.broadcast_to(video.astype(jnp.float32), (HD, ROWS)).T
    for part in range(ROWS // HD):
        wide = jnp.broadcast_to(
            video[:, part * HD : (part + 1) * HD].astype(jnp.float32), (ROWS, HD)
        )
        bias_ref[:, part * HD : (part + 1) * HD] = jnp.where(tall == wide, 0.0, masked_score)
    cosine, sine = tables(place[...], select_ref, range(4))
    cos_ref[...] = cosine
    sin_ref[...] = sine
    acc_ref[...] = jnp.zeros_like(acc_ref)
    square_ref[...] = jnp.zeros_like(square_ref)
    turn = turn_ref[...]
    for copy in loads:
        copy.wait()

    def keep(head, slot):
        return pltpu.make_async_copy(mine.at[slot], turned_ref.at[head], out_sem.at[slot])

    def one(head, slot):
        columns = pl.ds(pl.multiple_of(head * HD, HD), HD)
        q = rows_in[0, :, :, columns].reshape(ROWS, HD)
        k = rows_in[1, :, :, columns].reshape(ROWS, HD)
        q, k = rotate(q, k, cos_ref[...], sin_ref[...], turn)
        mine[slot, 0] = q.astype(jnp.bfloat16)
        mine[slot, 1] = k.astype(jnp.bfloat16)
        mine[slot, 2] = rows_in[2, :, :, columns].reshape(ROWS, HD)
        keep(head, slot).start()
        attended = attend(mine[slot, 0], mine[slot, 1], mine[slot, 2], bias_ref[...])
        square_ref[...] += squares(attended)
        return attended, head_weights(w_ref[:, columns], mod_ref[1:2, columns])

    def couple(pair, carry):
        first, second = (one(2 * pair + slot, slot) for slot in range(2))
        attended = jnp.concatenate([first[0], second[0]], axis=1)
        acc_ref[...] += project(attended, jnp.concatenate([first[1], second[1]], axis=1))
        for slot in range(2):
            keep(2 * pair + slot, slot).wait()
        return carry

    lax.fori_loop(0, heads // 2, couple, 0)
    acc_ref[...] = with_squares(acc_ref[...], square_ref[...])
    for side in range(2):
        sends[side].wait()
        groups = range(1, 4) if side == 0 else range(3)
        cosine, sine = tables(places[side], select_ref, groups)
        table_ref[side, 0] = cosine
        table_ref[side, 1] = sine
    for copy in sends[2:]:
        copy.wait()


def cut_kernel(
    heads, unit, count, scal_ref, table_ref, local_ref, turn_ref, w_ref, mod_ref,
    turned_ref, recv_ref, own_ref, left_out, right_out, shift_ref,
    span, mine, recv, acc_ref, square_ref, loc_sem, recv_sem,
):
    loads = []
    for side in range(2):
        copy = pltpu.make_async_copy(
            recv_ref.at[side], recv.at[side, :, pl.ds(FAR, unit * count)], recv_sem.at[side]
        )
        copy.start()
        loads.append(copy)
    a_low, b_low, n_low = scal_ref[0], scal_ref[1], scal_ref[2]
    a_high, b_high, n_high = scal_ref[3], scal_ref[4], scal_ref[5]
    low_count = jnp.where(a_low > 0, n_low, 0)
    high_count = jnp.where(a_high > 0, heads - n_high, 0)
    items = low_count + high_count

    def head_of(i):
        return jnp.where(i < low_count, i, n_high + i - low_count)

    def fetch(i, buffer):
        return pltpu.make_async_copy(turned_ref.at[head_of(i)], mine.at[buffer], loc_sem.at[buffer])

    @pl.when(items > 0)
    def _():
        fetch(jnp.int32(0), 0).start()

    span[...] = jnp.zeros_like(span)
    acc_ref[...] = jnp.zeros_like(acc_ref)
    square_ref[...] = jnp.zeros_like(square_ref)
    turn = turn_ref[...]
    for copy in loads:
        copy.wait()

    def one(i, carry):
        buffer = lax.rem(i, 2)
        fetch(i, buffer).wait()

        @pl.when(i + 1 < items)
        def _():
            fetch(i + 1, 1 - buffer).start()

        side = (i >= low_count).astype(jnp.int32)
        is_low = side == 0
        slot = jnp.where(is_low, i, i - low_count)
        head = head_of(i)
        a = jnp.where(is_low, a_low, a_high)
        b = jnp.where(is_low, b_low, b_high)
        ta, tb = cdiv(a, TILE), cdiv(b, TILE)
        offset = jnp.where(is_low, slot * ta + ta, slot * tb + FAR)
        row = lax.broadcasted_iota(jnp.int32, (REACH, HD), 0)
        keep = (row >= jnp.where(is_low, REACH - ta * TILE, 0)) & (
            row < jnp.where(is_low, REACH, tb * TILE)
        )
        cosine, sine = table_ref[side, 0], table_ref[side, 1]
        target = pl.ds(pl.multiple_of(jnp.where(is_low, ROWS - REACH, ROWS), 128), REACH)
        q, k, v = (recv[side, j, pl.ds(offset, FAR)].reshape(REACH, HD) for j in range(3))
        q, k = rotate(q, k, cosine, sine, turn)
        for j, x in enumerate((q, k, v.astype(jnp.float32))):
            span[j, target] = jnp.where(keep, x, 0.0).astype(jnp.bfloat16)
        for j in range(3):
            span[j, pl.ds(pl.multiple_of(jnp.where(is_low, ROWS, 0), ROWS), ROWS)] = mine[buffer, j]
        columns = pl.ds(pl.multiple_of(head * HD, HD), HD)
        weights = head_weights(w_ref[:, columns], mod_ref[1:2, columns])
        start = pl.multiple_of(ROWS - ta * TILE, TILE)
        extent = (ta + tb) * TILE

        def run(width):
            lane = lax.broadcasted_iota(jnp.int32, (1, width), 1)
            valid = (lane >= ta * TILE - a) & (lane < ta * TILE + b)
            bias = jnp.where(valid, 0.0, masked_score)

            rows = pl.ds(start, width)
            attended = attend(span[0, rows], span[1, rows], span[2, rows], bias)
            acc_ref[side, rows] += project(attended, weights)
            square_ref[side, rows] += squares(attended)

        below = 0
        for width in (128, 256, 384, 512, 528):

            @pl.when((extent > below) & (extent <= width))
            def _(width=width):
                run(width)

            below = width
        return carry

    lax.fori_loop(0, items, one, 0)
    for side in range(2):
        acc_ref[side] = with_squares(acc_ref[side], square_ref[side])
    row = lax.broadcasted_iota(jnp.int32, (ROWS, HD), 0)
    own = jnp.where(row < b_low, acc_ref[0, ROWS : 2 * ROWS], 0.0)
    own = own + jnp.where(row >= ROWS - a_high, acc_ref[1, 0:ROWS], 0.0)
    own = own + jnp.where((row >= b_low) & (row < ROWS - a_high), local_ref[...], 0.0)
    own_ref[...] = own.T[:ACCR]
    row = lax.broadcasted_iota(jnp.int32, (REACH, HD), 0)
    back = jnp.where(row >= REACH - a_low, acc_ref[0, ROWS - REACH : ROWS], 0.0)
    left_out[...] = back.T[:ACCR]
    back = jnp.where(row < b_high, acc_ref[1, ROWS : ROWS + REACH], 0.0)
    right_out[...] = back.T[:ACCR]
    shift = jnp.sum(w_ref[...].astype(jnp.float32) * mod_ref[0:1, :], axis=1, keepdims=True)
    shift_ref[...] = jnp.broadcast_to(shift, (LATC, HD))


def finish_kernel(
    features, ring, own_ref, left_ref, right_ref, shift_ref, guide_ref, out_ref,
    from_left, from_right, velocity, other, send_sem, recv_sem,
):
    me = lax.axis_index("req")
    parity = lax.axis_index("cfg")
    left, right = lax.rem(me + ring - 1, ring), lax.rem(me + 1, ring)
    partner = {"cfg": 1 - parity}
    barrier = pltpu.get_barrier_semaphore()
    for target in ({"req": left}, {"req": right}, partner):
        pl.semaphore_signal(barrier, inc=1, device_id=target, device_id_type=MESH)
    pl.semaphore_wait(barrier, 3)
    to_left = pltpu.make_async_remote_copy(
        left_ref, from_right, send_sem.at[0], recv_sem.at[0],
        device_id={"req": left}, device_id_type=MESH,
    )
    to_left.start()
    to_right = pltpu.make_async_remote_copy(
        right_ref, from_left, send_sem.at[1], recv_sem.at[1],
        device_id={"req": right}, device_id_type=MESH,
    )
    to_right.start()
    to_left.wait()
    to_right.wait()
    none = jnp.zeros((ACCR, ROWS - REACH), jnp.float32)
    total = own_ref[...]
    total = total + jnp.concatenate([none, from_right[...]], axis=1)
    total = total + jnp.concatenate([from_left[...], none], axis=1)
    inverse = lax.rsqrt(total[LATC : LATC + 1] * (1.0 / features) + 1e-06)
    velocity[...] = total[:LATC] * inverse + shift_ref[:, 0:1]
    half = LATC // 2
    give = pltpu.make_async_remote_copy(
        velocity.at[pl.ds(pl.multiple_of((1 - parity) * half, half), half)],
        other, send_sem.at[2], recv_sem.at[2], device_id=partner, device_id_type=MESH,
    )
    give.start()
    kept = velocity[pl.ds(pl.multiple_of(parity * half, half), half)]
    give.wait()
    theirs = other[...]
    conditional = jnp.where(parity == 0, kept, theirs)
    unconditional = jnp.where(parity == 0, theirs, kept)
    out_ref[...] = unconditional + guide_ref[0] * (conditional - unconditional)


def per_device(
    query_rows, key_rows, value_rows, positions, latents, w_head, modulation, guide_scale,
    step_sizes, lengths,
):
    features = query_rows.shape[2]
    heads = features // HD
    ring = lax.axis_size("req")
    unit, count = chunking(heads)
    bf16, f32 = jnp.bfloat16, jnp.float32
    sized = jax.ShapeDtypeStruct
    tiled = [
        x.reshape(TILES, TILE, features) for x in (query_rows, key_rows, value_rows)
    ]
    turn = jnp.asarray(turner())
    w_turned = w_head.T
    scal, place, packed = pl.pallas_call(
        functools.partial(pack_kernel, heads, unit, count),
        out_shape=[
            sized((8,), jnp.int32),
            sized((TILE, HD), bf16),
            sized((2, 3, unit * count, TILE, HD), bf16),
        ],
        in_specs=[SMEM, VMEM] + [ANY] * 3,
        out_specs=[SMEM, VMEM, ANY],
        scratch_shapes=[
            pltpu.VMEM((3, TILES, TILE, features), bf16),
            pltpu.VMEM((2, 3, unit * count, TILE, HD), bf16),
            pltpu.SemaphoreType.DMA((4, 3)),
            pltpu.SemaphoreType.DMA((count,)),
        ],
        name="pack",
    )(lengths, positions, *tiled)
    steps, table, local_acc, turned, recv = pl.pallas_call(
        functools.partial(main_kernel, heads, ring, unit, count),
        out_shape=[
            sized((1, ROWS), f32),
            sized((2, 2, REACH, HD), f32),
            sized((ROWS, HD), f32),
            sized((heads, 3, ROWS, HD), bf16),
            sized((2, 3, unit * count, TILE, HD), bf16),
        ],
        in_specs=[SMEM, SMEM, VMEM, ANY] + [VMEM] * 4 + [ANY] * 3,
        out_specs=[VMEM, VMEM, VMEM, ANY, ANY],
        scratch_shapes=[
            pltpu.VMEM((3, TILES, TILE, features), bf16),
            pltpu.VMEM((2, TILE, HD), bf16),
            pltpu.VMEM((ROWS, HD), f32),
            pltpu.VMEM((ROWS, HD), f32),
            pltpu.VMEM((ROWS, ROWS), f32),
            pltpu.VMEM((ROWS, HD), f32),
            pltpu.VMEM((2, 3, ROWS, HD), bf16),
            pltpu.SemaphoreType.DMA((4, 3)),
            pltpu.SemaphoreType.DMA((2, count)),
            pltpu.SemaphoreType.DMA((2, count)),
            pltpu.SemaphoreType.DMA((2,)),
            pltpu.SemaphoreType.DMA((2,)),
            pltpu.SemaphoreType.DMA((2,)),
        ],
        compiler_params=pltpu.CompilerParams(collective_id=1, has_side_effects=True),
        name="main",
    )(
        lengths, step_sizes, place, packed, jnp.asarray(selector()), turn, w_turned, modulation,
        *tiled,
    )
    own, back_left, back_right, shift = pl.pallas_call(
        functools.partial(cut_kernel, heads, unit, count),
        out_shape=[
            sized((ACCR, ROWS), f32),
            sized((ACCR, REACH), f32),
            sized((ACCR, REACH), f32),
            sized((LATC, HD), f32),
        ],
        in_specs=[SMEM] + [VMEM] * 5 + [ANY] * 2,
        out_specs=[VMEM] * 4,
        scratch_shapes=[
            pltpu.VMEM((3, SPAN, HD), bf16),
            pltpu.VMEM((2, 3, ROWS, HD), bf16),
            pltpu.VMEM((2, 3, 2 * FAR + unit * count, TILE, HD), bf16),
            pltpu.VMEM((2, SPAN, HD), f32),
            pltpu.VMEM((2, SPAN, HD), f32),
            pltpu.SemaphoreType.DMA((2,)),
            pltpu.SemaphoreType.DMA((2,)),
        ],
        name="cut",
    )(scal, table, local_acc, turn, w_turned, modulation, turned, recv)
    guided = pl.pallas_call(
        functools.partial(finish_kernel, features, ring),
        out_shape=sized((LATC // 2, ROWS), f32),
        in_specs=[VMEM, VMEM, VMEM, VMEM, SMEM],
        out_specs=VMEM,
        scratch_shapes=[
            pltpu.VMEM((ACCR, REACH), f32),
            pltpu.VMEM((ACCR, REACH), f32),
            pltpu.VMEM((LATC, ROWS), f32),
            pltpu.VMEM((LATC // 2, ROWS), f32),
            pltpu.SemaphoreType.DMA((3,)),
            pltpu.SemaphoreType.DMA((3,)),
        ],
        compiler_params=pltpu.CompilerParams(collective_id=0, has_side_effects=True),
        name="finish",
    )(own, back_left, back_right, shift, guide_scale)
    return (latents.T + steps * guided).T


def solution(mesh):
    in_specs = (
        P("cfg", "req", None),
        P("cfg", "req", None),
        P("cfg", "req", None),
        P(None, "req"),
        P("req", "cfg"),
        P(),
        P(),
        P(),
        P(),
        P(),
    )
    return jax.shard_map(
        per_device, mesh=mesh, in_specs=in_specs, out_specs=P("req", "cfg"), check_vma=False
    )
```

time: 173 us -> 123 us (0.71)
  the two profiles are of different devices: /device:TPU:17 before, /device:TPU:217 now
where the time goes in v2:
time: 123 us; the launch traced here: 122 us
  Pallas kernels  119 us (97%)
  other arithmetic  1.48 us (1%)
    pallas_call x1, Pallas kernels, per_device(): pl.pallas_call(functools.partial(main_kernel, heads, ring, unit, count),...  51.4 us
    pallas_call x1, Pallas kernels, per_device(): pl.pallas_call(functools.partial(cut_kernel, heads, unit, count), out_sha...  49.1 us
    pallas_call x1, Pallas kernels, per_device(): pl.pallas_call(functools.partial(finish_kernel, features, ring), out_shap...  11 us
    pallas_call x1, Pallas kernels, per_device(): pl.pallas_call(functools.partial(pack_kernel, heads, unit, count), out_sh...  7.93 us

profile of v2, /device:TPU:217, one launch (start us, length us, event | category | flops | bytes accessed | tf_op | source)
XLA Modules:
  0.0 121.6 jit_solution(9628626886083552405)
XLA Ops:
  0.0 7.9 %pack.1 = (s32[8]{0:T(128)}, bf16[16,128]{1,0:T(8,128)(2,1)}, bf16[2,3,170,16,128]{4,3,2,1,0:T(8,128)(2,1)}) custom-call(s32[256]{0:T(256)} %lens_ref.3, s32[3,512]{1,0:T(4,128)} %pos_ref.1, bf16[32,16,2560]{2,1,0:T(8,128)(2,1)} %bitcast.11, bf16[32,16,2560]{2,1,0:T(8,128)(2,1)} %bitcast.13, bf16[32,16,2560]{2,1,0:T(8,128)(2,1)} %bitcast.15), custom_call_target="tpu_custom_call" | custom-call | tf_op jit(solution)/shard_map/pack/pallas_call | solution.py:515
  7.9 51.4 %main.1 = (f32[1,512]{1,0:T(1,128)}, f32[2,2,384,128]{3,2,1,0:T(8,128)}, f32[512,128]{1,0:T(8,128)}, bf16[20,3,512,128]{3,2,1,0:T(8,128)(2,1)}, bf16[2,3,170,16,128]{4,3,2,1,0:T(8,128)(2,1)}) custom-call(s32[256]{0:T(256)} %lens_ref.3, f32[256]{0:T(256)} %step_ref.1, bf16[16,128]{1,0:T(8,128)(2,1)} %get-tuple-element.17.place, ...), custom_call_target="tpu_custom_call" | custom-call | tf_op jit(solution)/shard_map/main/pallas_call | solution.py:532
  59.3 0.0 copy-start
  59.4 0.0 copy-start.1
  59.4 49.1 %cut.1 = (f32[72,512]{1,0:T(8,128)}, f32[72,384]{1,0:T(8,128)}, f32[72,384]{1,0:T(8,128)}, f32[64,128]{1,0:T(8,128)}) custom-call(s32[8]{0:T(128)} %get-tuple-element.20.scal_ref, f32[2,2,384,128]{3,2,1,0:T(8,128)} %get-tuple-element.21.table_ref, f32[512,128]{1,0:T(8,128)} %get-tuple-element.22.local_ref, bf16[256,256]{1,0:T(8,128)(2,1)} %constant.4.clone.turn_ref, ...), custom_call_target="tpu_custom_call" | custom-call | tf_op jit(solution)/shard_map/cut/pallas_call | solution.py:564
  109.1 11.0 %finish.1 = f32[32,512]{1,0:T(8,128)} custom-call(f32[72,512]{1,0:T(8,128)} %get-tuple-element.25.own_ref, f32[72,384]{1,0:T(8,128)} %get-tuple-element.26.left_ref, f32[72,384]{1,0:T(8,128)} %get-tuple-element.27.right_ref, f32[64,128]{1,0:T(8,128)} %get-tuple-element.28.shift_ref, f32[1]{0:T(128)S(6)} %copy.13.guide_ref), custom_call_target="tpu_custom_call" | custom-call | tf_op jit(solution)/shard_map/finish/pallas_call | solution.py:585
  120.1 0.0 copy-done
  120.1 0.0 copy-done.1
  120.2 1.5 %fusion = f32[512,32]{0,1:T(8,128)} fusion(f32[512,32]{0,1:T(8,128)S(1)} %copy-done, f32[32,512]{1,0:T(8,128)} %finish.1, f32[512]{0:T(512)S(1)} %bitcast.19), kind=kLoop, calls=%fused_computation.1 | loop fusion | flops 32768 | bytes 198656 | tf_op jit(solution)/shard_map/transpose | solution.py:601
Async XLA Ops:
  59.3 60.8 %copy-start = (f32[512,32]{0,1:T(8,128)S(1)}, f32[512,32]{0,1:T(8,128)}, u32[]{:S(2)}) copy-start(f32[512,32]{0,1:T(8,128)} %param.16) | copy-start | bytes 196612
  59.4 60.8 %copy-start.1 = (f32[1,512]{1,0:T(1,128)S(1)}, f32[1,512]{1,0:T(1,128)}, u32[]{:S(2)}) copy-start(f32[1,512]{1,0:T(1,128)} %get-tuple-element.19) | copy-start | bytes 6148

commit v3 on v1

--- a/solution.py
+++ b/solution.py
@@ -19,7 +19,9 @@
 REACH = FAR * TILE
 SPAN = 2 * ROWS + 128
 ACCR = 72
+CHUNKS = (72, 58)
 masked_score = -1e30
+score_scale = math.log2(math.e) / math.sqrt(HD)
 rope_theta = 10000.0
 MESH = pl.DeviceIdType.MESH
 SMEM = pl.BlockSpec(memory_space=pltpu.SMEM)
@@ -48,7 +50,7 @@
 def chunk_tiles(heads):
     cap = capacity(heads)
     if cap >= 150:
-        return (48, 48, 42, cap - 138)
+        return CHUNKS + (cap - sum(CHUNKS),)
     return (FAR, cap - FAR)
 
 
@@ -86,8 +88,8 @@
 
 
 def turner():
-    table = np.zeros((HD, HD), np.float32)
-    for pair in range(HD // 2):
+    table = np.zeros((2 * HD, 2 * HD), np.float32)
+    for pair in range(HD):
         table[2 * pair + 1, 2 * pair] = -1.0
         table[2 * pair, 2 * pair + 1] = 1.0
     return table.astype(jnp.bfloat16)
@@ -207,81 +209,125 @@
     return jnp.cos(angle), jnp.sin(angle)
 
 
-def rotate(x, cosine, sine, turn):
-    swapped = jnp.dot(x, turn, preferred_element_type=jnp.float32)
-    return x.astype(jnp.float32) * cosine + swapped * sine
+def rotate(q, k, cosine, sine, turn):
+    both = jnp.concatenate([q, k], axis=1)
+    swapped = jnp.dot(both, turn, preferred_element_type=jnp.float32)
+    return (
+        q.astype(jnp.float32) * cosine + swapped[:, :HD] * sine,
+        k.astype(jnp.float32) * cosine + swapped[:, HD:] * sine,
+    )
 
 
 def attend(q, k, v, bias):
-    scale = math.log2(math.e) / math.sqrt(HD)
-    scores = lax.dot_general(q, k, (((1,), (1,)), ((), ())), preferred_element_type=jnp.float32)
-    scores = scores * scale + bias
-    top = jnp.max(scores, axis=1, keepdims=True)
-    weight = jnp.exp2(scores - top)
-    total = jnp.sum(weight, axis=1, keepdims=True)
-    summed = jnp.dot(weight.astype(jnp.bfloat16), v, preferred_element_type=jnp.float32)
-    return (summed * (1.0 / total)).astype(jnp.bfloat16)
-
-
-def head_weights(w_block, scale_row):
-    scaled = (w_block.astype(jnp.float32) * (1.0 + scale_row)).astype(jnp.bfloat16)
-    zeros = jnp.zeros((HD - LATC, HD), jnp.bfloat16)
-    first = jnp.concatenate([scaled, zeros], axis=0)
-    row = lax.broadcasted_iota(jnp.int32, (HD, HD), 0)
-    second = (row == LATC).astype(jnp.bfloat16)
-    return jnp.concatenate([first, second], axis=1)
-
-
-def contribution(attended, weights):
+    scores = lax.dot_general(k, q, (((1,), (1,)), ((), ())), preferred_element_type=jnp.float32)
+    scores = scores + bias
+    top = jnp.max(scores, axis=0, keepdims=True)
+    weight = jnp.exp2((scores - top) * score_scale).astype(jnp.bfloat16)
+    taller = jnp.concatenate([v.T, jnp.ones((TILE, v.shape[0]), jnp.bfloat16)], axis=0)
+    summed = jnp.dot(taller, weight, preferred_element_type=jnp.float32)
+    return (summed[:HD] * (1.0 / summed[HD : HD + 1])).astype(jnp.bfloat16)
+
+
+def add_head(acc_ref, index, lanes, attended, w_block, scale_row):
+    weights = (w_block.astype(jnp.float32) * (1.0 + scale_row)).astype(jnp.bfloat16)
+    acc_ref[index + (pl.ds(0, LATC), lanes)] += jnp.dot(
+        weights, attended, preferred_element_type=jnp.float32
+    )
     wide = attended.astype(jnp.float32)
-    squared = (wide * wide).astype(jnp.bfloat16)
-    joined = jnp.concatenate([attended, squared], axis=1)
-    return lax.dot_general(
-        joined, weights, (((1,), (1,)), ((), ())), preferred_element_type=jnp.float32
-    )
+    squared = wide * wide
+    total = squared[0:8]
+    for part in range(1, HD // 8):
+        total = total + squared[part * 8 : part * 8 + 8]
+    acc_ref[index + (pl.ds(LATC, 8), lanes)] += total
 
 
 def local_kernel(
-    scal_ref, place_ref, select_ref, turn_ref, seg_row_ref, seg_col_ref,
-    q_ref, k_ref, v_ref, w_ref, mod_ref, turned_ref, acc_ref, cos_ref, sin_ref, bias_ref,
+    heads, lens_ref, step_ref, scal_ref, place_ref, select_ref, turn_ref, w_ref, mod_ref,
+    q_ref, k_ref, v_ref, turned_ref, acc_ref, steps_ref, shift_ref,
+    rows_in, cos_ref, sin_ref, bias_ref, mine, in_sem, out_sem,
 ):
-    head = pl.program_id(0)
-
-    @pl.when(head == 0)
-    def _():
-        cosine, sine = tables(place_ref[...], select_ref, range(4))
-        cos_ref[...] = cosine
-        sin_ref[...] = sine
-        same = seg_col_ref[...] == seg_row_ref[...]
-        bias_ref[...] = jnp.where(same, 0.0, masked_score)
-        acc_ref[...] = jnp.zeros_like(acc_ref)
-
+    groups = 4 if heads % 4 == 0 else 1
+    width = heads // groups * HD
+    loads = []
+    for group in range(groups):
+        columns = pl.ds(group * width, width)
+        for j, source in enumerate((q_ref, k_ref, v_ref)):
+            copy = pltpu.make_async_copy(
+                source.at[:, :, columns], rows_in.at[j, :, :, columns], in_sem.at[group, j]
+            )
+            copy.start()
+            loads.append(copy)
+    low = lax.axis_index("req") * ROWS
+    lane = lax.broadcasted_iota(jnp.int32, (1, ROWS), 1) + low
+
+    def label(i, carry):
+        end, video, step = carry
+        end = end + lens_ref[i]
+        past = lane >= end
+        video = video + past.astype(jnp.int32)
+        following = step_ref[jnp.minimum(i + 1, lens_ref.shape[0] - 1)]
+        return end, video, jnp.where(past, following, step)
+
+    start = jnp.full((1, ROWS), step_ref[0], jnp.float32)
+    _, video, step = lax.fori_loop(
+        0, lens_ref.shape[0], label,
+        (jnp.int32(0), jnp.zeros((1, ROWS), jnp.int32), start), unroll=8,
+    )
+    steps_ref[...] = step
+    tall = jnp.broadcast_to(video.astype(jnp.float32), (HD, ROWS)).T
+    for part in range(ROWS // HD):
+        wide = jnp.broadcast_to(
+            video[:, part * HD : (part + 1) * HD].astype(jnp.float32), (ROWS, HD)
+        )
+        bias_ref[:, part * HD : (part + 1) * HD] = jnp.where(tall == wide, 0.0, masked_score)
+    cosine, sine = tables(place_ref[...], select_ref, range(4))
+    cos_ref[...] = cosine
+    sin_ref[...] = sine
+    acc_ref[...] = jnp.zeros_like(acc_ref)
+    shift = jnp.sum(w_ref[...].astype(jnp.float32) * mod_ref[0:1, :], axis=1, keepdims=True)
+    shift_ref[...] = jnp.broadcast_to(shift, (LATC, HD))
     turn = turn_ref[...]
-    turned_ref[0, 0] = rotate(q_ref[...], cos_ref[...], sin_ref[...], turn).astype(jnp.bfloat16)
-    turned_ref[0, 1] = rotate(k_ref[...], cos_ref[...], sin_ref[...], turn).astype(jnp.bfloat16)
-    turned_ref[0, 2] = v_ref[...]
+    for copy in loads:
+        copy.wait()
     first = scal_ref[1]
     last = ROWS - scal_ref[3]
-    start = jnp.minimum(first // HD * HD, ROWS // 2)
-    narrow = last <= start + ROWS // 2
-    weights = head_weights(w_ref[...], mod_ref[1:2, :])
-
-    def run(begin, width):
-        keys = turned_ref[0, 1, pl.ds(begin, width)]
-        values = turned_ref[0, 2, pl.ds(begin, width)]
-        for part in range(width // 128):
-            rows = pl.ds(begin + part * 128, 128)
-            bias = bias_ref[rows, pl.ds(begin, width)]
-            attended = attend(turned_ref[0, 0, rows], keys, values, bias)
-            acc_ref[rows] += contribution(attended, weights)
-
-    @pl.when((first < last) & narrow)
-    def _():
-        run(pl.multiple_of(start, HD), ROWS // 2)
-
-    @pl.when((first < last) & jnp.logical_not(narrow))
-    def _():
-        run(0, ROWS)
+    begin = pl.multiple_of(first // HD * HD, HD)
+    extent = jnp.where(first < last, cdiv(last, HD) * HD - begin, 0)
+
+    def keep(head, slot):
+        return pltpu.make_async_copy(mine.at[slot], turned_ref.at[head], out_sem.at[slot])
+
+    def one(head, carry):
+        slot = lax.rem(head, 2)
+        columns = pl.ds(pl.multiple_of(head * HD, HD), HD)
+
+        @pl.when(head >= 2)
+        def _():
+            keep(head, slot).wait()
+
+        q = rows_in[0, :, :, columns].reshape(ROWS, HD)
+        k = rows_in[1, :, :, columns].reshape(ROWS, HD)
+        q, k = rotate(q, k, cos_ref[...], sin_ref[...], turn)
+        mine[slot, 0] = q.astype(jnp.bfloat16)
+        mine[slot, 1] = k.astype(jnp.bfloat16)
+        mine[slot, 2] = rows_in[2, :, :, columns].reshape(ROWS, HD)
+        keep(head, slot).start()
+        for width in (128, 256, 384, 512):
+
+            @pl.when(extent == width)
+            def _(width=width):
+                window = pl.ds(begin, width)
+                attended = attend(
+                    mine[slot, 0, window], mine[slot, 1, window], mine[slot, 2, window],
+                    bias_ref[window, window],
+                )
+                add_head(acc_ref, (), window, attended, w_ref[:, columns], mod_ref[1:2, columns])
+
+        return carry
+
+    lax.fori_loop(0, heads, one, 0)
+    for slot in range(2):
+        keep(slot, slot).wait()
 
 
 def cut_kernel(heads, chunks, c, *refs):
@@ -299,14 +345,14 @@
         table_ref, before_ref = refs[:2]
         del refs[:2]
         if final:
-            local_ref, own_ref, left_out, right_out, shift_ref = refs[:5]
-            del refs[:5]
+            local_ref, own_ref, left_out, right_out = refs[:4]
+            del refs[:4]
         else:
             acc_ref = refs.pop(0)
     if final:
-        span, mine, recv, loc_sem, recv_sem, acc_ref = refs
+        span, mine, recv, bias_ref, loc_sem, recv_sem, acc_ref = refs
     else:
-        span, mine, recv, loc_sem, recv_sem = refs
+        span, mine, recv, bias_ref, loc_sem, recv_sem = refs
     begins = [sum(chunks[:i]) for i in range(len(chunks) + 1)]
     base = begins[here[0]]
     loads = []
@@ -329,8 +375,8 @@
             place_copies.append(copy)
     a_low, b_low, n_low = scal_ref[0], scal_ref[1], scal_ref[2]
     a_high, b_high, n_high = scal_ref[3], scal_ref[4], scal_ref[5]
-    ta_low = cdiv(a_low, TILE)
-    tb_high = cdiv(b_high, TILE)
+    ta_low, tb_low = cdiv(a_low, TILE), cdiv(b_low, TILE)
+    ta_high, tb_high = cdiv(a_high, TILE), cdiv(b_high, TILE)
 
     def done(limit, tiles, total):
         if limit == 0:
@@ -357,6 +403,19 @@
         fetch(jnp.int32(0), 0).start()
 
     span[...] = jnp.zeros_like(span)
+    shapes = []
+    for side, (a, b, ta, tb) in enumerate(
+        ((a_low, b_low, ta_low, tb_low), (a_high, b_high, ta_high, tb_high))
+    ):
+        over = ta + tb > TILES
+        skip = jnp.where(over, TILE, 0)
+        row = lax.broadcasted_iota(jnp.int32, (ROWS, HD), 0)
+        spot = row + skip
+        dead = ta * TILE - a
+        valid = (spot >= dead) & (spot < ta * TILE + b)
+        valid = valid | (over & (row - (ROWS - TILE) >= dead))
+        bias_ref[side] = jnp.where(valid, 0.0, masked_score)
+        shapes.append((over, ROWS - ta * TILE + skip))
     if c == 0:
         acc_ref[...] = jnp.zeros_like(acc_ref)
         for side, copy in enumerate(place_copies):
@@ -391,57 +450,64 @@
         keep = (row >= jnp.where(is_low, REACH - ta * TILE, 0)) & (
             row < jnp.where(is_low, REACH, tb * TILE)
         )
-        cosine, sine = table_ref[side, 0], table_ref[side, 1]
         target = pl.ds(pl.multiple_of(jnp.where(is_low, ROWS - REACH, ROWS), 128), REACH)
-        for j in range(3):
-            x = recv[side, j, pl.ds(offset, FAR)].reshape(REACH, HD)
-            if j < 2:
-                x = rotate(x, cosine, sine, turn)
-            else:
-                x = x.astype(jnp.float32)
+        q, k, v = (recv[side, j, pl.ds(offset, FAR)].reshape(REACH, HD) for j in range(3))
+        q, k = rotate(q, k, table_ref[side, 0], table_ref[side, 1], turn)
+        for j, x in enumerate((q, k, v.astype(jnp.float32))):
             span[j, target] = jnp.where(keep, x, 0.0).astype(jnp.bfloat16)
         for j in range(3):
             span[j, pl.ds(pl.multiple_of(jnp.where(is_low, ROWS, 0), ROWS), ROWS)] = mine[buffer, j]
+        over = ta + tb > TILES
+
+        @pl.when(over)
+        def _():
+            ahead = pl.ds(pl.multiple_of(ROWS - ta * TILE, TILE), TILE)
+            behind = pl.ds(pl.multiple_of(ROWS + (tb - 1) * TILE, TILE), TILE)
+            mixed = lax.broadcasted_iota(jnp.int32, (TILE, HD), 0) < b - (tb - 1) * TILE
+            for j in range(3):
+                merged = jnp.where(
+                    mixed, span[j, behind].astype(jnp.float32), span[j, ahead].astype(jnp.float32)
+                )
+                span[j, behind] = merged.astype(jnp.bfloat16)
+
         columns = pl.ds(pl.multiple_of(head * HD, HD), HD)
-        weights = head_weights(w_ref[:, columns], mod_ref[1:2, columns])
-        start = pl.multiple_of(ROWS - ta * TILE, TILE)
-        extent = (ta + tb) * TILE
-
-        def run(width):
-            keys = span[1, pl.ds(start, width)]
-            values = span[2, pl.ds(start, width)]
-            lane = lax.broadcasted_iota(jnp.int32, (1, width), 1)
-            valid = (lane >= ta * TILE - a) & (lane < ta * TILE + b)
-            bias = jnp.where(valid, 0.0, masked_score)
-            for part in range(width // 128):
-                rows = pl.ds(pl.multiple_of(start + part * 128, TILE), 128)
-                attended = attend(span[0, rows], keys, values, bias)
-                acc_ref[side, rows] += contribution(attended, weights)
-
+        start = pl.multiple_of(ROWS - ta * TILE + jnp.where(over, TILE, 0), TILE)
+        extent = jnp.minimum(ta + tb, TILES) * TILE
         below = 0
-        for width in (256, 384, 512, 640):
+        for width in (128, 256, 384, 512):
 
             @pl.when((extent > below) & (extent <= width))
             def _(width=width):
-                run(width)
+                rows = pl.ds(start, width)
+                bias = jnp.concatenate([bias_ref[side, 0:width]] * (width // HD), axis=1)
+                attended = attend(span[0, rows], span[1, rows], span[2, rows], bias)
+                add_head(
+                    acc_ref, (side,), pl.ds(0, width), attended,
+                    w_ref[:, columns], mod_ref[1:2, columns],
+                )
 
             below = width
         return carry
 
     lax.fori_loop(0, items, one, 0)
     if final:
-        row = lax.broadcasted_iota(jnp.int32, (ROWS, HD), 0)
-        own = jnp.where(row < b_low, acc_ref[0, ROWS : 2 * ROWS], 0.0)
-        own = own + jnp.where(row >= ROWS - a_high, acc_ref[1, 0:ROWS], 0.0)
-        own = own + jnp.where((row >= b_low) & (row < ROWS - a_high), local_ref[...], 0.0)
-        own_ref[...] = own.T[:ACCR]
-        row = lax.broadcasted_iota(jnp.int32, (REACH, HD), 0)
-        back = jnp.where(row >= REACH - a_low, acc_ref[0, ROWS - REACH : ROWS], 0.0)
-        left_out[...] = back.T[:ACCR]
-        back = jnp.where(row < b_high, acc_ref[1, ROWS : ROWS + REACH], 0.0)
-        right_out[...] = back.T[:ACCR]
-        shift = jnp.sum(w_ref[...].astype(jnp.float32) * mod_ref[0:1, :], axis=1, keepdims=True)
-        shift_ref[...] = jnp.broadcast_to(shift, (LATC, HD))
+        halves = []
+        lane = lax.broadcasted_iota(jnp.int32, (ACCR, 2 * ROWS), 1)
+        for side, (over, start) in enumerate(shapes):
+            placed = jnp.concatenate([acc_ref[side], jnp.zeros((ACCR, ROWS), jnp.float32)], axis=1)
+            placed = pltpu.roll(placed, start, 1)
+            swapped = jnp.concatenate([placed[:, ROWS:], placed[:, :ROWS]], axis=1)
+            extra = over & (lane < start)
+            placed = jnp.where(extra, swapped, placed)
+            halves.append((placed[:, :ROWS], placed[:, ROWS:]))
+        lane = lax.broadcasted_iota(jnp.int32, (ACCR, ROWS), 1)
+        own = jnp.where(lane < b_low, halves[0][1], 0.0)
+        own = own + jnp.where(lane >= ROWS - a_high, halves[1][0], 0.0)
+        own_ref[...] = own + jnp.where((lane >= b_low) & (lane < ROWS - a_high), local_ref[...], 0.0)
+        back = jnp.where(lane >= ROWS - a_low, halves[0][0], 0.0)
+        left_out[...] = back[:, ROWS - REACH :]
+        back = jnp.where(lane < b_high, halves[1][1], 0.0)
+        right_out[...] = back[:, :REACH]
 
 
 def finish_kernel(
@@ -472,7 +538,8 @@
     total = own_ref[...]
     total = total + jnp.concatenate([none, from_right[...]], axis=1)
     total = total + jnp.concatenate([from_left[...], none], axis=1)
-    inverse = lax.rsqrt(total[LATC : LATC + 1] * (1.0 / features) + 1e-06)
+    square = jnp.sum(total[LATC:], axis=0, keepdims=True)
+    inverse = lax.rsqrt(square * (1.0 / features) + 1e-06)
     velocity[...] = total[:LATC] * inverse + shift_ref[:, 0:1]
     half = LATC // 2
     give = pltpu.make_async_remote_copy(
@@ -531,49 +598,36 @@
         from_left.append(moved(to_right[c], 1, ring))
         from_right.append(moved(to_left[c], -1, ring))
 
-    video_ends = jnp.cumsum(lengths)
-    first_row = lax.axis_index("req") * ROWS
-    rows_here = first_row + jnp.arange(ROWS, dtype=jnp.int32)
-    videos = jnp.sum((video_ends[:, None] <= rows_here[None, :]).astype(jnp.int32), axis=0)
-    chosen = videos[None, :] == jnp.arange(step_sizes.shape[0], dtype=jnp.int32)[:, None]
-    steps = jnp.sum(jnp.where(chosen, step_sizes[:, None], 0.0), axis=0)
-
     select = jnp.asarray(selector())
     turn = jnp.asarray(turner())
     w_turned = w_head.T
     pair_ops = ROWS * ROWS * HD * 4
-    turned, local_acc = pl.pallas_call(
-        local_kernel,
-        grid=(heads,),
-        out_shape=[sized((heads, 3, ROWS, HD), bf16), sized((ROWS, HD), f32)],
-        in_specs=[
-            SMEM,
-            VMEM,
-            VMEM,
-            VMEM,
-            pl.BlockSpec((1, ROWS), lambda h: (0, 0)),
-            pl.BlockSpec((ROWS, 1), lambda h: (0, 0)),
-            pl.BlockSpec((ROWS, HD), lambda h: (0, h)),
-            pl.BlockSpec((ROWS, HD), lambda h: (0, h)),
-            pl.BlockSpec((ROWS, HD), lambda h: (0, h)),
-            pl.BlockSpec((LATC, HD), lambda h: (0, h)),
-            pl.BlockSpec((2, HD), lambda h: (0, h)),
+    turned, local_acc, steps, shift = pl.pallas_call(
+        functools.partial(local_kernel, heads),
+        out_shape=[
+            sized((heads, 3, ROWS, HD), bf16),
+            sized((ACCR, ROWS), f32),
+            sized((1, ROWS), f32),
+            sized((LATC, HD), f32),
         ],
-        out_specs=[
-            pl.BlockSpec((1, 3, ROWS, HD), lambda h: (h, 0, 0, 0)),
-            pl.BlockSpec((ROWS, HD), lambda h: (0, 0)),
-        ],
+        in_specs=[SMEM, SMEM, SMEM] + [VMEM] * 5 + [ANY] * 3,
+        out_specs=[ANY, VMEM, VMEM, VMEM],
         scratch_shapes=[
+            pltpu.VMEM((3, TILES, TILE, features), bf16),
             pltpu.VMEM((ROWS, HD), f32),
             pltpu.VMEM((ROWS, HD), f32),
             pltpu.VMEM((ROWS, ROWS), f32),
+            pltpu.VMEM((2, 3, ROWS, HD), bf16),
+            pltpu.SemaphoreType.DMA((4, 3)),
+            pltpu.SemaphoreType.DMA((2,)),
         ],
         cost_estimate=pl.CostEstimate(
             flops=heads * pair_ops, bytes_accessed=6 * ROWS * features * 2, transcendentals=0
         ),
         name="local",
     )(
-        scal, place, select, turn, videos[None, :], videos[:, None], q, k, v, w_turned, modulation
+        lengths, step_sizes, scal, place, select, turn, w_turned, modulation,
+        tiled(q), tiled(k), tiled(v),
     )
 
     acc = table = None
@@ -587,7 +641,7 @@
         if c > 0:
             operands += [table, acc]
             specs += [VMEM, VMEM]
-        acc_shape = sized((2, SPAN, HD), f32)
+        acc_shape = sized((2, ACCR, ROWS), f32)
         if final:
             operands.append(local_acc)
             specs.append(VMEM)
@@ -595,7 +649,6 @@
                 sized((ACCR, ROWS), f32),
                 sized((ACCR, REACH), f32),
                 sized((ACCR, REACH), f32),
-                sized((LATC, HD), f32),
             ]
         elif c == 0:
             out_shape = [acc_shape, sized((2, 2, REACH, HD), f32)]
@@ -605,11 +658,12 @@
             pltpu.VMEM((3, SPAN, HD), bf16),
             pltpu.VMEM((2, 3, ROWS, HD), bf16),
             pltpu.VMEM((2, 3, 2 * FAR + sum(chunks[i] for i in here), TILE, HD), bf16),
+            pltpu.VMEM((2, ROWS, HD), f32),
             pltpu.SemaphoreType.DMA((2,)),
             pltpu.SemaphoreType.DMA((2, 3)),
         ]
         if final:
-            scratch.append(pltpu.VMEM((2, SPAN, HD), f32))
+            scratch.append(pltpu.VMEM((2, ACCR, ROWS), f32))
         results = pl.pallas_call(
             functools.partial(cut_kernel, heads, chunks, c),
             out_shape=out_shape,
@@ -621,7 +675,7 @@
             ),
         )(*operands)
         if final:
-            own, back_left, back_right, shift = results
+            own, back_left, back_right = results
         elif c == 0:
             acc, table = results
         else:
@@ -643,7 +697,7 @@
         compiler_params=pltpu.CompilerParams(collective_id=0, has_side_effects=True),
         name="finish",
     )(own, back_left, back_right, shift, guide_scale)
-    return (latents.T + steps[None, :] * guided).T
+    return (latents.T + steps * guided).T
 
 
 def solution(mesh):

time: 173 us -> 127 us (0.73)
  Pallas kernels: 118 us -> 93.4 us
  waiting for transfers between devices: 31.2 us -> 14.1 us
  starting transfers between devices: 15.9 us -> 14 us
    ppermute x8 -> x6, waiting for transfers between devices: 31.2 us -> 14.1 us  [moved(): lax.ppermute(value, 'req', [(i, (i + step) % ring) for i in range(ring)])]
    pallas_call x1, Pallas kernels: 41.9 us -> 26.5 us  [per_device(): pl.pallas_call(functools.partial(local_kernel, heads), out_shape=[sized((...]
    pallas_call x4 -> x3, Pallas kernels: 32.6 us -> 26.7 us  [per_device(): pl.pallas_call(functools.partial(cut_kernel, heads, chunks, c), out_shape...]
    pallas_call x1, Pallas kernels: 35 us -> 31.9 us  [per_device(): pl.pallas_call(functools.partial(finish_kernel, features, ring), out_shap...]
    ppermute x8 -> x6, starting transfers between devices: 15.9 us -> 14 us  [moved(): lax.ppermute(value, 'req', [(i, (i + step) % ring) for i in range(ring)])]
  transfers between devices with their start and end apart: 8 -> 6, of which waited for: 2 -> 1; matrix products, arithmetic and copies ran while one was open for 1% -> 0% of each run, Pallas kernels for 41% -> 39%
where the time goes in v3:
time: 127 us; the launch traced here: 126 us
  Pallas kernels  93.4 us (74%)
  waiting for transfers between devices  14.1 us (11%)
  starting transfers between devices  14 us (11%)
  local copies, waits for them, and re-layouts  2.04 us (2%)
  other arithmetic  1.48 us (1%)
    pallas_call x1, Pallas kernels, per_device(): pl.pallas_call(functools.partial(finish_kernel, features, ring), out_shap...  31.9 us
    pallas_call x3, Pallas kernels, per_device(): pl.pallas_call(functools.partial(cut_kernel, heads, chunks, c), out_shape...  26.7 us
    pallas_call x1, Pallas kernels, per_device(): pl.pallas_call(functools.partial(local_kernel, heads), out_shape=[sized((...  26.5 us
    ppermute x6, waiting for transfers between devices, moved(): lax.ppermute(value, 'req', [(i, (i + step) % ring) for i in range(ring)])  14.1 us
    ppermute x6, starting transfers between devices, moved(): lax.ppermute(value, 'req', [(i, (i + step) % ring) for i in range(ring)])  14 us
    pallas_call x1, Pallas kernels, per_device(): pl.pallas_call(functools.partial(pack_kernel, heads, chunks), out_shape=[...  8.3 us
  transfers between devices with their start and end apart: 6, of which 1 were waited for; matrix products, arithmetic and copies ran while one was open for 0% of the time, Pallas kernels for 39%

profile of v3, /device:TPU:17, one launch (start us, length us, event | category | flops | bytes accessed | tf_op | source)
XLA Modules:
  0.0 125.8 jit_solution(14432960396694117951)
XLA Ops:
  0.0 8.3 %pack.1 = (s32[8]{0:T(128)}, bf16[16,128]{1,0:T(8,128)(2,1)}, bf16[3,73,16,128]{3,2,1,0:T(8,128)(2,1)}, bf16[3,58,16,128]{3,2,1,0:T(8,128)(2,1)}, bf16[3,40,16,1...) custom-call(s32[256]{0:T(256)} %lens_ref.3, ...), custom_call_target="tpu_custom_call" | custom-call | tf_op jit(solution)/shard_map/pack/pallas_call | solution.py:580
  8.3 0.1 collective-permute-start.4
  8.5 6.5 %collective-permute-start.5 = (bf16[3,73,16,128]{3,2,1,0:T(8,128)(2,1)}, bf16[3,73,16,128]{3,2,1,0:T(8,128)(2,1)S(1)}, u32[]{:S(2)}, u32[]{:S(2)}) collective-permute-start(bf16[3,73,16,128]{3,2,1,0:T(8,128)(2,1)} %get-tuple-element.31), channel_id=1, source_target_pairs={{0,127},{1,0},{2,1},{3,2},{4,3},{5,4},{6,5},{7,6},{8,7},{9,8},{10,... | collective-permute-start | bytes 2691080 | tf_op jit(solution)/shard_map/ppermute | solution.py:559
  15.0 0.0 collective-permute-start
  15.0 5.7 %collective-permute-start.2 = (bf16[3,58,16,128]{3,2,1,0:T(8,128)(2,1)}, bf16[3,58,16,128]{3,2,1,0:T(8,128)(2,1)S(1)}, u32[]{:S(2)}, u32[]{:S(2)}) collective-permute-start(bf16[3,58,16,128]{3,2,1,0:T(8,128)(2,1)} %get-tuple-element.28), channel_id=1, source_target_pairs={{0,127},{1,0},{2,1},{3,2},{4,3},{5,4},{6,5},{7,6},{8,7},{9,8},{10,... | collective-permute-start | bytes 2138120 | tf_op jit(solution)/shard_map/ppermute | solution.py:559
  20.7 0.0 collective-permute-start.1
  20.7 14.0 %collective-permute-done.4.refs_6_ = bf16[3,73,16,128]{3,2,1,0:T(8,128)(2,1)S(1)} collective-permute-done((bf16[3,73,16,128]{3,2,1,0:T(8,128)(2,1)}, bf16[3,73,16,128]{3,2,1,0:T(8,128)(2,1)S(1)}, u32[]{:S(2)}, u32[]{:S(2)}) %collective-permute-start.4) | collective-permute-done | bytes 897056 | tf_op jit(solution)/shard_map/ppermute | solution.py:559
  34.7 1.6 %collective-permute-start.3 = (bf16[3,40,16,128]{3,2,1,0:T(8,128)(2,1)}, bf16[3,40,16,128]{3,2,1,0:T(8,128)(2,1)}, u32[]{:S(2)}, u32[]{:S(2)}) collective-permute-start(bf16[3,40,16,128]{3,2,1,0:T(8,128)(2,1)} %get-tuple-element.29), channel_id=1, source_target_pairs={{0,127},{1,0},{2,1},{3,2},{4,3},{5,4},{6,5},{7,6},{8,7},{9,8},{10,... | collective-permute-start | bytes 1474568 | tf_op jit(solution)/shard_map/ppermute | solution.py:559
  37.0 26.5 %local.1 = (bf16[20,3,512,128]{3,2,1,0:T(8,128)(2,1)}, f32[72,512]{1,0:T(8,128)}, f32[1,512]{1,0:T(1,128)}, f32[64,128]{1,0:T(8,128)}) custom-call(s32[256]{0:T(256)} %lens_ref.3, f32[256]{0:T(256)} %step_ref.1, s32[8]{0:T(128)} %get-tuple-element.22.scal_ref.refs_0_, bf16[16,128]{1,0:T(8,128)(2,1)} %get-tuple-element.23.place_ref, ...), custom_call_target="tpu_custom_call" | custom-call | flops 2684354560 | bytes 15728640 | tf_op jit(solution)/shard_map/local/pallas_call | solution.py:605
  63.5 0.0 collective-permute-done.5.refs_7_.refs_8_
  63.6 0.0 copy-start.1
  63.6 1.0 copy-done.1
  64.5 18.5 %shard_map.118 = (f32[2,72,512]{2,1,0:T(8,128)}, f32[2,2,384,128]{3,2,1,0:T(8,128)}) custom-call(s32[8]{0:T(128)} %get-tuple-element.22.scal_ref.refs_0_, bf16[3,4,16,128]{3,2,1,0:T(8,128)(2,1)} %constant.4.clone.select_ref.refs_1_, bf16[256,256]{1,0:T(8,128)(2,1)} %constant.5.clone.turn_ref.refs_2_, bf16[64,2560]{1,0:T(8,128)(2,1)} %bitcast.12, ...), custom_call_target="tpu_custom_call" | custom-call | flops 894784832 | bytes 4194304 | tf_op jit(solution)/shard_map/pallas_call | solution.py:667
  83.0 0.0 collective-permute-done.refs_7_.refs_6_
  83.0 0.0 collective-permute-done.2.refs_9_.refs_8_
  83.0 0.8 copy-done.2
  83.8 0.3 copy-done.3
  84.1 4.1 %shard_map.119.refs_11_ = f32[2,72,512]{2,1,0:T(8,128)} custom-call(s32[8]{0:T(128)} %get-tuple-element.22.scal_ref.refs_0_, bf16[3,4,16,128]{3,2,1,0:T(8,128)(2,1)} %constant.4.clone.select_ref.refs_1_, bf16[256,256]{1,0:T(8,128)(2,1)} %constant.5.clone.turn_ref.refs_2_, bf16[64,2560]{1,0:T(8,128)(2,1)} %bitcast.13, f32[2,2560]{1,0:T(2,128)} %refs_4_.5, ...), custom_call_target="tpu_custom_call" | custom-call | flops 894784832 | bytes 4194304 | tf_op jit(solution)/shard_map/pallas_call | solution.py:667
  88.2 0.0 collective-permute-done.1.refs_7_
  88.2 0.0 collective-permute-done.3.refs_9_
  88.2 0.0 copy-start.4
  88.2 4.2 %shard_map.120 = (f32[72,512]{1,0:T(8,128)}, f32[72,384]{1,0:T(8,128)}, f32[72,384]{1,0:T(8,128)}) custom-call(s32[8]{0:T(128)} %get-tuple-element.22.scal_ref.refs_0_, bf16[3,4,16,128]{3,2,1,0:T(8,128)(2,1)} %constant.4.clone.select_ref.refs_1_, bf16[256,256]{1,0:T(8,128)(2,1)} %constant.5.clone.turn_ref.refs_2_, bf16[64,2560]{1,0:T(8,128)(2,1)} %bitcast.14, ...), custom_call_target="tpu_custom_call" | custom-call | flops 894784832 | bytes 4194304 | tf_op jit(solution)/shard_map/pallas_call | solution.py:667
  92.4 31.9 %finish.1 = f32[32,512]{1,0:T(8,128)} custom-call(f32[72,512]{1,0:T(8,128)} %get-tuple-element.35.own_ref, f32[72,384]{1,0:T(8,128)} %get-tuple-element.36.left_ref, f32[72,384]{1,0:T(8,128)} %get-tuple-element.37.right_ref, f32[64,128]{1,0:T(8,128)} %get-tuple-element.38.shift_ref, f32[1]{0:T(128)S(6)} %copy.13.guide_ref), custom_call_target="tpu_custom_call" | custom-call | tf_op jit(solution)/shard_map/finish/pallas_call | solution.py:684
  124.3 1.5 %fusion = f32[512,32]{0,1:T(8,128)} fusion(f32[512,32]{0,1:T(8,128)S(1)} %copy-done.4, f32[32,512]{1,0:T(8,128)} %finish.1, f32[512]{0:T(512)S(1)} %bitcast.21), kind=kLoop, calls=%fused_computation.1 | loop fusion | flops 32768 | bytes 198656 | tf_op jit(solution)/shard_map/transpose | solution.py:700
  (7 shorter events, 0.0 us)
Async XLA Ops:
  8.3 26.4 %collective-permute-start.4 = (bf16[3,73,16,128]{3,2,1,0:T(8,128)(2,1)}, bf16[3,73,16,128]{3,2,1,0:T(8,128)(2,1)S(1)}, u32[]{:S(2)}, u32[]{:S(2)}) collective-permute-start(bf16[3,73,16,128]{3,2,1,0:T(8,128)(2,1)} %get-tuple-element.30), channel_id=1, source_target_pairs={{0,1},{1,2},{2,3},{3,4},{4,5},{5,6},{6,7},{7,8},{8,9},{9,10},{10,1... | collective-permute-start | bytes 2691080 | tf_op jit(solution)/shard_map/ppermute | solution.py:559
  8.5 55.1 %collective-permute-start.5 = (bf16[3,73,16,128]{3,2,1,0:T(8,128)(2,1)}, bf16[3,73,16,128]{3,2,1,0:T(8,128)(2,1)S(1)}, u32[]{:S(2)}, u32[]{:S(2)}) collective-permute-start(bf16[3,73,16,128]{3,2,1,0:T(8,128)(2,1)} %get-tuple-element.31), channel_id=1, source_target_pairs={{0,127},{1,0},{2,1},{3,2},{4,3},{5,4},{6,5},{7,6},{8,7},{9,8},{10,... | collective-permute-start | bytes 2691080 | tf_op jit(solution)/shard_map/ppermute | solution.py:559
  15.0 68.0 %collective-permute-start = (bf16[3,58,16,128]{3,2,1,0:T(8,128)(2,1)}, bf16[3,58,16,128]{3,2,1,0:T(8,128)(2,1)S(1)}, u32[]{:S(2)}, u32[]{:S(2)}) collective-permute-start(bf16[3,58,16,128]{3,2,1,0:T(8,128)(2,1)} %get-tuple-element.26), channel_id=1, source_target_pairs={{0,1},{1,2},{2,3},{3,4},{4,5},{5,6},{6,7},{7,8},{8,9},{9,10},{10,1... | collective-permute-start | bytes 2138120 | tf_op jit(solution)/shard_map/ppermute | solution.py:559
  15.0 68.0 %collective-permute-start.2 = (bf16[3,58,16,128]{3,2,1,0:T(8,128)(2,1)}, bf16[3,58,16,128]{3,2,1,0:T(8,128)(2,1)S(1)}, u32[]{:S(2)}, u32[]{:S(2)}) collective-permute-start(bf16[3,58,16,128]{3,2,1,0:T(8,128)(2,1)} %get-tuple-element.28), channel_id=1, source_target_pairs={{0,127},{1,0},{2,1},{3,2},{4,3},{5,4},{6,5},{7,6},{8,7},{9,8},{10,... | collective-permute-start | bytes 2138120 | tf_op jit(solution)/shard_map/ppermute | solution.py:559
  20.7 67.5 %collective-permute-start.1 = (bf16[3,40,16,128]{3,2,1,0:T(8,128)(2,1)}, bf16[3,40,16,128]{3,2,1,0:T(8,128)(2,1)}, u32[]{:S(2)}, u32[]{:S(2)}) collective-permute-start(bf16[3,40,16,128]{3,2,1,0:T(8,128)(2,1)} %get-tuple-element.27), channel_id=1, source_target_pairs={{0,1},{1,2},{2,3},{3,4},{4,5},{5,6},{6,7},{7,8},{8,9},{9,10},{10,1... | collective-permute-start | bytes 1474568 | tf_op jit(solution)/shard_map/ppermute | solution.py:559
  34.7 28.8 %copy-start = (bf16[3,73,16,128]{3,2,1,0:T(8,128)(2,1)}, bf16[3,73,16,128]{3,2,1,0:T(8,128)(2,1)S(1)}, u32[]{:S(2)}) copy-start(bf16[3,73,16,128]{3,2,1,0:T(8,128)(2,1)S(1)} %collective-permute-done.4.refs_6_) | copy-start | bytes 2691076
  34.7 53.4 %collective-permute-start.3 = (bf16[3,40,16,128]{3,2,1,0:T(8,128)(2,1)}, bf16[3,40,16,128]{3,2,1,0:T(8,128)(2,1)}, u32[]{:S(2)}, u32[]{:S(2)}) collective-permute-start(bf16[3,40,16,128]{3,2,1,0:T(8,128)(2,1)} %get-tuple-element.29), channel_id=1, source_target_pairs={{0,127},{1,0},{2,1},{3,2},{4,3},{5,4},{6,5},{7,6},{8,7},{9,8},{10,... | collective-permute-start | bytes 1474568 | tf_op jit(solution)/shard_map/ppermute | solution.py:559
  63.6 1.0 copy-start.1
  83.0 0.8 copy-start.2
  83.0 1.1 copy-start.3
  88.2 36.1 %copy-start.4 = (f32[512,32]{0,1:T(8,128)S(1)}, f32[512,32]{0,1:T(8,128)}, u32[]{:S(2)}) copy-start(f32[512,32]{0,1:T(8,128)} %param.16) | copy-start | bytes 196612
  88.2 36.1 %copy-start.5 = (f32[1,512]{1,0:T(1,128)S(1)}, f32[1,512]{1,0:T(1,128)}, u32[]{:S(2)}) copy-start(f32[1,512]{1,0:T(1,128)} %get-tuple-element.24) | copy-start | bytes 6148

commit v4 on v3

--- a/solution.py
+++ b/solution.py
@@ -19,7 +19,7 @@
 REACH = FAR * TILE
 SPAN = 2 * ROWS + 128
 ACCR = 72
-CHUNKS = (72, 58)
+CHUNKS = (104,)
 masked_score = -1e30
 score_scale = math.log2(math.e) / math.sqrt(HD)
 rope_theta = 10000.0
@@ -154,23 +154,28 @@
     pieces = [placed[a : a + 1, g * HD : (g + 1) * HD] for a in range(3) for g in range(4)]
     pieces.append(jnp.zeros((TILE - 12, HD), jnp.float32))
     place_ref[...] = jnp.concatenate(pieces, axis=0).astype(jnp.bfloat16)
-    for copy in loads:
-        copy.wait()
-
-    def pack(direction, first_tile, first_head, tiles, total):
-        def one(slot, carry):
-            columns = pl.ds(pl.multiple_of((first_head + slot) * HD, HD), HD)
+
+    def pack(direction, first_tile, first_head, tiles, begin, end):
+        def one(head, carry):
+            columns = pl.ds(pl.multiple_of(head * HD, HD), HD)
             for j in range(3):
-                packed[direction, j, pl.ds(slot * tiles, FAR)] = rows_in[
+                packed[direction, j, pl.ds((head - first_head) * tiles, FAR)] = rows_in[
                     j, pl.ds(first_tile, FAR), :, columns
                 ]
             return carry
 
-        lax.fori_loop(0, total, one, 0)
+        lax.fori_loop(begin, end, one, 0)
 
     ta, tb = cdiv(a_high, TILE), cdiv(b_low, TILE)
-    pack(0, TILES - ta, 0, ta, jnp.where(a_high > 0, n_high, 0))
-    pack(1, 0, n_low, tb, jnp.where(b_low > 0, heads - n_low, 0))
+    last_right = jnp.where(a_high > 0, n_high, 0)
+    first_left = jnp.where(b_low > 0, n_low, heads)
+    each = heads // groups
+    for group in range(groups):
+        for copy in loads[3 * group : 3 * group + 3]:
+            copy.wait()
+        begin, end = group * each, (group + 1) * each
+        pack(0, TILES - ta, 0, ta, begin, jnp.minimum(end, last_right))
+        pack(1, 0, n_low, tb, jnp.maximum(begin, first_left), end)
     stores = []
     for direction, targets in enumerate((right_refs, left_refs)):
         begin = 0
@@ -350,9 +355,9 @@
         else:
             acc_ref = refs.pop(0)
     if final:
-        span, mine, recv, bias_ref, loc_sem, recv_sem, acc_ref = refs
+        span, recv, bias_ref, loc_sem, recv_sem, acc_ref = refs
     else:
-        span, mine, recv, bias_ref, loc_sem, recv_sem = refs
+        span, recv, bias_ref, loc_sem, recv_sem = refs
     begins = [sum(chunks[:i]) for i in range(len(chunks) + 1)]
     base = begins[here[0]]
     loads = []
@@ -396,11 +401,10 @@
         return jnp.where(i < low_count, low_first + i, n_high + high_first + i - low_count)
 
     def fetch(i, buffer):
-        return pltpu.make_async_copy(turned_ref.at[head_of(i)], mine.at[buffer], loc_sem.at[buffer])
-
-    @pl.when(items > 0)
-    def _():
-        fetch(jnp.int32(0), 0).start()
+        rows = pl.ds(pl.multiple_of(jnp.where(i < low_count, ROWS, 0), ROWS), ROWS)
+        return pltpu.make_async_copy(
+            turned_ref.at[head_of(i)], span.at[buffer, :, rows], loc_sem.at[buffer]
+        )
 
     span[...] = jnp.zeros_like(span)
     shapes = []
@@ -426,6 +430,11 @@
             table_ref[side, 1] = sine
     else:
         acc_ref[...] = before_ref[...]
+
+    @pl.when(items > 0)
+    def _():
+        fetch(jnp.int32(0), 0).start()
+
     for copy in loads:
         copy.wait()
     turn = turn_ref[...]
@@ -446,17 +455,24 @@
         b = jnp.where(is_low, b_low, b_high)
         ta, tb = cdiv(a, TILE), cdiv(b, TILE)
         offset = jnp.where(is_low, slot * ta + ta, slot * tb + FAR) - base
-        row = lax.broadcasted_iota(jnp.int32, (REACH, HD), 0)
-        keep = (row >= jnp.where(is_low, REACH - ta * TILE, 0)) & (
-            row < jnp.where(is_low, REACH, tb * TILE)
-        )
-        target = pl.ds(pl.multiple_of(jnp.where(is_low, ROWS - REACH, ROWS), 128), REACH)
-        q, k, v = (recv[side, j, pl.ds(offset, FAR)].reshape(REACH, HD) for j in range(3))
-        q, k = rotate(q, k, table_ref[side, 0], table_ref[side, 1], turn)
-        for j, x in enumerate((q, k, v.astype(jnp.float32))):
-            span[j, target] = jnp.where(keep, x, 0.0).astype(jnp.bfloat16)
-        for j in range(3):
-            span[j, pl.ds(pl.multiple_of(jnp.where(is_low, ROWS, 0), ROWS), ROWS)] = mine[buffer, j]
+        first = jnp.where(is_low, REACH - ta * TILE, 0)
+        last = jnp.where(is_low, REACH, tb * TILE)
+        target = jnp.where(is_low, ROWS - REACH, ROWS)
+        for block in range(REACH // HD):
+            low, high = block * HD, (block + 1) * HD
+
+            @pl.when((first < high) & (last > low))
+            def _(low=low, high=high):
+                row = lax.broadcasted_iota(jnp.int32, (HD, HD), 0) + low
+                keep = (row >= first) & (row < last)
+                tiles = pl.ds(offset + low // TILE, HD // TILE)
+                q, k, v = (recv[side, j, tiles].reshape(HD, HD) for j in range(3))
+                cosine, sine = table_ref[side, 0, low:high], table_ref[side, 1, low:high]
+                q, k = rotate(q, k, cosine, sine, turn)
+                rows = pl.ds(pl.multiple_of(target + low, HD), HD)
+                for j, x in enumerate((q, k, v.astype(jnp.float32))):
+                    span[buffer, j, rows] = jnp.where(keep, x, 0.0).astype(jnp.bfloat16)
+
         over = ta + tb > TILES
 
         @pl.when(over)
@@ -466,9 +482,9 @@
             mixed = lax.broadcasted_iota(jnp.int32, (TILE, HD), 0) < b - (tb - 1) * TILE
             for j in range(3):
                 merged = jnp.where(
-                    mixed, span[j, behind].astype(jnp.float32), span[j, ahead].astype(jnp.float32)
+                    mixed, span[buffer, j, behind].astype(jnp.float32), span[buffer, j, ahead].astype(jnp.float32)
                 )
-                span[j, behind] = merged.astype(jnp.bfloat16)
+                span[buffer, j, behind] = merged.astype(jnp.bfloat16)
 
         columns = pl.ds(pl.multiple_of(head * HD, HD), HD)
         start = pl.multiple_of(ROWS - ta * TILE + jnp.where(over, TILE, 0), TILE)
@@ -480,7 +496,9 @@
             def _(width=width):
                 rows = pl.ds(start, width)
                 bias = jnp.concatenate([bias_ref[side, 0:width]] * (width // HD), axis=1)
-                attended = attend(span[0, rows], span[1, rows], span[2, rows], bias)
+                attended = attend(
+                    span[buffer, 0, rows], span[buffer, 1, rows], span[buffer, 2, rows], bias
+                )
                 add_head(
                     acc_ref, (side,), pl.ds(0, width), attended,
                     w_ref[:, columns], mod_ref[1:2, columns],
@@ -655,8 +673,7 @@
         else:
             out_shape = [acc_shape]
         scratch = [
-            pltpu.VMEM((3, SPAN, HD), bf16),
-            pltpu.VMEM((2, 3, ROWS, HD), bf16),
+            pltpu.VMEM((2, 3, SPAN, HD), bf16),
             pltpu.VMEM((2, 3, 2 * FAR + sum(chunks[i] for i in here), TILE, HD), bf16),
             pltpu.VMEM((2, ROWS, HD), f32),
             pltpu.SemaphoreType.DMA((2,)),

time: 127 us -> 105 us (0.83)
  waiting for transfers between devices: 14.1 us -> 0.01 us
  Pallas kernels: 93.4 us -> 85.1 us
    ppermute x6 -> x4, waiting for transfers between devices: 14.1 us -> 0.01 us  [moved(): lax.ppermute(value, 'req', [(i, (i + step) % ring) for i in range(ring)])]
    pallas_call x3 -> x2, Pallas kernels: 26.7 us -> 22.5 us  [per_device(): pl.pallas_call(functools.partial(cut_kernel, heads, chunks, c), out_shape...]
    pallas_call x1, Pallas kernels: 31.9 us -> 29.5 us  [per_device(): pl.pallas_call(functools.partial(finish_kernel, features, ring), out_shap...]
    pallas_call x1, Pallas kernels: 8.3 us -> 6.97 us  [per_device(): pl.pallas_call(functools.partial(pack_kernel, heads, chunks), out_shape=[...]
    ppermute x6 -> x4, starting transfers between devices: 14 us -> 13.5 us  [moved(): lax.ppermute(value, 'req', [(i, (i + step) % ring) for i in range(ring)])]
  transfers between devices with their start and end apart: 6 -> 4, of which waited for: 1 -> 0; matrix products, arithmetic and copies ran while one was open for 0% -> 0% of each run, Pallas kernels for 39% -> 43%
where the time goes in v4:
time: 105 us; the launch traced here: 103 us
  Pallas kernels  85.1 us (81%)
  starting transfers between devices  13.5 us (13%)
  local copies, waits for them, and re-layouts  2.43 us (2%)
  other arithmetic  1.49 us (1%)
    pallas_call x1, Pallas kernels, per_device(): pl.pallas_call(functools.partial(finish_kernel, features, ring), out_shap...  29.5 us
    pallas_call x1, Pallas kernels, per_device(): pl.pallas_call(functools.partial(local_kernel, heads), out_shape=[sized((...  26.2 us
    pallas_call x2, Pallas kernels, per_device(): pl.pallas_call(functools.partial(cut_kernel, heads, chunks, c), out_shape...  22.5 us
    ppermute x4, starting transfers between devices, moved(): lax.ppermute(value, 'req', [(i, (i + step) % ring) for i in range(ring)])  13.5 us
    pallas_call x1, Pallas kernels, per_device(): pl.pallas_call(functools.partial(pack_kernel, heads, chunks), out_shape=[...  6.97 us
    unnamed x10, local copies, waits for them, and re-layouts  2.43 us
  transfers between devices with their start and end apart: 4, of which 0 were waited for; matrix products, arithmetic and copies ran while one was open for 0% of the time, Pallas kernels for 43%

profile of v4, /device:TPU:17, one launch (start us, length us, event | category | flops | bytes accessed | tf_op | source)
XLA Modules:
  0.0 103.3 jit_solution(7321228272920263727)
XLA Ops:
  0.0 7.0 %pack.1 = (s32[8]{0:T(128)}, bf16[16,128]{1,0:T(8,128)(2,1)}, bf16[3,105,16,128]{3,2,1,0:T(8,128)(2,1)}, bf16[3,66,16,128]{3,2,1,0:T(8,128)(2,1)}, bf16[3,105,16...) custom-call(s32[256]{0:T(256)} %lens_ref.3, s32[3,512]{1,0:T(4,128)} %pos_ref.1, bf16[32,16,2560]{2,1,0:T(8,128)(2,1)} %bitcast.11, ...), custom_call_target="tpu_custom_call" | custom-call | tf_op jit(solution)/shard_map/pack/pallas_call | solution.py:598
  7.0 1.3 %collective-permute-start = (bf16[3,105,16,128]{3,2,1,0:T(8,128)(2,1)}, bf16[3,105,16,128]{3,2,1,0:T(8,128)(2,1)S(1)}, u32[]{:S(2)}, u32[]{:S(2)}) collective-permute-start(bf16[3,105,16,128]{3,2,1,0:T(8,128)(2,1)} %get-tuple-element.24), channel_id=1, source_target_pairs={{0,1},{1,2},{2,3},{3,4},{4,5},{5,6},{6,7},{7,8},{8,9},{9,10},{10,1... | collective-permute-start | bytes 3870728 | tf_op jit(solution)/shard_map/ppermute | solution.py:577
  8.3 6.5 %collective-permute-start.2 = (bf16[3,105,16,128]{3,2,1,0:T(8,128)(2,1)}, bf16[3,105,16,128]{3,2,1,0:T(8,128)(2,1)S(1)}, u32[]{:S(2)}, u32[]{:S(2)}) collective-permute-start(bf16[3,105,16,128]{3,2,1,0:T(8,128)(2,1)} %get-tuple-element.26), channel_id=1, source_target_pairs={{0,127},{1,0},{2,1},{3,2},{4,3},{5,4},{6,5},{7,6},{8,7},{9,8},{10,... | collective-permute-start | bytes 3870728 | tf_op jit(solution)/shard_map/ppermute | solution.py:577
  14.7 0.0 collective-permute-start.1
  14.8 5.7 %collective-permute-start.3 = (bf16[3,66,16,128]{3,2,1,0:T(8,128)(2,1)}, bf16[3,66,16,128]{3,2,1,0:T(8,128)(2,1)}, u32[]{:S(2)}, u32[]{:S(2)}) collective-permute-start(bf16[3,66,16,128]{3,2,1,0:T(8,128)(2,1)} %get-tuple-element.27), channel_id=1, source_target_pairs={{0,127},{1,0},{2,1},{3,2},{4,3},{5,4},{6,5},{7,6},{8,7},{9,8},{10,... | collective-permute-start | bytes 2433032 | tf_op jit(solution)/shard_map/ppermute | solution.py:577
  21.1 26.2 %local.1 = (bf16[20,3,512,128]{3,2,1,0:T(8,128)(2,1)}, f32[72,512]{1,0:T(8,128)}, f32[1,512]{1,0:T(1,128)}, f32[64,128]{1,0:T(8,128)}) custom-call(s32[256]{0:T(256)} %lens_ref.3, f32[256]{0:T(256)} %step_ref.1, s32[8]{0:T(128)} %get-tuple-element.20.scal_ref.refs_0_, bf16[16,128]{1,0:T(8,128)(2,1)} %get-tuple-element.21.place_ref, ...), custom_call_target="tpu_custom_call" | custom-call | flops 2684354560 | bytes 15728640 | tf_op jit(solution)/shard_map/local/pallas_call | solution.py:623
  47.3 0.0 collective-permute-done.refs_6_
  47.3 0.0 copy-start
  47.3 0.0 collective-permute-done.2.refs_7_.refs_8_
  47.3 0.0 copy-start.1
  47.3 1.1 %copy-done = bf16[3,105,16,128]{3,2,1,0:T(8,128)(2,1)} copy-done((bf16[3,105,16,128]{3,2,1,0:T(8,128)(2,1)}, bf16[3,105,16,128]{3,2,1,0:T(8,128)(2,1)S(1)}, u32[]{:S(2)}) %copy-start) | copy-done | bytes 1290264
  48.4 0.4 copy-done.1
  48.8 17.8 %shard_map.118 = (f32[2,72,512]{2,1,0:T(8,128)}, f32[2,2,384,128]{3,2,1,0:T(8,128)}) custom-call(s32[8]{0:T(128)} %get-tuple-element.20.scal_ref.refs_0_, bf16[3,4,16,128]{3,2,1,0:T(8,128)(2,1)} %constant.4.clone.select_ref.refs_1_, bf16[256,256]{1,0:T(8,128)(2,1)} %constant.5.clone.turn_ref.refs_2_, bf16[64,2560]{1,0:T(8,128)(2,1)} %bitcast.18, ...), custom_call_target="tpu_custom_call" | custom-call | flops 1342177280 | bytes 4194304 | tf_op jit(solution)/shard_map/pallas_call | solution.py:684
  66.7 0.0 collective-permute-done.1.refs_7_
  66.7 0.0 copy-start.2
  66.7 0.0 collective-permute-done.3.refs_9_
  66.7 0.9 copy-done.2
  67.6 0.0 copy-start.3
  67.6 0.0 copy-start.4
  67.6 4.7 %shard_map.119 = (f32[72,512]{1,0:T(8,128)}, f32[72,384]{1,0:T(8,128)}, f32[72,384]{1,0:T(8,128)}) custom-call(s32[8]{0:T(128)} %get-tuple-element.20.scal_ref.refs_0_, bf16[3,4,16,128]{3,2,1,0:T(8,128)(2,1)} %constant.4.clone.select_ref.refs_1_, bf16[256,256]{1,0:T(8,128)(2,1)} %constant.5.clone.turn_ref.refs_2_, bf16[64,2560]{1,0:T(8,128)(2,1)} %bitcast.19, ...), custom_call_target="tpu_custom_call" | custom-call | flops 1342177280 | bytes 4194304 | tf_op jit(solution)/shard_map/pallas_call | solution.py:684
  72.3 29.5 %finish.1 = f32[32,512]{1,0:T(8,128)} custom-call(f32[72,512]{1,0:T(8,128)} %get-tuple-element.31.own_ref, f32[72,384]{1,0:T(8,128)} %get-tuple-element.32.left_ref, f32[72,384]{1,0:T(8,128)} %get-tuple-element.33.right_ref, f32[64,128]{1,0:T(8,128)} %get-tuple-element.34.shift_ref, f32[1]{0:T(128)S(6)} %copy.13.guide_ref), custom_call_target="tpu_custom_call" | custom-call | tf_op jit(solution)/shard_map/finish/pallas_call | solution.py:701
  101.8 0.0 copy-done.3
  101.8 0.0 copy-done.4
  101.8 1.5 %fusion = f32[512,32]{0,1:T(8,128)} fusion(f32[512,32]{0,1:T(8,128)S(1)} %copy-done.3, f32[32,512]{1,0:T(8,128)} %finish.1, f32[512]{0:T(512)S(1)} %bitcast.20), kind=kLoop, calls=%fused_computation.1 | loop fusion | flops 32768 | bytes 198656 | tf_op jit(solution)/shard_map/transpose | solution.py:717
Async XLA Ops:
  7.0 40.3 %collective-permute-start = (bf16[3,105,16,128]{3,2,1,0:T(8,128)(2,1)}, bf16[3,105,16,128]{3,2,1,0:T(8,128)(2,1)S(1)}, u32[]{:S(2)}, u32[]{:S(2)}) collective-permute-start(bf16[3,105,16,128]{3,2,1,0:T(8,128)(2,1)} %get-tuple-element.24), channel_id=1, source_target_pairs={{0,1},{1,2},{2,3},{3,4},{4,5},{5,6},{6,7},{7,8},{8,9},{9,10},{10,1... | collective-permute-start | bytes 3870728 | tf_op jit(solution)/shard_map/ppermute | solution.py:577
  8.3 39.0 %collective-permute-start.2 = (bf16[3,105,16,128]{3,2,1,0:T(8,128)(2,1)}, bf16[3,105,16,128]{3,2,1,0:T(8,128)(2,1)S(1)}, u32[]{:S(2)}, u32[]{:S(2)}) collective-permute-start(bf16[3,105,16,128]{3,2,1,0:T(8,128)(2,1)} %get-tuple-element.26), channel_id=1, source_target_pairs={{0,127},{1,0},{2,1},{3,2},{4,3},{5,4},{6,5},{7,6},{8,7},{9,8},{10,... | collective-permute-start | bytes 3870728 | tf_op jit(solution)/shard_map/ppermute | solution.py:577
  14.7 51.9 %collective-permute-start.1 = (bf16[3,66,16,128]{3,2,1,0:T(8,128)(2,1)}, bf16[3,66,16,128]{3,2,1,0:T(8,128)(2,1)S(1)}, u32[]{:S(2)}, u32[]{:S(2)}) collective-permute-start(bf16[3,66,16,128]{3,2,1,0:T(8,128)(2,1)} %get-tuple-element.25), channel_id=1, source_target_pairs={{0,1},{1,2},{2,3},{3,4},{4,5},{5,6},{6,7},{7,8},{8,9},{9,10},{10,1... | collective-permute-start | bytes 2433032 | tf_op jit(solution)/shard_map/ppermute | solution.py:577
  14.8 51.9 %collective-permute-start.3 = (bf16[3,66,16,128]{3,2,1,0:T(8,128)(2,1)}, bf16[3,66,16,128]{3,2,1,0:T(8,128)(2,1)}, u32[]{:S(2)}, u32[]{:S(2)}) collective-permute-start(bf16[3,66,16,128]{3,2,1,0:T(8,128)(2,1)} %get-tuple-element.27), channel_id=1, source_target_pairs={{0,127},{1,0},{2,1},{3,2},{4,3},{5,4},{6,5},{7,6},{8,7},{9,8},{10,... | collective-permute-start | bytes 2433032 | tf_op jit(solution)/shard_map/ppermute | solution.py:577
  47.3 1.1 %copy-start = (bf16[3,105,16,128]{3,2,1,0:T(8,128)(2,1)}, bf16[3,105,16,128]{3,2,1,0:T(8,128)(2,1)S(1)}, u32[]{:S(2)}) copy-start(bf16[3,105,16,128]{3,2,1,0:T(8,128)(2,1)S(1)} %collective-permute-done.refs_6_) | copy-start | bytes 3870724
  47.3 1.5 %copy-start.1 = (bf16[3,105,16,128]{3,2,1,0:T(8,128)(2,1)}, bf16[3,105,16,128]{3,2,1,0:T(8,128)(2,1)S(1)}, u32[]{:S(2)}) copy-start(bf16[3,105,16,128]{3,2,1,0:T(8,128)(2,1)S(1)} %collective-permute-done.2.refs_7_.refs_8_) | copy-start | bytes 3870724
  66.7 0.9 copy-start.2
  67.6 34.2 %copy-start.3 = (f32[512,32]{0,1:T(8,128)S(1)}, f32[512,32]{0,1:T(8,128)}, u32[]{:S(2)}) copy-start(f32[512,32]{0,1:T(8,128)} %param.16) | copy-start | bytes 196612
  67.6 34.2 %copy-start.4 = (f32[1,512]{1,0:T(1,128)S(1)}, f32[1,512]{1,0:T(1,128)}, u32[]{:S(2)}) copy-start(f32[1,512]{1,0:T(1,128)} %get-tuple-element.22) | copy-start | bytes 6148

commit v5 on v4

--- a/solution.py
+++ b/solution.py
@@ -19,7 +19,8 @@
 REACH = FAR * TILE
 SPAN = 2 * ROWS + 128
 ACCR = 72
-CHUNKS = (104,)
+CHUNKS = (56, 60)
+ROOM = 28 << 20
 masked_score = -1e30
 score_scale = math.log2(math.e) / math.sqrt(HD)
 rope_theta = 10000.0
@@ -197,6 +198,23 @@
         copy.wait()
 
 
+def cos_sin(angle):
+    turns = jnp.floor(angle * (2.0 / math.pi) + 0.5)
+    rest = angle - turns * 1.5703125
+    rest = rest - turns * 4.837512969970703125e-4
+    rest = rest - turns * 7.54978995489188216e-8
+    square = rest * rest
+    sine = (-1.9515295891e-4 * square + 8.3321608736e-3) * square - 1.6666654611e-1
+    sine = sine * square * rest + rest
+    cosine = (2.443315711809948e-5 * square - 1.388731625493765e-3) * square
+    cosine = (cosine + 4.166664568298827e-2) * square * square - 0.5 * square + 1.0
+    quadrant = turns.astype(jnp.int32)
+    odd = (quadrant & 1) == 1
+    first, second = jnp.where(odd, sine, cosine), jnp.where(odd, cosine, sine)
+    first = jnp.where(((quadrant + 1) & 2) == 2, -first, first)
+    return first, jnp.where((quadrant & 2) == 2, -second, second)
+
+
 def tables(place, select_ref, groups):
     parts = []
     for group in groups:
@@ -211,7 +229,7 @@
             angle = term if angle is None else angle + term
         parts.append(angle)
     angle = jnp.concatenate(parts, axis=0)
-    return jnp.cos(angle), jnp.sin(angle)
+    return cos_sin(angle)
 
 
 def rotate(q, k, cosine, sine, turn):
@@ -249,19 +267,8 @@
 def local_kernel(
     heads, lens_ref, step_ref, scal_ref, place_ref, select_ref, turn_ref, w_ref, mod_ref,
     q_ref, k_ref, v_ref, turned_ref, acc_ref, steps_ref, shift_ref,
-    rows_in, cos_ref, sin_ref, bias_ref, mine, in_sem, out_sem,
+    cos_ref, sin_ref, bias_ref, mine, out_sem,
 ):
-    groups = 4 if heads % 4 == 0 else 1
-    width = heads // groups * HD
-    loads = []
-    for group in range(groups):
-        columns = pl.ds(group * width, width)
-        for j, source in enumerate((q_ref, k_ref, v_ref)):
-            copy = pltpu.make_async_copy(
-                source.at[:, :, columns], rows_in.at[j, :, :, columns], in_sem.at[group, j]
-            )
-            copy.start()
-            loads.append(copy)
     low = lax.axis_index("req") * ROWS
     lane = lax.broadcasted_iota(jnp.int32, (1, ROWS), 1) + low
 
@@ -292,8 +299,6 @@
     shift = jnp.sum(w_ref[...].astype(jnp.float32) * mod_ref[0:1, :], axis=1, keepdims=True)
     shift_ref[...] = jnp.broadcast_to(shift, (LATC, HD))
     turn = turn_ref[...]
-    for copy in loads:
-        copy.wait()
     first = scal_ref[1]
     last = ROWS - scal_ref[3]
     begin = pl.multiple_of(first // HD * HD, HD)
@@ -310,12 +315,12 @@
         def _():
             keep(head, slot).wait()
 
-        q = rows_in[0, :, :, columns].reshape(ROWS, HD)
-        k = rows_in[1, :, :, columns].reshape(ROWS, HD)
+        q = q_ref[:, columns]
+        k = k_ref[:, columns]
         q, k = rotate(q, k, cos_ref[...], sin_ref[...], turn)
         mine[slot, 0] = q.astype(jnp.bfloat16)
         mine[slot, 1] = k.astype(jnp.bfloat16)
-        mine[slot, 2] = rows_in[2, :, :, columns].reshape(ROWS, HD)
+        mine[slot, 2] = v_ref[:, columns]
         keep(head, slot).start()
         for width in (128, 256, 384, 512):
 
@@ -628,24 +633,23 @@
             sized((1, ROWS), f32),
             sized((LATC, HD), f32),
         ],
-        in_specs=[SMEM, SMEM, SMEM] + [VMEM] * 5 + [ANY] * 3,
+        in_specs=[SMEM, SMEM, SMEM] + [VMEM] * 8,
         out_specs=[ANY, VMEM, VMEM, VMEM],
         scratch_shapes=[
-            pltpu.VMEM((3, TILES, TILE, features), bf16),
             pltpu.VMEM((ROWS, HD), f32),
             pltpu.VMEM((ROWS, HD), f32),
             pltpu.VMEM((ROWS, ROWS), f32),
             pltpu.VMEM((2, 3, ROWS, HD), bf16),
-            pltpu.SemaphoreType.DMA((4, 3)),
             pltpu.SemaphoreType.DMA((2,)),
         ],
         cost_estimate=pl.CostEstimate(
             flops=heads * pair_ops, bytes_accessed=6 * ROWS * features * 2, transcendentals=0
         ),
+        compiler_params=pltpu.CompilerParams(vmem_limit_bytes=ROOM),
         name="local",
     )(
         lengths, step_sizes, scal, place, select, turn, w_turned, modulation,
-        tiled(q), tiled(k), tiled(v),
+        q, k, v,
     )
 
     acc = table = None
@@ -690,6 +694,7 @@
             cost_estimate=pl.CostEstimate(
                 flops=heads * pair_ops // count, bytes_accessed=4 << 20, transcendentals=0
             ),
+            compiler_params=pltpu.CompilerParams(vmem_limit_bytes=ROOM),
         )(*operands)
         if final:
             own, back_left, back_right = results

time: 105 us -> 111 us (1.057); the launches traced: 103 us -> 111 us
  waiting for transfers between devices: 0.01 us -> 9.85 us
  Pallas kernels: 85.1 us -> 77.3 us
  local copies, waits for them, and re-layouts: 2.43 us -> 6.75 us
    ppermute x4 -> x6, waiting for transfers between devices: 0.01 us -> 9.85 us  [moved(): lax.ppermute(value, 'req', [(i, (i + step) % ring) for i in range(ring)])]
    pallas_call x2 -> x3, Pallas kernels: 22.5 us -> 17.4 us  [per_device(): pl.pallas_call(functools.partial(cut_kernel, heads, chunks, c), out_shape...]
    unnamed x10 -> x34, local copies, waits for them, and re-layouts: 2.43 us -> 6.75 us
    pallas_call x1, Pallas kernels: 29.5 us -> 25.3 us  [per_device(): pl.pallas_call(functools.partial(finish_kernel, features, ring), out_shap...]
    ppermute x4 -> x6, starting transfers between devices: 13.5 us -> 14.6 us  [moved(): lax.ppermute(value, 'req', [(i, (i + step) % ring) for i in range(ring)])]
  transfers between devices with their start and end apart: 4 -> 6, of which waited for: 0 -> 1; matrix products, arithmetic and copies ran while one was open for 0% -> 0% of each run, Pallas kernels for 43% -> 39%
where the time goes in v5:
time: 111 us
  Pallas kernels  77.3 us (70%)
  starting transfers between devices  14.6 us (13%)
  waiting for transfers between devices  9.85 us (9%)
  local copies, waits for them, and re-layouts  6.75 us (6%)
  other arithmetic  1.49 us (1%)
    pallas_call x1, Pallas kernels, per_device(): pl.pallas_call(functools.partial(local_kernel, heads), out_shape=[sized((...  27.3 us
    pallas_call x1, Pallas kernels, per_device(): pl.pallas_call(functools.partial(finish_kernel, features, ring), out_shap...  25.3 us
    pallas_call x3, Pallas kernels, per_device(): pl.pallas_call(functools.partial(cut_kernel, heads, chunks, c), out_shape...  17.4 us
    ppermute x6, starting transfers between devices, moved(): lax.ppermute(value, 'req', [(i, (i + step) % ring) for i in range(ring)])  14.6 us
    ppermute x6, waiting for transfers between devices, moved(): lax.ppermute(value, 'req', [(i, (i + step) % ring) for i in range(ring)])  9.85 us
    pallas_call x1, Pallas kernels, per_device(): pl.pallas_call(functools.partial(pack_kernel, heads, chunks), out_shape=[...  7.24 us
    unnamed x34, local copies, waits for them, and re-layouts  6.75 us
  transfers between devices with their start and end apart: 6, of which 1 were waited for; matrix products, arithmetic and copies ran while one was open for 0% of the time, Pallas kernels for 39%

profile of v5, /device:TPU:17, one launch (start us, length us, event | category | flops | bytes accessed | tf_op | source)
XLA Modules:
  0.0 110.9 jit_solution(8455886486862964562)
XLA Ops:
  0.0 0.0 copy-start.5
  0.1 7.2 %pack.1 = (s32[8]{0:T(128)}, bf16[16,128]{1,0:T(8,128)(2,1)}, bf16[3,57,16,128]{3,2,1,0:T(8,128)(2,1)}, bf16[3,60,16,128]{3,2,1,0:T(8,128)(2,1)}, bf16[3,54,16,1...) custom-call(s32[256]{0:T(256)} %lens_ref.3, ...), custom_call_target="tpu_custom_call" | custom-call | tf_op jit(solution)/shard_map/pack/pallas_call | solution.py:603
  7.3 1.3 %collective-permute-start.4 = (bf16[3,57,16,128]{3,2,1,0:T(8,128)(2,1)}, bf16[3,57,16,128]{3,2,1,0:T(8,128)(2,1)S(1)}, u32[]{:S(2)}, u32[]{:S(2)}) collective-permute-start(bf16[3,57,16,128]{3,2,1,0:T(8,128)(2,1)} %get-tuple-element.30), channel_id=1, source_target_pairs={{0,1},{1,2},{2,3},{3,4},{4,5},{5,6},{6,7},{7,8},{8,9},{9,10},{10,1... | collective-permute-start | bytes 2101256 | tf_op jit(solution)/shard_map/ppermute | solution.py:582
  8.6 6.5 %collective-permute-start.5 = (bf16[3,57,16,128]{3,2,1,0:T(8,128)(2,1)}, bf16[3,57,16,128]{3,2,1,0:T(8,128)(2,1)S(1)}, u32[]{:S(2)}, u32[]{:S(2)}) collective-permute-start(bf16[3,57,16,128]{3,2,1,0:T(8,128)(2,1)} %get-tuple-element.31), channel_id=1, source_target_pairs={{0,127},{1,0},{2,1},{3,2},{4,3},{5,4},{6,5},{7,6},{8,7},{9,8},{10,... | collective-permute-start | bytes 2101256 | tf_op jit(solution)/shard_map/ppermute | solution.py:582
  15.1 0.0 collective-permute-start
  15.1 5.7 %collective-permute-start.2 = (bf16[3,60,16,128]{3,2,1,0:T(8,128)(2,1)}, bf16[3,60,16,128]{3,2,1,0:T(8,128)(2,1)S(1)}, u32[]{:S(2)}, u32[]{:S(2)}) collective-permute-start(bf16[3,60,16,128]{3,2,1,0:T(8,128)(2,1)} %get-tuple-element.28), channel_id=1, source_target_pairs={{0,127},{1,0},{2,1},{3,2},{4,3},{5,4},{6,5},{7,6},{8,7},{9,8},{10,... | collective-permute-start | bytes 2211848 | tf_op jit(solution)/shard_map/ppermute | solution.py:582
  20.8 9.8 %collective-permute-done.4.refs_6_ = bf16[3,57,16,128]{3,2,1,0:T(8,128)(2,1)S(1)} collective-permute-done((bf16[3,57,16,128]{3,2,1,0:T(8,128)(2,1)}, bf16[3,57,16,128]{3,2,1,0:T(8,128)(2,1)S(1)}, u32[]{:S(2)}, u32[]{:S(2)}) %collective-permute-start.4) | collective-permute-done | bytes 700448 | tf_op jit(solution)/shard_map/ppermute | solution.py:582
  30.6 1.2 %collective-permute-start.3 = (bf16[3,54,16,128]{3,2,1,0:T(8,128)(2,1)}, bf16[3,54,16,128]{3,2,1,0:T(8,128)(2,1)S(1)}, u32[]{:S(2)}, u32[]{:S(2)}) collective-permute-start(bf16[3,54,16,128]{3,2,1,0:T(8,128)(2,1)} %get-tuple-element.29), channel_id=1, source_target_pairs={{0,127},{1,0},{2,1},{3,2},{4,3},{5,4},{6,5},{7,6},{8,7},{9,8},{10,... | collective-permute-start | bytes 1990664 | tf_op jit(solution)/shard_map/ppermute | solution.py:582
  32.5 0.0 copy-start.2
  32.5 1.7 %copy-done.2 = bf16[1,512,2560]{2,1,0:T(8,128)(2,1)S(1)} copy-done((bf16[1,512,2560]{2,1,0:T(8,128)(2,1)S(1)}, bf16[1,512,2560]{2,1,0:T(8,128)(2,1)}, u32[]{:S(2)}) %copy-start.2) | copy-done | bytes 2621464
  34.2 1.7 %copy-done.3 = bf16[1,512,2560]{2,1,0:T(8,128)(2,1)S(1)} copy-done((bf16[1,512,2560]{2,1,0:T(8,128)(2,1)S(1)}, bf16[1,512,2560]{2,1,0:T(8,128)(2,1)}, u32[]{:S(2)}) %copy-start.3) | copy-done | bytes 2621464
  36.0 0.6 copy-done.11
  36.6 0.7 copy-done.14
  37.3 27.3 %local.1 = (bf16[20,3,512,128]{3,2,1,0:T(8,128)(2,1)S(1)}, f32[72,512]{1,0:T(8,128)S(1)}, f32[1,512]{1,0:T(1,128)S(1)}, f32[64,128]{1,0:T(8,128)S(1)}) custom-call(s32[256]{0:T(256)S(1)} %copy-done.13, f32[256]{0:T(256)S(1)} %copy-done.15, s32[8]{0:T(128)S(1)} %copy-done.11, bf16[16,128]{1,0:T(8,128)(2,1)S(1)} %copy-done.14, ...), custom_call_target="tpu_custom_call" | custom-call | flops 2684354560 | bytes 15728640 | tf_op jit(solution)/shard_map/local/pallas_call | solution.py:628
  64.6 0.0 copy-start.10
  64.6 13.2 %shard_map.118 = (f32[2,72,512]{2,1,0:T(8,128)S(1)}, f32[2,2,384,128]{3,2,1,0:T(8,128)S(1)}) custom-call(s32[8]{0:T(128)S(1)} %copy-done.12, bf16[3,4,16,128]{3,2,1,0:T(8,128)(2,1)S(1)} %copy-done.5, bf16[256,256]{1,0:T(8,128)(2,1)S(1)} %copy-done.4, bf16[64,2560]{1,0:T(8,128)(2,1)S(1)} %bitcast.15, f32[2,2560]{1,0:T(2,128)S(1)} %copy-done.6, ...), custom_call_target="tpu_custom_call" | custom-call | flops 894784832 | bytes 4194304 | tf_op jit(solution)/shard_map/pallas_call | solution.py:688
  77.9 2.5 %shard_map.119.refs_11_ = f32[2,72,512]{2,1,0:T(8,128)S(1)} custom-call(s32[8]{0:T(128)S(1)} %copy-done.12, bf16[3,4,16,128]{3,2,1,0:T(8,128)(2,1)S(1)} %copy-done.5, bf16[256,256]{1,0:T(8,128)(2,1)S(1)} %copy-done.4, bf16[64,2560]{1,0:T(8,128)(2,1)S(1)} %bitcast.16, f32[2,2560]{1,0:T(2,128)S(1)} %copy-done.6, ...), custom_call_target="tpu_custom_call" | custom-call | flops 894784832 | bytes 4194304 | tf_op jit(solution)/shard_map/pallas_call | solution.py:688
  80.4 0.0 copy-start.16
  80.4 1.7 %shard_map.120 = (f32[72,512]{1,0:T(8,128)S(1)}, f32[72,384]{1,0:T(8,128)S(1)}, f32[72,384]{1,0:T(8,128)S(1)}) custom-call(s32[8]{0:T(128)S(1)} %copy-done.12, bf16[3,4,16,128]{3,2,1,0:T(8,128)(2,1)S(1)} %copy-done.5, bf16[256,256]{1,0:T(8,128)(2,1)S(1)} %copy-done.4, bf16[64,2560]{1,0:T(8,128)(2,1)S(1)} %bitcast.17, f32[2,2560]{1,0:T(2,128)S(1)} %copy-done.6, ...), custom_call_target="tpu_custom_call" | custom-call | flops 894784832 | bytes 4194304 | tf_op jit(solution)/shard_map/pallas_call | solution.py:688
  82.1 0.6 copy-done.7
  82.8 0.6 copy-done.8
  83.4 0.6 copy-done.9
  84.1 25.3 %finish.1 = f32[32,512]{1,0:T(8,128)} custom-call(f32[72,512]{1,0:T(8,128)} %copy-done.7, f32[72,384]{1,0:T(8,128)} %copy-done.8, f32[72,384]{1,0:T(8,128)} %copy-done.9, f32[64,128]{1,0:T(8,128)} %copy-done.10, f32[1]{0:T(128)S(6)} %copy.13.guide_ref), custom_call_target="tpu_custom_call" | custom-call | tf_op jit(solution)/shard_map/finish/pallas_call | solution.py:706
  109.4 1.5 %fusion = f32[512,32]{0,1:T(8,128)} fusion(f32[512,32]{0,1:T(8,128)S(1)} %copy-done.16, f32[32,512]{1,0:T(8,128)} %finish.1, f32[512]{0:T(512)S(1)} %bitcast.24), kind=kLoop, calls=%fused_computation.1 | loop fusion | flops 32768 | bytes 198656 | tf_op jit(solution)/shard_map/transpose | solution.py:722
  (29 shorter events, 0.1 us)
Async XLA Ops:
  0.0 32.4 %copy-start = (bf16[2560,64]{0,1:T(8,128)(2,1)S(1)}, bf16[2560,64]{0,1:T(8,128)(2,1)}, u32[]{:S(2)}) copy-start(bf16[2560,64]{0,1:T(8,128)(2,1)} %param.17) | copy-start | bytes 983044
  0.0 32.4 %copy-start.1 = (bf16[1,512,2560]{2,1,0:T(8,128)(2,1)S(1)}, bf16[1,512,2560]{2,1,0:T(8,128)(2,1)}, u32[]{:S(2)}) copy-start(bf16[1,512,2560]{2,1,0:T(8,128)(2,1)} %param.12) | copy-start | bytes 7864324
  0.0 32.4 %copy-start.4 = (bf16[256,256]{1,0:T(8,128)(2,1)S(1)}, bf16[256,256]{1,0:T(8,128)(2,1)}, u32[]{:S(2)}) copy-start(bf16[256,256]{1,0:T(8,128)(2,1)} %constant.5.clone.turn_ref.refs_2_) | copy-start | bytes 393220
  0.0 32.4 %copy-start.5 = (bf16[3,4,16,128]{3,2,1,0:T(8,128)(2,1)S(1)}, bf16[3,4,16,128]{3,2,1,0:T(8,128)(2,1)}, u32[]{:S(2)}) copy-start(bf16[3,4,16,128]{3,2,1,0:T(8,128)(2,1)} %constant.4.clone.select_ref.refs_1_) | copy-start | bytes 147460
  0.0 32.4 %copy-start.6 = (f32[2,2560]{1,0:T(2,128)S(1)}, f32[2,2560]{1,0:T(2,128)}, u32[]{:S(2)}) copy-start(f32[2,2560]{1,0:T(2,128)} %refs_4_.5) | copy-start | bytes 61444
  0.0 32.4 %copy-start.13 = (s32[256]{0:T(256)S(1)}, s32[256]{0:T(256)}, u32[]{:S(2)}) copy-start(s32[256]{0:T(256)} %lens_ref.3) | copy-start | bytes 3076
  0.0 32.4 %copy-start.15 = (f32[256]{0:T(256)S(1)}, f32[256]{0:T(256)}, u32[]{:S(2)}) copy-start(f32[256]{0:T(256)} %step_ref.1) | copy-start | bytes 3076
  7.3 23.3 %collective-permute-start.4 = (bf16[3,57,16,128]{3,2,1,0:T(8,128)(2,1)}, bf16[3,57,16,128]{3,2,1,0:T(8,128)(2,1)S(1)}, u32[]{:S(2)}, u32[]{:S(2)}) collective-permute-start(bf16[3,57,16,128]{3,2,1,0:T(8,128)(2,1)} %get-tuple-element.30), channel_id=1, source_target_pairs={{0,1},{1,2},{2,3},{3,4},{4,5},{5,6},{6,7},{7,8},{8,9},{9,10},{10,1... | collective-permute-start | bytes 2101256 | tf_op jit(solution)/shard_map/ppermute | solution.py:582
  8.6 56.0 %collective-permute-start.5 = (bf16[3,57,16,128]{3,2,1,0:T(8,128)(2,1)}, bf16[3,57,16,128]{3,2,1,0:T(8,128)(2,1)S(1)}, u32[]{:S(2)}, u32[]{:S(2)}) collective-permute-start(bf16[3,57,16,128]{3,2,1,0:T(8,128)(2,1)} %get-tuple-element.31), channel_id=1, source_target_pairs={{0,127},{1,0},{2,1},{3,2},{4,3},{5,4},{6,5},{7,6},{8,7},{9,8},{10,... | collective-permute-start | bytes 2101256 | tf_op jit(solution)/shard_map/ppermute | solution.py:582
  15.1 62.8 %collective-permute-start = (bf16[3,60,16,128]{3,2,1,0:T(8,128)(2,1)}, bf16[3,60,16,128]{3,2,1,0:T(8,128)(2,1)S(1)}, u32[]{:S(2)}, u32[]{:S(2)}) collective-permute-start(bf16[3,60,16,128]{3,2,1,0:T(8,128)(2,1)} %get-tuple-element.26), channel_id=1, source_target_pairs={{0,1},{1,2},{2,3},{3,4},{4,5},{5,6},{6,7},{7,8},{8,9},{9,10},{10,1... | collective-permute-start | bytes 2211848 | tf_op jit(solution)/shard_map/ppermute | solution.py:582
  15.1 62.8 %collective-permute-start.2 = (bf16[3,60,16,128]{3,2,1,0:T(8,128)(2,1)}, bf16[3,60,16,128]{3,2,1,0:T(8,128)(2,1)S(1)}, u32[]{:S(2)}, u32[]{:S(2)}) collective-permute-start(bf16[3,60,16,128]{3,2,1,0:T(8,128)(2,1)} %get-tuple-element.28), channel_id=1, source_target_pairs={{0,127},{1,0},{2,1},{3,2},{4,3},{5,4},{6,5},{7,6},{8,7},{9,8},{10,... | collective-permute-start | bytes 2211848 | tf_op jit(solution)/shard_map/ppermute | solution.py:582
  20.8 59.6 %collective-permute-start.1 = (bf16[3,54,16,128]{3,2,1,0:T(8,128)(2,1)}, bf16[3,54,16,128]{3,2,1,0:T(8,128)(2,1)S(1)}, u32[]{:S(2)}, u32[]{:S(2)}) collective-permute-start(bf16[3,54,16,128]{3,2,1,0:T(8,128)(2,1)} %get-tuple-element.27), channel_id=1, source_target_pairs={{0,1},{1,2},{2,3},{3,4},{4,5},{5,6},{6,7},{7,8},{8,9},{9,10},{10,1... | collective-permute-start | bytes 1990664 | tf_op jit(solution)/shard_map/ppermute | solution.py:582
  30.6 49.8 %collective-permute-start.3 = (bf16[3,54,16,128]{3,2,1,0:T(8,128)(2,1)}, bf16[3,54,16,128]{3,2,1,0:T(8,128)(2,1)S(1)}, u32[]{:S(2)}, u32[]{:S(2)}) collective-permute-start(bf16[3,54,16,128]{3,2,1,0:T(8,128)(2,1)} %get-tuple-element.29), channel_id=1, source_target_pairs={{0,127},{1,0},{2,1},{3,2},{4,3},{5,4},{6,5},{7,6},{8,7},{9,8},{10,... | collective-permute-start | bytes 1990664 | tf_op jit(solution)/shard_map/ppermute | solution.py:582
  32.5 1.7 %copy-start.2 = (bf16[1,512,2560]{2,1,0:T(8,128)(2,1)S(1)}, bf16[1,512,2560]{2,1,0:T(8,128)(2,1)}, u32[]{:S(2)}) copy-start(bf16[1,512,2560]{2,1,0:T(8,128)(2,1)} %param.13) | copy-start | bytes 7864324
  34.2 1.7 %copy-start.3 = (bf16[1,512,2560]{2,1,0:T(8,128)(2,1)S(1)}, bf16[1,512,2560]{2,1,0:T(8,128)(2,1)}, u32[]{:S(2)}) copy-start(bf16[1,512,2560]{2,1,0:T(8,128)(2,1)} %param.14) | copy-start | bytes 7864324
  36.0 0.6 copy-start.11
  36.6 0.7 copy-start.14
  37.3 27.3 %copy-start.12 = (s32[8]{0:T(128)S(1)}, s32[8]{0:T(128)}, u32[]{:S(2)}) copy-start(s32[8]{0:T(128)} %get-tuple-element.22.scal_ref.refs_0_) | copy-start | bytes 100
  64.6 13.2 %copy-start.10 = (f32[64,128]{1,0:T(8,128)}, f32[64,128]{1,0:T(8,128)S(1)}, u32[]{:S(2)}) copy-start(f32[64,128]{1,0:T(8,128)S(1)} %get-tuple-element.38.shift_ref) | copy-start | bytes 98308
  80.4 29.0 %copy-start.16 = (f32[512,32]{0,1:T(8,128)S(1)}, f32[512,32]{0,1:T(8,128)}, u32[]{:S(2)}) copy-start(f32[512,32]{0,1:T(8,128)} %param.16) | copy-start | bytes 196612
  82.1 0.7 copy-start.7
  82.8 0.6 copy-start.8
  83.4 0.6 copy-start.9

commit v6 on v5

--- a/solution.py
+++ b/solution.py
@@ -19,7 +19,7 @@
 REACH = FAR * TILE
 SPAN = 2 * ROWS + 128
 ACCR = 72
-CHUNKS = (56, 60)
+CHUNKS = (80,)
 ROOM = 28 << 20
 masked_score = -1e30
 score_scale = math.log2(math.e) / math.sqrt(HD)
@@ -611,6 +611,7 @@
             pltpu.SemaphoreType.DMA((4, 3)),
             pltpu.SemaphoreType.DMA((2, count + 1)),
         ],
+        compiler_params=pltpu.CompilerParams(vmem_limit_bytes=56 << 20),
         name="pack",
     )(lengths, positions, tiled(q), tiled(k), tiled(v))
     scal, place = outs[:2]
@@ -716,7 +717,9 @@
             pltpu.SemaphoreType.DMA((3,)),
             pltpu.SemaphoreType.DMA((3,)),
         ],
-        compiler_params=pltpu.CompilerParams(collective_id=0, has_side_effects=True),
+        compiler_params=pltpu.CompilerParams(
+            collective_id=0, has_side_effects=True, vmem_limit_bytes=ROOM
+        ),
         name="finish",
     )(own, back_left, back_right, shift, guide_scale)
     return (latents.T + steps * guided).T

time: 111 us -> 91.4 us (0.82)
  waiting for transfers between devices: 9.85 us -> 0.01 us
  Pallas kernels: 77.3 us -> 72.2 us
  local copies, waits for them, and re-layouts: 6.75 us -> 4.05 us
    ppermute x6 -> x4, waiting for transfers between devices: 9.85 us -> 0.01 us  [moved(): lax.ppermute(value, 'req', [(i, (i + step) % ring) for i in range(ring)])]
    pallas_call x1, Pallas kernels: 25.3 us -> 21.5 us  [per_device(): pl.pallas_call(functools.partial(finish_kernel, features, ring), out_shap...]
    unnamed x34 -> x24, local copies, waits for them, and re-layouts: 6.75 us -> 4.05 us
    pallas_call x3 -> x2, Pallas kernels: 17.4 us -> 16 us  [per_device(): pl.pallas_call(functools.partial(cut_kernel, heads, chunks, c), out_shape...]
    ppermute x6 -> x4, starting transfers between devices: 14.6 us -> 13.5 us  [moved(): lax.ppermute(value, 'req', [(i, (i + step) % ring) for i in range(ring)])]
  transfers between devices with their start and end apart: 6 -> 4, of which waited for: 1 -> 0; matrix products, arithmetic and copies ran while one was open for 0% -> 0% of each run, Pallas kernels for 39% -> 45%
where the time goes in v6:
time: 91.4 us; the launch traced here: 91.2 us
  Pallas kernels  72.2 us (79%)
  starting transfers between devices  13.5 us (15%)
  local copies, waits for them, and re-layouts  4.05 us (4%)
    pallas_call x1, Pallas kernels, per_device(): pl.pallas_call(functools.partial(local_kernel, heads), out_shape=[sized((...  27.1 us
    pallas_call x1, Pallas kernels, per_device(): pl.pallas_call(functools.partial(finish_kernel, features, ring), out_shap...  21.5 us
    pallas_call x2, Pallas kernels, per_device(): pl.pallas_call(functools.partial(cut_kernel, heads, chunks, c), out_shape...  16 us
    ppermute x4, starting transfers between devices, moved(): lax.ppermute(value, 'req', [(i, (i + step) % ring) for i in range(ring)])  13.5 us
    pallas_call x1, Pallas kernels, per_device(): pl.pallas_call(functools.partial(pack_kernel, heads, chunks), out_shape=[...  7.58 us
    unnamed x24, local copies, waits for them, and re-layouts  4.05 us
  transfers between devices with their start and end apart: 4, of which 0 were waited for; matrix products, arithmetic and copies ran while one was open for 0% of the time, Pallas kernels for 45%

profile of v6, /device:TPU:17, one launch (start us, length us, event | category | flops | bytes accessed | tf_op | source)
XLA Modules:
  0.0 91.2 jit_solution(12776728236977572362)
XLA Ops:
  0.0 0.0 copy-start.6
  0.0 0.0 copy-start.8
  0.0 0.0 copy-start.10
  0.0 7.6 %pack.1 = (s32[8]{0:T(128)}, bf16[16,128]{1,0:T(8,128)(2,1)}, bf16[3,81,16,128]{3,2,1,0:T(8,128)(2,1)}, bf16[3,90,16,128]{3,2,1,0:T(8,128)(2,1)}, bf16[3,81,16,1...) custom-call(s32[256]{0:T(256)} %lens_ref.3, s32[3,512]{1,0:T(4,128)} %pos_ref.1, bf16[32,16,2560]{2,1,0:T(8,128)(2,1)} %bitcast.14, ...), custom_call_target="tpu_custom_call" | custom-call | tf_op jit(solution)/shard_map/pack/pallas_call | solution.py:603
  7.6 1.3 %collective-permute-start = (bf16[3,81,16,128]{3,2,1,0:T(8,128)(2,1)}, bf16[3,81,16,128]{3,2,1,0:T(8,128)(2,1)S(1)}, u32[]{:S(2)}, u32[]{:S(2)}) collective-permute-start(bf16[3,81,16,128]{3,2,1,0:T(8,128)(2,1)} %get-tuple-element.24), channel_id=1, source_target_pairs={{0,1},{1,2},{2,3},{3,4},{4,5},{5,6},{6,7},{7,8},{8,9},{9,10},{10,1... | collective-permute-start | bytes 2985992 | tf_op jit(solution)/shard_map/ppermute | solution.py:582
  8.9 6.5 %collective-permute-start.2 = (bf16[3,81,16,128]{3,2,1,0:T(8,128)(2,1)}, bf16[3,81,16,128]{3,2,1,0:T(8,128)(2,1)S(1)}, u32[]{:S(2)}, u32[]{:S(2)}) collective-permute-start(bf16[3,81,16,128]{3,2,1,0:T(8,128)(2,1)} %get-tuple-element.26), channel_id=1, source_target_pairs={{0,127},{1,0},{2,1},{3,2},{4,3},{5,4},{6,5},{7,6},{8,7},{9,8},{10,... | collective-permute-start | bytes 2985992 | tf_op jit(solution)/shard_map/ppermute | solution.py:582
  15.4 0.0 collective-permute-start.1
  15.4 5.7 %collective-permute-start.3 = (bf16[3,90,16,128]{3,2,1,0:T(8,128)(2,1)}, bf16[3,90,16,128]{3,2,1,0:T(8,128)(2,1)S(1)}, u32[]{:S(2)}, u32[]{:S(2)}) collective-permute-start(bf16[3,90,16,128]{3,2,1,0:T(8,128)(2,1)} %get-tuple-element.27), channel_id=1, source_target_pairs={{0,127},{1,0},{2,1},{3,2},{4,3},{5,4},{6,5},{7,6},{8,7},{9,8},{10,... | collective-permute-start | bytes 3317768 | tf_op jit(solution)/shard_map/ppermute | solution.py:582
  21.8 0.0 copy-start.3
  21.8 1.0 %copy-done.3 = bf16[2560,64]{0,1:T(8,128)(2,1)S(1)} copy-done((bf16[2560,64]{0,1:T(8,128)(2,1)S(1)}, bf16[2560,64]{0,1:T(8,128)(2,1)}, u32[]{:S(2)}) %copy-start.3) | copy-done | bytes 327704
  22.8 0.9 copy-done.4
  23.7 0.8 copy-done.5
  24.5 0.7 copy-done.7
  25.1 0.7 copy-done.9
  25.8 27.1 %local.1 = (bf16[20,3,512,128]{3,2,1,0:T(8,128)(2,1)S(1)}, f32[72,512]{1,0:T(8,128)S(1)}, f32[1,512]{1,0:T(1,128)S(1)}, f32[64,128]{1,0:T(8,128)S(1)}) custom-call(s32[256]{0:T(256)S(1)} %copy-done.8, f32[256]{0:T(256)S(1)} %copy-done.10, s32[8]{0:T(128)S(1)} %copy-done.7, bf16[16,128]{1,0:T(8,128)(2,1)S(1)} %copy-done.9, ...), custom_call_target="tpu_custom_call" | custom-call | flops 2684354560 | bytes 15728640 | tf_op jit(solution)/shard_map/local/pallas_call | solution.py:629
  53.0 0.0 collective-permute-done.refs_6_
  53.0 0.0 collective-permute-done.2.refs_7_.refs_8_
  53.0 14.1 %shard_map.118 = (f32[2,72,512]{2,1,0:T(8,128)S(1)}, f32[2,2,384,128]{3,2,1,0:T(8,128)S(1)}) custom-call(s32[8]{0:T(128)S(1)} %copy-done.7, bf16[3,4,16,128]{3,2,1,0:T(8,128)(2,1)S(1)} %copy-done.5, bf16[256,256]{1,0:T(8,128)(2,1)S(1)} %copy-done.4, bf16[64,2560]{1,0:T(8,128)(2,1)S(1)} %bitcast.21, f32[2,2560]{1,0:T(2,128)S(1)} %copy-done.6, ...), custom_call_target="tpu_custom_call" | custom-call | flops 1342177280 | bytes 4194304 | tf_op jit(solution)/shard_map/pallas_call | solution.py:689
  67.1 0.0 collective-permute-done.1.refs_7_
  67.1 0.0 collective-permute-done.3.refs_9_
  67.1 0.0 copy-start.11
  67.1 1.9 %shard_map.119 = (f32[72,512]{1,0:T(8,128)S(1)}, f32[72,384]{1,0:T(8,128)S(1)}, f32[72,384]{1,0:T(8,128)S(1)}) custom-call(s32[8]{0:T(128)S(1)} %copy-done.7, bf16[3,4,16,128]{3,2,1,0:T(8,128)(2,1)S(1)} %copy-done.5, bf16[256,256]{1,0:T(8,128)(2,1)S(1)} %copy-done.4, bf16[64,2560]{1,0:T(8,128)(2,1)S(1)} %bitcast.22, f32[2,2560]{1,0:T(2,128)S(1)} %copy-done.6, ...), custom_call_target="tpu_custom_call" | custom-call | flops 1342177280 | bytes 4194304 | tf_op jit(solution)/shard_map/pallas_call | solution.py:689
  69.0 21.5 %finish.1 = f32[32,512]{1,0:T(8,128)S(1)} custom-call(f32[72,512]{1,0:T(8,128)S(1)} %get-tuple-element.31.own_ref, f32[72,384]{1,0:T(8,128)S(1)} %get-tuple-element.32.left_ref, f32[72,384]{1,0:T(8,128)S(1)} %get-tuple-element.33.right_ref, f32[64,128]{1,0:T(8,128)S(1)} %get-tuple-element.34.shift_ref, f32[1]{0:T(128)S(6)} %copy.13.guide_ref), custom_call_target="tpu_custom_call" | custom-call | tf_op jit(solution)/shard_map/finish/pallas_call | solution.py:707
  90.6 0.6 fusion
  (14 shorter events, 0.0 us)
Async XLA Ops:
  0.0 21.7 %copy-start = (bf16[1,512,2560]{2,1,0:T(8,128)(2,1)S(1)}, bf16[1,512,2560]{2,1,0:T(8,128)(2,1)}, u32[]{:S(2)}) copy-start(bf16[1,512,2560]{2,1,0:T(8,128)(2,1)} %param.12) | copy-start | bytes 7864324
  0.0 21.7 %copy-start.1 = (bf16[1,512,2560]{2,1,0:T(8,128)(2,1)S(1)}, bf16[1,512,2560]{2,1,0:T(8,128)(2,1)}, u32[]{:S(2)}) copy-start(bf16[1,512,2560]{2,1,0:T(8,128)(2,1)} %param.13) | copy-start | bytes 7864324
  0.0 21.8 %copy-start.2 = (bf16[1,512,2560]{2,1,0:T(8,128)(2,1)S(1)}, bf16[1,512,2560]{2,1,0:T(8,128)(2,1)}, u32[]{:S(2)}) copy-start(bf16[1,512,2560]{2,1,0:T(8,128)(2,1)} %param.14) | copy-start | bytes 7864324
  0.0 21.8 %copy-start.6 = (f32[2,2560]{1,0:T(2,128)S(1)}, f32[2,2560]{1,0:T(2,128)}, u32[]{:S(2)}) copy-start(f32[2,2560]{1,0:T(2,128)} %refs_4_.3) | copy-start | bytes 61444
  0.0 21.8 %copy-start.8 = (s32[256]{0:T(256)S(1)}, s32[256]{0:T(256)}, u32[]{:S(2)}) copy-start(s32[256]{0:T(256)} %lens_ref.3) | copy-start | bytes 3076
  0.0 21.8 %copy-start.10 = (f32[256]{0:T(256)S(1)}, f32[256]{0:T(256)}, u32[]{:S(2)}) copy-start(f32[256]{0:T(256)} %step_ref.1) | copy-start | bytes 3076
  7.6 45.3 %collective-permute-start = (bf16[3,81,16,128]{3,2,1,0:T(8,128)(2,1)}, bf16[3,81,16,128]{3,2,1,0:T(8,128)(2,1)S(1)}, u32[]{:S(2)}, u32[]{:S(2)}) collective-permute-start(bf16[3,81,16,128]{3,2,1,0:T(8,128)(2,1)} %get-tuple-element.24), channel_id=1, source_target_pairs={{0,1},{1,2},{2,3},{3,4},{4,5},{5,6},{6,7},{7,8},{8,9},{9,10},{10,1... | collective-permute-start | bytes 2985992 | tf_op jit(solution)/shard_map/ppermute | solution.py:582
  8.9 44.1 %collective-permute-start.2 = (bf16[3,81,16,128]{3,2,1,0:T(8,128)(2,1)}, bf16[3,81,16,128]{3,2,1,0:T(8,128)(2,1)S(1)}, u32[]{:S(2)}, u32[]{:S(2)}) collective-permute-start(bf16[3,81,16,128]{3,2,1,0:T(8,128)(2,1)} %get-tuple-element.26), channel_id=1, source_target_pairs={{0,127},{1,0},{2,1},{3,2},{4,3},{5,4},{6,5},{7,6},{8,7},{9,8},{10,... | collective-permute-start | bytes 2985992 | tf_op jit(solution)/shard_map/ppermute | solution.py:582
  15.4 51.7 %collective-permute-start.1 = (bf16[3,90,16,128]{3,2,1,0:T(8,128)(2,1)}, bf16[3,90,16,128]{3,2,1,0:T(8,128)(2,1)S(1)}, u32[]{:S(2)}, u32[]{:S(2)}) collective-permute-start(bf16[3,90,16,128]{3,2,1,0:T(8,128)(2,1)} %get-tuple-element.25), channel_id=1, source_target_pairs={{0,1},{1,2},{2,3},{3,4},{4,5},{5,6},{6,7},{7,8},{8,9},{9,10},{10,1... | collective-permute-start | bytes 3317768 | tf_op jit(solution)/shard_map/ppermute | solution.py:582
  15.4 51.7 %collective-permute-start.3 = (bf16[3,90,16,128]{3,2,1,0:T(8,128)(2,1)}, bf16[3,90,16,128]{3,2,1,0:T(8,128)(2,1)S(1)}, u32[]{:S(2)}, u32[]{:S(2)}) collective-permute-start(bf16[3,90,16,128]{3,2,1,0:T(8,128)(2,1)} %get-tuple-element.27), channel_id=1, source_target_pairs={{0,127},{1,0},{2,1},{3,2},{4,3},{5,4},{6,5},{7,6},{8,7},{9,8},{10,... | collective-permute-start | bytes 3317768 | tf_op jit(solution)/shard_map/ppermute | solution.py:582
  21.8 1.0 %copy-start.3 = (bf16[2560,64]{0,1:T(8,128)(2,1)S(1)}, bf16[2560,64]{0,1:T(8,128)(2,1)}, u32[]{:S(2)}) copy-start(bf16[2560,64]{0,1:T(8,128)(2,1)} %param.17) | copy-start | bytes 983044
  22.8 0.9 copy-start.4
  23.7 0.8 copy-start.5
  24.5 0.7 copy-start.7
  25.1 0.7 copy-start.9
  67.1 23.4 %copy-start.11 = (f32[512,32]{0,1:T(8,128)S(1)}, f32[512,32]{0,1:T(8,128)}, u32[]{:S(2)}) copy-start(f32[512,32]{0,1:T(8,128)} %param.16) | copy-start | bytes 196612
